TPU v7x, 32 devices: a whole 2x2x4 slice. The times are simulated.
32 devices in a mesh: fsdp: 32 (over z, y, x, core).
Axes of the slice: x: 2, y: 2, z: 4, core: 2. Of those that a mesh axis runs over, the one named last changes fastest.
Arguments:
- tokens: bfloat16 [4096, 2048], P('fsdp'), may hold values from -6 to 6
- cotangent: bfloat16 [4096, 2048], P('fsdp'), may hold values from -6 to 6
- segment_ids: int32 [4096], P('fsdp'), may hold values from 0 to 7, never falling along the last dimension, each value on 1 to 1024 neighbouring positions
- expert_ids: int32 [4096, 4], P('fsdp'), may hold values from 0 to 7, all different within a row
- route_weights: float32 [4096, 4], P('fsdp'), may hold values from 0.2 to 0.6
- pair_order: int32 [32, 512], P('fsdp'), may hold values from 0 to 511, each once within a row
- norm_in_gain: bfloat16 [2048], P('fsdp'), may hold values from 0.5 to 1.5
- qkv_weight: bfloat16 [2048, 6144], P('fsdp'), may hold values from -0.125 to 0.125
- qkv_bias: bfloat16 [6144], P('fsdp'), may hold values from -1.5 to 1.5
- out_weight: bfloat16 [2048, 2048], P('fsdp'), may hold values from -0.5 to 0.5
- norm_mid_gain: bfloat16 [2048], P('fsdp'), may hold values from 0.5 to 1.5
- shared_gate: bfloat16 [2048], P('fsdp'), may hold values from -0.125 to 0.125
- shared_in: bfloat16 [2048, 11264], P('fsdp'), may hold values from -0.125 to 0.125
- shared_out: bfloat16 [5632, 2048], P('fsdp'), may hold values from -0.078125 to 0.078125
- expert_in: bfloat16 [32, 2048, 704], P('fsdp'), may hold values from -0.125 to 0.125
- expert_out: bfloat16 [32, 352, 2048], P('fsdp'), may hold values from -0.15625 to 0.15625
Outputs:
- output: bfloat16 [4096, 2048], P('fsdp')
- input_grad: float32 [4096, 2048], P('fsdp')
- norm_in_gain_grad: float32 [2048], P('fsdp')
- qkv_weight_grad: float32 [2048, 6144], P('fsdp')
- qkv_bias_grad: float32 [6144], P('fsdp')
- out_weight_grad: float32 [2048, 2048], P('fsdp')
- norm_mid_gain_grad: float32 [2048], P('fsdp')
- shared_gate_grad: float32 [2048], P('fsdp')
- shared_in_grad: float32 [2048, 11264], P('fsdp')
- shared_out_grad: float32 [5632, 2048], P('fsdp')
- expert_in_grad: float32 [32, 2048, 704], P('fsdp')
- expert_out_grad: float32 [32, 352, 2048], P('fsdp')
Inputs may be any that keep to these rules, and one draw needn't show every extreme that they name: `segment_ids`: ids never fall along the tokens; each sequence holds 1 to 1024 tokens and one holds exactly 1024. `expert_ids`: each token names 4 different experts. `pair_order`: each row is a permutation of that device's pairs; pair t * 4 + k is local token t's k-th expert.
All inputs are finite; a program needn't handle non-finite values.
Results may differ from a plain program's by a relative error of at most 0.015.
Values may be sent and summed in bfloat16 or wider, within the bound.
A program may use at most 576 MiB of HBM per device.

v0:
```python
from functools import partial

import jax
import jax.numpy as jnp
from jax import lax
from jax.sharding import PartitionSpec as P

HEAD_DIM = 128
EXP_PARTS = 4
SEQ = 1024


EPSILON = 1e-06
THETA = 1000000.0
MASKED = -1e30
HIGHEST = lax.Precision.HIGHEST


def passed_along(value, axis, steps):
    count = lax.axis_size(axis)
    leading, last = (max(0, -steps), min(count, count - steps))
    return lax.ppermute(value, axis, [(source, source + steps) for source in range(leading, last)])


def rms_norm(vector, factor):
    return vector * lax.rsqrt(jnp.mean(vector * vector, axis=-1, keepdims=True) + EPSILON) * factor


def rotate(vector, cosine, sine_table):
    middle = vector.shape[-1] // 2
    turned = jnp.concatenate([-vector[..., middle:], vector[..., :middle]], axis=-1)
    return vector * cosine + turned * sine_table


def swiglu(joined):
    middle = joined.shape[-1] // 2
    return jax.nn.silu(joined[..., :middle]) * joined[..., middle:]


def fetch_weights(
    norm_in_gain,
    qkv_weight,
    qkv_bias,
    out_weight,
    norm_mid_gain,
    shared_gate,
    shared_in,
    shared_out,
):
    return (
        lax.all_gather(norm_in_gain, "fsdp", axis=0, tiled=True),
        lax.all_gather(qkv_weight, "fsdp", axis=0, tiled=True),
        lax.all_gather(qkv_bias, "fsdp", axis=0, tiled=True),
        lax.all_gather(out_weight, "fsdp", axis=0, tiled=True),
        lax.all_gather(norm_mid_gain, "fsdp", axis=0, tiled=True),
        lax.all_gather(shared_gate, "fsdp", axis=0, tiled=True),
        lax.all_gather(shared_in, "fsdp", axis=0, tiled=True),
        lax.all_gather(shared_out, "fsdp", axis=0, tiled=True),
    )


def masked_scores(queries, key_window, allowed, score_scale):
    scores = (
        jnp.einsum("qhd,khd->hqk", queries, key_window, preferred_element_type=jnp.float32)
        * score_scale
    )
    return jnp.where(allowed[None], scores, MASKED)


def per_device(
    tokens,
    cotangent,
    segment_ids,
    expert_ids,
    route_weights,
    pair_order,
    norm_in_gain,
    qkv_weight,
    qkv_bias,
    out_weight,
    norm_mid_gain,
    shared_gate,
    shared_in,
    shared_out,
    expert_in,
    expert_out,
):
    local_rows = tokens.shape[0]
    model_width = tokens.shape[1]
    shard_count = lax.axis_size("fsdp")
    device_index = lax.axis_index("fsdp")
    head_size = HEAD_DIM
    head_count = model_width // head_size
    back_span = (SEQ + local_rows - 2) // local_rows
    window = (back_span + 1) * local_rows
    lead = back_span * local_rows
    top_k = expert_ids.shape[1]
    expert_count = shard_count // EXP_PARTS
    capacity = (9 * local_rows * top_k + 8 * expert_count - 1) // (8 * expert_count)
    score_scale = head_size ** (-0.5)
    bf_type = jnp.bfloat16
    fl_type = jnp.float32
    fetched = fetch_weights(
        norm_in_gain,
        qkv_weight,
        qkv_bias,
        out_weight,
        norm_mid_gain,
        shared_gate,
        shared_in,
        shared_out,
    )
    gain_in, qkv_full, bias_full, out_full, gain_mid, gate_full, shared_in_full, shared_out_full = (
        fetched
    )
    id_tags = segment_ids + 1
    id_parts = []
    for distance in range(back_span, 0, -1):
        id_parts.append(passed_along(id_tags, "fsdp", distance))
    key_ids = jnp.concatenate(id_parts + [id_tags])
    key_block = jnp.arange(window, dtype=jnp.int32) // local_rows
    key_valid = device_index - back_span + key_block >= 0
    query_slot = jnp.arange(local_rows, dtype=jnp.int32)
    earlier = jnp.logical_not(key_valid)[None, :] | (key_ids[None, :] < id_tags[:, None])
    positions = (
        lead + query_slot - jnp.sum(earlier.astype(jnp.int32), axis=1, dtype=jnp.int32)
    ).astype(fl_type)
    causal = jnp.arange(window, dtype=jnp.int32)[None, :] <= query_slot[:, None] + lead
    allowed = causal & key_valid[None, :] & (key_ids[None, :] == id_tags[:, None])
    inverse = THETA ** (-jnp.arange(0, head_size, 2, dtype=fl_type) / head_size)
    angles = positions[:, None] * inverse[None, :]
    angles = jnp.concatenate([angles, angles], axis=-1)[:, None, :]
    cosine = jnp.cos(angles)
    sine_table = jnp.sin(angles)
    turn = partial(rotate, cosine=cosine, sine_table=sine_table)
    inputs = tokens.astype(fl_type)
    gain_in32 = gain_in.astype(fl_type)
    normed = rms_norm(inputs, gain_in32)
    normed_low = normed.astype(bf_type)
    projected = jnp.dot(normed_low, qkv_full, preferred_element_type=fl_type) + bias_full.astype(
        fl_type
    )
    query_raw = projected[:, :model_width].reshape(local_rows, head_count, head_size)
    key_raw = projected[:, model_width : 2 * model_width].reshape(local_rows, head_count, head_size)
    queries = turn(query_raw).astype(bf_type)
    key_rows = turn(key_raw).astype(bf_type)
    values = projected[:, 2 * model_width :].astype(bf_type)
    pair_kv = jnp.stack([key_rows.reshape(local_rows, model_width), values])
    kv_parts = []
    for distance in range(back_span, 0, -1):
        kv_parts.append(passed_along(pair_kv, "fsdp", distance))
    kv_window = jnp.concatenate(kv_parts + [pair_kv], axis=1)
    key_window = kv_window[0].reshape(window, head_count, head_size)
    value_window = kv_window[1].reshape(window, head_count, head_size)
    scores = masked_scores(queries, key_window, allowed, score_scale)
    top_score = jnp.max(scores, axis=-1, keepdims=True)
    exp_total = jnp.sum(jnp.exp(scores - top_score), axis=-1, keepdims=True)
    log_total = top_score + jnp.log(exp_total)
    attention = jnp.exp(scores - log_total)
    attention_low = attention.astype(bf_type)
    attended = jnp.einsum(
        "hqk,khd->qhd", attention_low, value_window, preferred_element_type=fl_type
    )
    attended_low = attended.reshape(local_rows, model_width).astype(bf_type)
    hidden = inputs + jnp.dot(attended_low, out_full, preferred_element_type=fl_type)
    gain_mid32 = gain_mid.astype(fl_type)
    mid_low = rms_norm(hidden, gain_mid32).astype(bf_type)
    shared_pre = jnp.dot(mid_low, shared_in_full, preferred_element_type=fl_type)
    shared_act_low = swiglu(shared_pre).astype(bf_type)
    shared_value = jnp.dot(shared_act_low, shared_out_full, preferred_element_type=fl_type)
    shared_scale = jax.nn.sigmoid(jnp.dot(mid_low, gate_full, preferred_element_type=fl_type))
    flat_experts = expert_ids.reshape(-1)
    order_row = pair_order[0]
    ranked = flat_experts[order_row]
    onehot = (ranked[:, None] == jnp.arange(expert_count, dtype=jnp.int32)[None, :]).astype(
        jnp.int32
    )
    running = jnp.cumsum(onehot, axis=0, dtype=jnp.int32)
    slot_ranked = jnp.sum(running * onehot, axis=-1, dtype=jnp.int32) - 1
    slots = jnp.zeros_like(flat_experts).at[order_row].set(slot_ranked)
    kept_pairs = slots < capacity
    slot_place = jnp.where(kept_pairs, flat_experts * capacity + slots, expert_count * capacity)
    slot_pick = jnp.where(kept_pairs, slot_place, 0)
    kept_float = kept_pairs.astype(fl_type)
    pair_weights = route_weights.reshape(-1) * kept_float

    def dispatch(pair_rows):
        slot_table = (
            jnp.zeros((expert_count * capacity, model_width), bf_type)
            .at[slot_place]
            .set(pair_rows, mode="drop")
        )
        copies = jnp.broadcast_to(
            slot_table.reshape(expert_count, 1, capacity, model_width),
            (expert_count, EXP_PARTS, capacity, model_width),
        )
        arrived = lax.all_to_all(
            copies.reshape(shard_count, capacity, model_width),
            "fsdp",
            split_axis=0,
            concat_axis=0,
            tiled=True,
        )
        return arrived.reshape(shard_count * capacity, model_width)

    def collect(returned):
        summed = jnp.sum(
            returned.reshape(expert_count, EXP_PARTS, capacity, model_width).astype(fl_type), axis=1
        )
        picked = summed.reshape(expert_count * capacity, model_width)[slot_pick]
        return picked * kept_float[:, None]

    weight_in_local = expert_in[0]
    weight_out_local = expert_out[0]
    arrived_rows = dispatch(jnp.repeat(mid_low, top_k, axis=0))
    expert_pre = jnp.dot(arrived_rows, weight_in_local, preferred_element_type=fl_type)
    expert_act_low = swiglu(expert_pre).astype(bf_type)
    expert_part = jnp.dot(expert_act_low, weight_out_local, preferred_element_type=fl_type).astype(
        bf_type
    )
    returned = lax.all_to_all(
        expert_part.reshape(shard_count, capacity, model_width),
        "fsdp",
        split_axis=0,
        concat_axis=0,
        tiled=True,
    )
    pair_out = collect(returned)
    routed = jnp.sum(
        (pair_out * route_weights.reshape(-1)[:, None]).reshape(local_rows, top_k, model_width),
        axis=1,
    )
    output = (hidden + routed + shared_scale[:, None] * shared_value).astype(bf_type)
    fetched = fetch_weights(
        norm_in_gain,
        qkv_weight,
        qkv_bias,
        out_weight,
        norm_mid_gain,
        shared_gate,
        shared_in,
        shared_out,
    )
    gain_in, qkv_full, bias_full, out_full, gain_mid, gate_full, shared_in_full, shared_out_full = (
        fetched
    )
    grad_out = cotangent.astype(fl_type)
    d_shared_low = (shared_scale[:, None] * grad_out).astype(bf_type)
    d_shared_act = jnp.einsum(
        "tc,fc->tf", d_shared_low, shared_out_full, preferred_element_type=fl_type
    )
    shared_pull = jax.vjp(swiglu, shared_pre)[1]
    d_shared_pre_low = shared_pull(d_shared_act)[0].astype(bf_type)
    d_mid = jnp.einsum(
        "tf,cf->tc", d_shared_pre_low, shared_in_full, preferred_element_type=fl_type
    )
    d_logit = jnp.sum(grad_out * shared_value, axis=-1) * shared_scale * (1.0 - shared_scale)
    d_mid = d_mid + d_logit[:, None] * gate_full.astype(fl_type)
    gate_grad = jnp.dot(d_logit, mid_low.astype(fl_type), precision=HIGHEST)
    d_part_low = (jnp.repeat(grad_out, top_k, axis=0) * pair_weights[:, None]).astype(bf_type)
    d_arrived = dispatch(d_part_low)
    d_expert_act = jnp.einsum(
        "rc,fc->rf", d_arrived, weight_out_local, preferred_element_type=fl_type
    )
    expert_out_grad = jnp.einsum(
        "rf,rc->fc", expert_act_low, d_arrived, preferred_element_type=fl_type
    )
    expert_pull = jax.vjp(swiglu, expert_pre)[1]
    d_expert_pre_low = expert_pull(d_expert_act)[0].astype(bf_type)
    expert_in_grad = jnp.einsum(
        "rc,rf->cf", arrived_rows, d_expert_pre_low, preferred_element_type=fl_type
    )
    d_rows = jnp.einsum(
        "rf,cf->rc", d_expert_pre_low, weight_in_local, preferred_element_type=fl_type
    )
    returned_grads = lax.all_to_all(
        d_rows.reshape(shard_count, capacity, model_width),
        "fsdp",
        split_axis=0,
        concat_axis=0,
        tiled=True,
    )
    d_mid = d_mid + jnp.sum(collect(returned_grads).reshape(local_rows, top_k, model_width), axis=1)
    mid_pull = jax.vjp(rms_norm, hidden, gain_mid32)[1]
    d_hidden_part, d_gain_mid = mid_pull(d_mid)
    d_hidden = grad_out + d_hidden_part
    d_attn_low = d_hidden.astype(bf_type)
    d_attended_low = (
        jnp.einsum("tc,rc->tr", d_attn_low, out_full, preferred_element_type=fl_type)
        .astype(bf_type)
        .reshape(local_rows, head_count, head_size)
    )
    scores = masked_scores(queries, key_window, allowed, score_scale)
    attention = jnp.exp(scores - log_total)
    attention_low = attention.astype(bf_type)
    d_attention = jnp.einsum(
        "qhd,khd->hqk", d_attended_low, value_window, preferred_element_type=fl_type
    )
    row_delta = jnp.sum(attention * d_attention, axis=-1, keepdims=True)
    d_scores_low = (attention * (d_attention - row_delta)).astype(bf_type)
    d_queries = (
        jnp.einsum("hqk,khd->qhd", d_scores_low, key_window, preferred_element_type=fl_type)
        * score_scale
    )
    d_keys = (
        jnp.einsum("hqk,qhd->khd", d_scores_low, queries, preferred_element_type=fl_type)
        * score_scale
    )
    d_values = jnp.einsum(
        "hqk,qhd->khd", attention_low, d_attended_low, preferred_element_type=fl_type
    )
    d_kv = jnp.stack([d_keys.reshape(window, model_width), d_values.reshape(window, model_width)])
    kv_grad_sum = d_kv[:, lead:]
    for distance in range(1, back_span + 1):
        grad_block = d_kv[
            :, (back_span - distance) * local_rows : (back_span - distance + 1) * local_rows
        ]
        kv_grad_sum = kv_grad_sum + passed_along(
            grad_block.astype(jnp.bfloat16), "fsdp", -distance
        ).astype(grad_block.dtype)
    turn_pull = jax.vjp(turn, query_raw)[1]
    d_query_raw = turn_pull(d_queries)[0]
    d_key_raw = turn_pull(kv_grad_sum[0].reshape(local_rows, head_count, head_size))[0]
    d_projected_low = jnp.concatenate(
        [
            d_query_raw.reshape(local_rows, model_width),
            d_key_raw.reshape(local_rows, model_width),
            kv_grad_sum[1],
        ],
        axis=1,
    ).astype(bf_type)
    bias_grad = jnp.sum(d_projected_low.astype(fl_type), axis=0)
    d_normed = jnp.einsum("tc,rc->tr", d_projected_low, qkv_full, preferred_element_type=fl_type)
    in_pull = jax.vjp(rms_norm, inputs, gain_in32)[1]
    d_inputs, d_gain_in = in_pull(d_normed)
    input_grad = d_hidden + d_inputs
    input_grads = lax.psum_scatter(
        jnp.concatenate(
            [
                jnp.einsum(
                    "tr,tc->rc", normed_low, d_projected_low, preferred_element_type=fl_type
                ),
                jnp.einsum("tr,tc->rc", attended_low, d_attn_low, preferred_element_type=fl_type),
                jnp.einsum("tr,tc->rc", mid_low, d_shared_pre_low, preferred_element_type=fl_type),
            ],
            axis=1,
        ),
        "fsdp",
        scatter_dimension=0,
        tiled=True,
    )
    shared_out_grad = lax.psum_scatter(
        jnp.einsum("tr,tc->rc", shared_act_low, d_shared_low, preferred_element_type=fl_type),
        "fsdp",
        scatter_dimension=0,
        tiled=True,
    )
    gain_in_grad, qkv_bias_grad, gain_mid_grad, shared_gate_grad = (
        lax.psum_scatter(d_gain_in, "fsdp", scatter_dimension=0, tiled=True),
        lax.psum_scatter(bias_grad, "fsdp", scatter_dimension=0, tiled=True),
        lax.psum_scatter(d_gain_mid, "fsdp", scatter_dimension=0, tiled=True),
        lax.psum_scatter(gate_grad, "fsdp", scatter_dimension=0, tiled=True),
    )
    qkv_weight_grad = input_grads[:, : 3 * model_width]
    out_weight_grad = input_grads[:, 3 * model_width : 4 * model_width]
    shared_in_grad = input_grads[:, 4 * model_width :]
    return (
        output,
        input_grad,
        gain_in_grad,
        qkv_weight_grad,
        qkv_bias_grad,
        out_weight_grad,
        gain_mid_grad,
        shared_gate_grad,
        shared_in_grad,
        shared_out_grad,
        expert_in_grad[None],
        expert_out_grad[None],
    )


def solution(mesh):
    placed = (
        P("fsdp", None),
        P("fsdp", None),
        P("fsdp"),
        P("fsdp", None),
        P("fsdp", None),
        P("fsdp", None),
        P("fsdp"),
        P("fsdp", None),
        P("fsdp"),
        P("fsdp", None),
        P("fsdp"),
        P("fsdp"),
        P("fsdp", None),
        P("fsdp", None),
        P("fsdp", None, None),
        P("fsdp", None, None),
    )
    return jax.shard_map(
        per_device,
        mesh=mesh,
        in_specs=placed,
        out_specs=(
            P("fsdp", None),
            P("fsdp", None),
            P("fsdp"),
            P("fsdp", None),
            P("fsdp"),
            P("fsdp", None),
            P("fsdp"),
            P("fsdp"),
            P("fsdp", None),
            P("fsdp", None),
            P("fsdp", None, None),
            P("fsdp", None, None),
        ),
        check_vma=False,
    )
```

profile of v0, /device:TPU:0, one launch (start us, length us, event | category | flops | bytes accessed | tf_op | source)
XLA Modules:
  0.0 4377.5 jit_solution(3733190533553801391)
XLA Ops:
  40.2 43.3 all-reduce.17
  104.5 63.5 %all-gather.5.cloned.1.call-done = bf16[2048,6144]{1,0:T(8,128)(2,1)} async-done(((bf16[64,6144]{1,0:T(8,128)(2,1)}), bf16[2048,6144]{1,0:T(8,128)(2,1)}) %all-gather.5.cloned.1.call-update) | async-done | bytes 25165840 | tf_op jit(solution)/shard_map/all_gather | solution.py:52
  168.0 10.2 convolution_add_fusion
  218.0 16.7 collective-permute-done.8
  239.4 23.5 collective-permute-done.9
  262.8 37.8 collective-permute-start.14
  312.6 22.1 collective-permute-done.14
  337.9 10.5 fusion.91
  399.4 163.6 %all-to-all-start = ((bf16[32,72,2048]{2,1,0:T(8,128)(2,1)}), bf16[32,72,2048]{2,1,0:T(8,128)(2,1)}, u32[]{:S(2)}, u32[]{:S(2)}) async-start(bf16[32,72,2048]{2,1,0:T(8,128)(2,1)} %bitcast.138), calls=%async_computation | async-start | bytes 18874368 | tf_op jit(solution)/shard_map/all_to_all | solution.py:197
  579.7 246.2 %all-to-all-done = bf16[32,72,2048]{2,1,0:T(8,128)(2,1)} async-done(((bf16[32,72,2048]{2,1,0:T(8,128)(2,1)}), bf16[32,72,2048]{2,1,0:T(8,128)(2,1)}, u32[]{:S(2)}, u32[]{:S(2)}) %all-to-all-start) | async-done | bytes 9437216 | tf_op jit(solution)/shard_map/all_to_all | solution.py:197
  836.5 12.1 fusion.13
  848.6 196.8 %all-to-all-done.2 = bf16[32,72,2048]{2,1,0:T(8,128)(2,1)} async-done(((bf16[32,72,2048]{2,1,0:T(8,128)(2,1)}), bf16[32,72,2048]{2,1,0:T(8,128)(2,1)}, u32[]{:S(2)}, u32[]{:S(2)}) %all-to-all-start.2) | async-done | bytes 9437216 | tf_op jit(solution)/shard_map/all_to_all | solution.py:197
  1045.4 13.4 fusion.60
  1081.5 13.6 fusion.11
  1095.1 289.9 %all-to-all-done.1 = bf16[32,72,2048]{2,1,0:T(8,128)(2,1)} async-done(((bf16[32,72,2048]{2,1,0:T(8,128)(2,1)}), bf16[32,72,2048]{2,1,0:T(8,128)(2,1)}, u32[]{:S(2)}, u32[]{:S(2)}) %all-to-all-start.1) | async-done | bytes 9437216 | tf_op jit(solution)/shard_map/all_to_all | solution.py:221
  1411.2 20.0 fusion.96
  1431.2 15.5 fusion.61
  1446.7 12.2 multiply_reduce_fusion.5
  1459.0 349.8 %all-to-all-done.3 = f32[32,72,2048]{2,1,0:T(8,128)} async-done(((f32[32,72,2048]{2,1,0:T(8,128)}), f32[32,72,2048]{2,1,0:T(8,128)}, u32[]{:S(2)}, u32[]{:S(2)}) %all-to-all-start.3) | async-done | bytes 18874400 | tf_op jit(solution)/shard_map/all_to_all | solution.py:276
  1841.2 24.0 multiply_reduce_fusion.3
  1875.3 12.7 multiply_reduce_fusion
  1919.7 34.3 fusion.59
  1967.0 10.0 fusion.62
  1983.0 33.3 collective-permute-done.20
  2021.2 20.7 fusion.67
  2041.9 101.9 %pad_maximum_fusion = f32[2048,19456]{1,0:T(8,128)} fusion(f32[2048,11264]{1,0:T(8,128)} %fusion.59, f32[2048,2048]{1,0:T(8,128)} %fusion.62, f32[2048,6144]{1,0:T(8,128)} %fusion.67), kind=kLoop, calls=%fused_computation.6 | loop fusion | flops 79691776 | bytes 318767104 | tf_op jit(solution)/shard_map/concatenate | solution.py:338
  2145.3 17.8 fusion.65
  2173.5 11.2 convolution_bitcast_fusion
  2185.6 20.8 fusion.47
  2206.3 115.1 %all-reduce.16 = (f32[2048]{0:T(1024)S(1)}, f32[6144]{0:T(1024)S(1)}, f32[2048]{0:T(1024)S(1)}, f32[2048]{0:T(1024)S(1)}) all-reduce(f32[2048]{0:T(1024)S(1)} %get-tuple-element.14, f32[6144]{0:T(1024)S(1)} %convert_reduce_fusion.1, f32[2048]{0:T(1024)S(1)} %copy-done.53, ...), channel_id=2, replica_groups=mesh['fsdp'=32] {'fsdp'}, use_global_device_ids=true, to_apply=%region_20.21.clone | all-reduce | flops 12288 | bytes 98304
  2326.4 1548.9 %reduce-scatter.3.cloned.1.call-done = f32[64,19456]{1,0:T(8,128)} async-done(((f32[2048,19456]{1,0:T(8,128)}), f32[64,19456]{1,0:T(8,128)}) %reduce-scatter.3.cloned.1.call-update) | async-done | bytes 4980752 | tf_op jit(solution)/shard_map/reduce_scatter | solution.py:337
  3883.6 486.9 %reduce-scatter.5.cloned.1.call-done = f32[176,2048]{1,0:T(8,128)} async-done(((f32[5632,2048]{1,0:T(8,128)}), f32[176,2048]{1,0:T(8,128)}) %reduce-scatter.5.cloned.1.call-update) | async-done | bytes 1441808 | tf_op jit(solution)/shard_map/reduce_scatter | solution.py:352
  (381 shorter events, 363.5 us)
Async XLA Ops:
  7.3 160.8 %all-gather.5.cloned.1.call-start = ((), (), s32[]{:S(2)}) async-start(), calls=%async_computation.6 | async-start | bytes 25952256 | tf_op jit(solution)/shard_map/all_gather | solution.py:52
  8.0 366.0 %all-gather.7.cloned.1.call-start = ((), (), s32[]{:S(2)}) async-start(), calls=%async_computation.7 | async-start | bytes 8650752 | tf_op jit(solution)/shard_map/all_gather | solution.py:54
  8.7 1402.4 %all-gather.9.cloned.1.call-start = ((), (), s32[]{:S(2)}) async-start(), calls=%async_computation.8 | async-start | bytes 47579136 | tf_op jit(solution)/shard_map/all_gather | solution.py:57
  10.1 89.1 %collective-permute-start.7 = (s32[128]{0:T(128)S(1)}, s32[128]{0:T(128)S(1)}, u32[]{:S(2)}, u32[]{:S(2)}) collective-permute-start(s32[128]{0:T(128)S(1)} %broadcast_add_fusion.1), channel_id=1, source_target_pairs={{0,1},{1,2},{2,3},{3,4},{4,5},{5,6},{6,7},{7,8},{8,9},{9,10},{10,1... | collective-permute-start | bytes 1544 | tf_op jit(solution)/shard_map/ppermute | solution.py:22
  12.5 86.7 %collective-permute-start.6 = (s32[128]{0:T(128)S(1)}, s32[128]{0:T(128)S(1)}, u32[]{:S(2)}, u32[]{:S(2)}) collective-permute-start(s32[128]{0:T(128)S(1)} %broadcast_add_fusion.1), channel_id=1, source_target_pairs={{0,2},{1,3},{2,4},{3,5},{4,6},{5,7},{6,8},{7,9},{8,10},{9,11},{10,... | collective-permute-start | bytes 1544 | tf_op jit(solution)/shard_map/ppermute | solution.py:22
  16.9 82.3 %collective-permute-start.5 = (s32[128]{0:T(128)S(1)}, s32[128]{0:T(128)S(1)}, u32[]{:S(2)}, u32[]{:S(2)}) collective-permute-start(s32[128]{0:T(128)S(1)} %broadcast_add_fusion.1), channel_id=1, source_target_pairs={{0,3},{1,4},{2,5},{3,6},{4,7},{5,8},{6,9},{7,10},{8,11},{9,12},{10... | collective-permute-start | bytes 1544 | tf_op jit(solution)/shard_map/ppermute | solution.py:22
  21.3 77.9 %collective-permute-start.4 = (s32[128]{0:T(128)S(1)}, s32[128]{0:T(128)S(1)}, u32[]{:S(2)}, u32[]{:S(2)}) collective-permute-start(s32[128]{0:T(128)S(1)} %broadcast_add_fusion.1), channel_id=1, source_target_pairs={{0,4},{1,5},{2,6},{3,7},{4,8},{5,9},{6,10},{7,11},{8,12},{9,13},{1... | collective-permute-start | bytes 1544 | tf_op jit(solution)/shard_map/ppermute | solution.py:22
  24.7 60.0 %collective-permute-start = (s32[128]{0:T(128)S(1)}, s32[128]{0:T(128)S(1)}, u32[]{:S(2)}, u32[]{:S(2)}) collective-permute-start(s32[128]{0:T(128)S(1)} %broadcast_add_fusion.1), channel_id=1, source_target_pairs={{0,8},{1,9},{2,10},{3,11},{4,12},{5,13},{6,14},{7,15},{8,16},{9,17... | collective-permute-start | bytes 1544 | tf_op jit(solution)/shard_map/ppermute | solution.py:22
  93.4 5.8 collective-permute-start.3
  194.4 40.4 collective-permute-start.8
  197.1 105.9 %collective-permute-start.10 = (bf16[2,128,2048]{2,1,0:T(8,128)(2,1)}, bf16[2,128,2048]{2,1,0:T(8,128)(2,1)}, u32[]{:S(2)}, u32[]{:S(2)}) collective-permute-start(bf16[2,128,2048]{2,1,0:T(8,128)(2,1)} %pad_maximum_fusion.3), channel_id=1, source_target_pairs={{0,6},{1,7},{2,8},{3,9},{4,10},{5,11},{6,12},{7,13},{8,14},{9,15},... | collective-permute-start | bytes 3145736 | tf_op jit(solution)/shard_map/ppermute | solution.py:22
  201.6 61.3 %collective-permute-start.9 = (bf16[2,128,2048]{2,1,0:T(8,128)(2,1)}, bf16[2,128,2048]{2,1,0:T(8,128)(2,1)}, u32[]{:S(2)}, u32[]{:S(2)}) collective-permute-start(bf16[2,128,2048]{2,1,0:T(8,128)(2,1)} %pad_maximum_fusion.3), channel_id=1, source_target_pairs={{0,7},{1,8},{2,9},{3,10},{4,11},{5,12},{6,13},{7,14},{8,15},{9,16}... | collective-permute-start | bytes 3145736 | tf_op jit(solution)/shard_map/ppermute | solution.py:22
  205.8 103.3 %collective-permute-start.12 = (bf16[2,128,2048]{2,1,0:T(8,128)(2,1)}, bf16[2,128,2048]{2,1,0:T(8,128)(2,1)}, u32[]{:S(2)}, u32[]{:S(2)}) collective-permute-start(bf16[2,128,2048]{2,1,0:T(8,128)(2,1)} %pad_maximum_fusion.3), channel_id=1, source_target_pairs={{0,4},{1,5},{2,6},{3,7},{4,8},{5,9},{6,10},{7,11},{8,12},{9,13},{1... | collective-permute-start | bytes 3145736 | tf_op jit(solution)/shard_map/ppermute | solution.py:22
  209.7 96.9 %collective-permute-start.11 = (bf16[2,128,2048]{2,1,0:T(8,128)(2,1)}, bf16[2,128,2048]{2,1,0:T(8,128)(2,1)}, u32[]{:S(2)}, u32[]{:S(2)}) collective-permute-start(bf16[2,128,2048]{2,1,0:T(8,128)(2,1)} %pad_maximum_fusion.3), channel_id=1, source_target_pairs={{0,5},{1,6},{2,7},{3,8},{4,9},{5,10},{6,11},{7,12},{8,13},{9,14},{... | collective-permute-start | bytes 3145736 | tf_op jit(solution)/shard_map/ppermute | solution.py:22
  234.8 76.8 %collective-permute-start.13 = (bf16[2,128,2048]{2,1,0:T(8,128)(2,1)}, bf16[2,128,2048]{2,1,0:T(8,128)(2,1)S(1)}, u32[]{:S(2)}, u32[]{:S(2)}) collective-permute-start(bf16[2,128,2048]{2,1,0:T(8,128)(2,1)} %pad_maximum_fusion.3), channel_id=1, source_target_pairs={{0,3},{1,4},{2,5},{3,6},{4,7},{5,8},{6,9},{7,10},{8,11},{9,12},{10... | collective-permute-start | bytes 3145736 | tf_op jit(solution)/shard_map/ppermute | solution.py:22
  262.8 71.9 %collective-permute-start.14 = (bf16[2,128,2048]{2,1,0:T(8,128)(2,1)}, bf16[2,128,2048]{2,1,0:T(8,128)(2,1)S(1)}, u32[]{:S(2)}, u32[]{:S(2)}) collective-permute-start(bf16[2,128,2048]{2,1,0:T(8,128)(2,1)} %pad_maximum_fusion.3), channel_id=1, source_target_pairs={{0,2},{1,3},{2,4},{3,5},{4,6},{5,7},{6,8},{7,9},{8,10},{9,11},{10,... | collective-permute-start | bytes 3145736 | tf_op jit(solution)/shard_map/ppermute | solution.py:22
  302.9 32.8 collective-permute-start.15
  399.4 426.4 %all-to-all-start = ((bf16[32,72,2048]{2,1,0:T(8,128)(2,1)}), bf16[32,72,2048]{2,1,0:T(8,128)(2,1)}, u32[]{:S(2)}, u32[]{:S(2)}) async-start(bf16[32,72,2048]{2,1,0:T(8,128)(2,1)} %bitcast.138), calls=%async_computation | async-start | bytes 18874368 | tf_op jit(solution)/shard_map/all_to_all | solution.py:197
  832.3 213.1 %all-to-all-start.2 = ((bf16[32,72,2048]{2,1,0:T(8,128)(2,1)}), bf16[32,72,2048]{2,1,0:T(8,128)(2,1)}, u32[]{:S(2)}, u32[]{:S(2)}) async-start(bf16[32,72,2048]{2,1,0:T(8,128)(2,1)} %bitcast.139), calls=%async_computation.2 | async-start | bytes 18874368 | tf_op jit(solution)/shard_map/all_to_all | solution.py:197
  1066.4 318.6 %all-to-all-start.1 = ((bf16[32,72,2048]{2,1,0:T(8,128)(2,1)}), bf16[32,72,2048]{2,1,0:T(8,128)(2,1)}, u32[]{:S(2)}, u32[]{:S(2)}) async-start(bf16[32,72,2048]{2,1,0:T(8,128)(2,1)} %bitcast.140), calls=%async_computation.1 | async-start | bytes 18874368 | tf_op jit(solution)/shard_map/all_to_all | solution.py:221
  1070.1 361.0 %all-gather.11.cloned.1.call-start = ((), (), s32[]{:S(2)}) async-start(), calls=%async_computation.9 | async-start | bytes 23789568 | tf_op jit(solution)/shard_map/all_gather | solution.py:58
  1385.0 423.8 %all-to-all-start.3 = ((f32[32,72,2048]{2,1,0:T(8,128)}), f32[32,72,2048]{2,1,0:T(8,128)}, u32[]{:S(2)}, u32[]{:S(2)}) async-start(f32[32,72,2048]{2,1,0:T(8,128)} %fusion.11), calls=%async_computation.3 | async-start | bytes 37748736 | tf_op jit(solution)/shard_map/all_to_all | solution.py:276
  1389.0 2486.3 %reduce-scatter.3.cloned.1.call-start = ((), (), s32[]{:S(2)}) async-start(), calls=%async_computation.10 | async-start | bytes 164364288 | tf_op jit(solution)/shard_map/reduce_scatter | solution.py:337
  1915.6 46.6 %collective-permute-start.16 = (bf16[2,128,2048]{1,2,0:T(8,128)(2,1)}, bf16[2,128,2048]{1,2,0:T(8,128)(2,1)}, u32[]{:S(2)}, u32[]{:S(2)}) collective-permute-start(bf16[2,128,2048]{1,2,0:T(8,128)(2,1)} %get-tuple-element.28), channel_id=1, source_target_pairs={{1,0},{2,1},{3,2},{4,3},{5,4},{6,5},{7,6},{8,7},{9,8},{10,9},{11,1... | collective-permute-start | bytes 3145736 | tf_op jit(solution)/shard_map/ppermute | solution.py:22
  1916.9 46.7 %collective-permute-start.23 = (bf16[2,128,2048]{1,2,0:T(8,128)(2,1)}, bf16[2,128,2048]{1,2,0:T(8,128)(2,1)}, u32[]{:S(2)}, u32[]{:S(2)}) collective-permute-start(bf16[2,128,2048]{1,2,0:T(8,128)(2,1)} %get-tuple-element.29), channel_id=1, source_target_pairs={{8,0},{9,1},{10,2},{11,3},{12,4},{13,5},{14,6},{15,7},{16,8},{17,9... | collective-permute-start | bytes 3145736 | tf_op jit(solution)/shard_map/ppermute | solution.py:22
  1918.2 46.8 %collective-permute-start.22 = (bf16[2,128,2048]{1,2,0:T(8,128)(2,1)}, bf16[2,128,2048]{1,2,0:T(8,128)(2,1)}, u32[]{:S(2)}, u32[]{:S(2)}) collective-permute-start(bf16[2,128,2048]{1,2,0:T(8,128)(2,1)} %get-tuple-element.30), channel_id=1, source_target_pairs={{7,0},{8,1},{9,2},{10,3},{11,4},{12,5},{13,6},{14,7},{15,8},{16,9}... | collective-permute-start | bytes 3145736 | tf_op jit(solution)/shard_map/ppermute | solution.py:22
  1954.0 29.0 collective-permute-start.21
  1955.3 61.0 %collective-permute-start.20 = (bf16[2,128,2048]{1,2,0:T(8,128)(2,1)}, bf16[2,128,2048]{1,2,0:T(8,128)(2,1)S(1)}, u32[]{:S(2)}, u32[]{:S(2)}) collective-permute-start(bf16[2,128,2048]{1,2,0:T(8,128)(2,1)} %get-tuple-element.32), channel_id=1, source_target_pairs={{5,0},{6,1},{7,2},{8,3},{9,4},{10,5},{11,6},{12,7},{13,8},{14,9},{... | collective-permute-start | bytes 3145736 | tf_op jit(solution)/shard_map/ppermute | solution.py:22
  1962.2 54.6 %collective-permute-start.19 = (bf16[2,128,2048]{1,2,0:T(8,128)(2,1)S(1)}, bf16[2,128,2048]{1,2,0:T(8,128)(2,1)S(1)}, u32[]{:S(2)}, u32[]{:S(2)}) collective-permute-start(bf16[2,128,2048]{1,2,0:T(8,128)(2,1)S(1)} %copy-done.36), channel_id=1, source_target_pairs={{4,0},{5,1},{6,2},{7,3},{8,4},{9,5},{10,6},{11,7},{12,8},{13,9},{1... | collective-permute-start | bytes 3145736 | tf_op jit(solution)/shard_map/ppermute | solution.py:22
  1963.7 53.2 %collective-permute-start.18 = (bf16[2,128,2048]{1,2,0:T(8,128)(2,1)S(1)}, bf16[2,128,2048]{1,2,0:T(8,128)(2,1)S(1)}, u32[]{:S(2)}, u32[]{:S(2)}) collective-permute-start(bf16[2,128,2048]{1,2,0:T(8,128)(2,1)S(1)} %copy-done.35), channel_id=1, source_target_pairs={{3,0},{4,1},{5,2},{6,3},{7,4},{8,5},{9,6},{10,7},{11,8},{12,9},{13... | collective-permute-start | bytes 3145736 | tf_op jit(solution)/shard_map/ppermute | solution.py:22
  1965.0 51.8 %collective-permute-start.17 = (bf16[2,128,2048]{1,2,0:T(8,128)(2,1)S(1)}, bf16[2,128,2048]{1,2,0:T(8,128)(2,1)S(1)}, u32[]{:S(2)}, u32[]{:S(2)}) collective-permute-start(bf16[2,128,2048]{1,2,0:T(8,128)(2,1)S(1)} %copy-done.34), channel_id=1, source_target_pairs={{2,0},{3,1},{4,2},{5,3},{6,4},{7,5},{8,6},{9,7},{10,8},{11,9},{12,... | collective-permute-start | bytes 3145736 | tf_op jit(solution)/shard_map/ppermute | solution.py:22
  2143.9 2226.6 %reduce-scatter.5.cloned.1.call-start = ((), (), s32[]{:S(2)}) async-start(), calls=%async_computation.11 | async-start | bytes 47579136 | tf_op jit(solution)/shard_map/reduce_scatter | solution.py:352
  (93 other events, 6542.4 us)
Sparse Core Ops, SparseCore 0:
  10.9 157.0 all-gather.4
  170.9 93.7 all-gather.6
  267.5 455.4 all-gather.8
  1073.5 290.4 all-gather.10
  2144.0 1731.2 reduce-scatter.2
  3878.0 492.4 reduce-scatter.4
where the time goes:
time: 4400 us; the launch traced here: 4380 us
  waiting for transfers between devices  3290 us (75%)
  matrix products  301 us (7%)
  starting transfers between devices  273 us (6%)
  other arithmetic  185 us (4%)
  blocking collectives  158 us (4%)
  local copies, waits for them, and re-layouts  154 us (4%)
    reduce_scatter x1, waiting for transfers between devices, per_device(): lax.psum_scatter(jnp.concatenate([jnp.einsum('tr,tc->rc', normed_low, d_p...  1550 us
    reduce_scatter x1, waiting for transfers between devices, per_device(): lax.psum_scatter(jnp.einsum('tr,tc->rc', shared_act_low, d_shared_low, pr...  487 us
    all_to_all x2, waiting for transfers between devices, dispatch(): lax.all_to_all(copies.reshape(shard_count, capacity, model_width), 'fsdp'...  443 us
    all_to_all x1, waiting for transfers between devices, per_device(): lax.all_to_all(d_rows.reshape(shard_count, capacity, model_width), 'fsdp'...  350 us
    all_to_all x1, waiting for transfers between devices, per_device(): lax.all_to_all(expert_part.reshape(shard_count, capacity, model_width), '...  290 us
    all_to_all x2, starting transfers between devices, dispatch(): lax.all_to_all(copies.reshape(shard_count, capacity, model_width), 'fsdp'...  168 us
    unnamed x2, blocking collectives  158 us
    ppermute x24, waiting for transfers between devices, passed_along(): lax.ppermute(value, axis, [(source, source + steps) for source in range(l...  106 us
  transfers between devices with their start and end apart: 34, of which 16 were waited for; matrix products, arithmetic and copies ran while one was open for 9% of the time, Pallas kernels for 0%

commit v1 on v0

v1 whole, which is shorter than its diff:
```python
import functools

import jax
import jax.numpy as jnp
from jax import lax
from jax.experimental import pallas as pl
from jax.experimental.pallas import tpu as pltpu
from jax.sharding import PartitionSpec as P

HEAD_DIM = 128
EXP_PARTS = 4
SEQ = 1024

EPSILON = 1e-06
THETA = 1000000.0
MASKED = -1e30
BF = jnp.bfloat16
FL = jnp.float32
AXIS = "fsdp"
MESH = pl.DeviceIdType.MESH
PLAN = {
    1: (("f", 0), ("s", 0), ("z", 0)),
    4: (("f", 0), ("f", 1), ("s", 0), ("f", 2), ("s", 1), ("f", 3), ("z", 0), ("s", 2), ("z", 1),
        ("s", 3), ("z", 2), ("z", 3)),
}


def place(length):
    me = lax.axis_index(AXIS)
    z, y, x, c = me // 8, (me // 4) % 2, (me // 2) % 2, me % 2

    def device(dz=0, y=y, x=x, c=c):
        return (((z + dz) * 2 + y) * 2 + x) * 2 + c

    return (z if length > 1 else z * 0), y, x, c, device


def greet(length, p, device, y, x, c):
    barrier = pltpu.get_barrier_semaphore()
    for other in (device(c=1 - c), device(x=1 - x), device(y=1 - y)):
        pl.semaphore_signal(barrier, inc=1, device_id=(other,), device_id_type=MESH)
    sides = ((-1, p > 0), (1, p < length - 1)) if length > 1 else ()
    for dz, there in sides:
        @pl.when(there)
        def _():
            pl.semaphore_signal(barrier, inc=1, device_id=(device(dz),), device_id_type=MESH)
    peers = 3
    for _, there in sides:
        peers = peers + there.astype(jnp.int32)
    pl.semaphore_wait(barrier, peers)


def gather_body(length, x_ref, o_ref, send_sem, recv_sem, own_sem):
    p, y, x, c, device = place(length)
    greet(length, p, device, y, x, c)

    def block(h, z, yy, xx, cc):
        return o_ref.at[z, yy, xx, cc, h]

    def code(h, z, yy, xx, cc):
        return h * (8 * length) + ((z * 2 + yy) * 2 + xx) * 2 + cc

    def copy(src, h, where, slot, target):
        return pltpu.make_async_remote_copy(
            src_ref=src,
            dst_ref=block(h, *where),
            send_sem=send_sem.at[slot],
            recv_sem=recv_sem.at[code(h, *where)],
            device_id=(target,),
            device_id_type=MESH,
        )

    def arrived(h, where):
        copy(block(h, *where), h, where, 0, device(c=1 - c)).wait_recv()

    per_half = 9 * length
    started = []

    def send(src, h, where, slot, target, there=None):
        made = copy(src, h, where, h * per_half + slot, target)
        if there is None:
            made.start()
        else:
            pl.when(there)(made.start)
        started.append((made, there))

    own = [pltpu.make_async_copy(x_ref.at[h], block(h, p, y, x, c), own_sem.at[h]) for h in range(2)]
    for h in range(2):
        own[h].start()

    if length == 4:
        order = [
            p,
            jnp.where(p == 0, 1, p - 1),
            jnp.where(p == 0, 2, jnp.where(p == 3, 1, p + 1)),
            jnp.where(p < 2, 3, 0),
        ]
    else:
        order = [p]

    def sides(h, z):
        first = (z, 1 - y, x, c) if h == 0 else (z, y, 1 - x, c)
        seconds = (
            [(z, y, 1 - x, c), (z, 1 - y, 1 - x, c)]
            if h == 0
            else [(z, 1 - y, x, c), (z, 1 - y, 1 - x, c)]
        )
        first_to = device(y=1 - y) if h == 0 else device(x=1 - x)
        second_to = device(x=1 - x) if h == 0 else device(y=1 - y)
        return first, seconds, first_to, second_to

    def stage_z(j):
        z = order[j]
        for h in range(2):
            where = (z, y, x, c)
            if j:
                arrived(h, where)
            src = block(h, *where) if j else x_ref.at[h]
            if length > 1:
                right = (p < length - 1) & (z <= p)
                left = (p > 0) & (z >= p)
                send(src, h, where, 9 * j, device(1), right)
                send(src, h, where, 9 * j + 1, device(-1), left)
            _, _, first_to, second_to = sides(h, z)
            send(src, h, where, 9 * j + 2, first_to)
            send(src, h, where, 9 * j + 3, second_to)
            send(src, h, where, 9 * j + 4, device(c=1 - c))

    def stage_first(j):
        z = order[j]
        for h in range(2):
            first, _, _, second_to = sides(h, z)
            arrived(h, first)
            send(block(h, *first), h, first, 9 * j + 5, second_to)
            send(block(h, *first), h, first, 9 * j + 6, device(c=1 - c))

    def stage_second(j):
        z = order[j]
        for i in range(2):
            for h in range(2):
                _, seconds, _, _ = sides(h, z)
                arrived(h, seconds[i])
                send(block(h, *seconds[i]), h, seconds[i], 9 * j + 7 + i, device(c=1 - c))

    stage_z(0)
    for j in range(length):
        if j + 1 < length:
            stage_z(j + 1)
        stage_first(j)
        if j:
            stage_second(j - 1)
    stage_second(length - 1)
    for j in range(length):
        for h in range(2):
            for yy, xx in ((y, x), (1 - y, x), (y, 1 - x), (1 - y, 1 - x)):
                arrived(h, (order[j], yy, xx, 1 - c))
    for h in range(2):
        own[h].wait()
    for made, there in started:
        if there is None:
            made.wait_send()
        else:
            pl.when(there)(made.wait_send)


def gather(value, length, collective_id):
    rows, width = value.shape
    half = rows // 2
    out = pl.pallas_call(
        functools.partial(gather_body, length),
        out_shape=jax.ShapeDtypeStruct((length, 2, 2, 2, 2, half, width), value.dtype),
        in_specs=[pl.BlockSpec(memory_space=pltpu.VMEM)],
        out_specs=pl.BlockSpec(memory_space=pl.ANY),
        scratch_shapes=[
            pltpu.SemaphoreType.DMA((18 * length,)),
            pltpu.SemaphoreType.DMA((16 * length,)),
            pltpu.SemaphoreType.DMA((2,)),
        ],
        compiler_params=pltpu.CompilerParams(collective_id=collective_id, has_side_effects=True),
    )(value.reshape(2, half, width))
    return out.reshape(8 * length * rows, width)


def scatter_body(length, in_ref, o_ref, pair_in, near, first_in, second_in, z_in, total,
                 send_sem, pair_sem, load_sem, first_sem, second_sem, z_sem):
    p, y, x, c, device = place(length)
    greet(length, p, device, y, x, c)
    half, width = o_ref.shape[1:]
    order = [3, 0, 2, 1] if length == 4 else [0]
    step = min(16, half)
    started = []

    def part(h, z, far, cc):
        if h == 0:
            return in_ref.at[z, :, (1 - x if far else x), cc, h]
        return in_ref.at[z, (1 - y if far else y), :, cc, h]

    def send(src, dst, slot, sem, target, there=None):
        made = pltpu.make_async_remote_copy(
            src_ref=src, dst_ref=dst, send_sem=send_sem.at[slot], recv_sem=sem,
            device_id=(target,), device_id_type=MESH,
        )
        if there is None:
            made.start()
        else:
            pl.when(there)(made.start)
        started.append((made, there))
        return made

    first_to = (device(x=1 - x), device(y=1 - y))
    second_to = (device(y=1 - y), device(x=1 - x))
    place_s = (y, x)
    slot = lambda h, z, k: (h * length + z) * 6 + k
    pairs, loads, firsts, seconds = {}, {}, {}, {}
    for far in (1, 0):
        for z in order:
            for h in range(2):
                k = (h * length + z) * 2 + far
                pairs[h, z, far] = send(
                    part(h, z, far, 1 - c), pair_in.at[h, z, far], slot(h, z, far),
                    pair_sem.at[k], device(c=1 - c),
                )
                loads[h, z, far] = pltpu.make_async_copy(
                    part(h, z, far, c), near.at[h, z, far], load_sem.at[k]
                )
                loads[h, z, far].start()

    def add(target, sources):
        def body(i, _):
            rows = pl.ds(pl.multiple_of(i * step, step), step)
            value = sources[0][rows, :].astype(FL)
            for source in sources[1:]:
                value = value + source[rows, :].astype(FL)
            target[rows, :] = value.astype(target.dtype)
            return 0
        lax.fori_loop(0, half // step, body, 0)

    def stage_first(z):
        for h in range(2):
            pairs[h, z, 1].wait_recv()
            loads[h, z, 1].wait()
            for s in range(2):
                add(near.at[h, z, 1, s], [near.at[h, z, 1, s], pair_in.at[h, z, 1, s]])
            firsts[h, z] = send(
                near.at[h, z, 1], first_in.at[h, z], slot(h, z, 2),
                first_sem.at[h * length + z], first_to[h],
            )

    def stage_second(z):
        for h in range(2):
            s = 1 - place_s[h]
            pairs[h, z, 0].wait_recv()
            loads[h, z, 0].wait()
            firsts[h, z].wait_recv()
            add(near.at[h, z, 0, s],
                [near.at[h, z, 0, s], pair_in.at[h, z, 0, s], first_in.at[h, z, s]])
            seconds[h, z] = send(
                near.at[h, z, 0, s], second_in.at[h, z], slot(h, z, 3),
                second_sem.at[h * length + z], second_to[h],
            )

    def stage_z(z):
        for h in range(2):
            s = place_s[h]
            seconds[h, z].wait_recv()
            sources = [near.at[h, z, 0, s], pair_in.at[h, z, 0, s], first_in.at[h, z, s],
                       second_in.at[h, z]]
            if length == 1:
                add(o_ref.at[h], sources)
                continue
            add(total.at[h, z], sources)
            for side, sender in ((0, (p > 0) & (p <= z)), (1, (p < length - 1) & (p >= z))):
                @pl.when(sender)
                def _():
                    k = (h * length + z) * 2 + side
                    pltpu.make_async_remote_copy(
                        src_ref=near.at[h, z, 0, s], dst_ref=z_in.at[h, z, side],
                        send_sem=send_sem.at[0], recv_sem=z_sem.at[k],
                        device_id=(device(c=1 - c),), device_id_type=MESH,
                    ).wait_recv()
                    add(total.at[h, z], [total.at[h, z], z_in.at[h, z, side]])
            @pl.when(p == z)
            def _():
                add(o_ref.at[h], [total.at[h, z]])
            @pl.when(p != z)
            def _():
                add(near.at[h, z, 0, s], [total.at[h, z]])
            send(near.at[h, z, 0, s], z_in.at[h, z, 0], slot(h, z, 4),
                 z_sem.at[(h * length + z) * 2], device(1), p < z)
            send(near.at[h, z, 0, s], z_in.at[h, z, 1], slot(h, z, 5),
                 z_sem.at[(h * length + z) * 2 + 1], device(-1), p > z)

    stages = {"f": stage_first, "s": stage_second, "z": stage_z}
    for kind, i in PLAN[length]:
        stages[kind](order[i])
    for made, there in started:
        if there is None:
            made.wait_send()
        else:
            pl.when(there)(made.wait_send)


def scatter(value, length, collective_id):
    rows, width = value.shape[0] // (8 * length), value.shape[1]
    half = rows // 2
    out = pl.pallas_call(
        functools.partial(scatter_body, length),
        out_shape=jax.ShapeDtypeStruct((2, half, width), FL),
        in_specs=[pl.BlockSpec(memory_space=pl.ANY)],
        out_specs=pl.BlockSpec(memory_space=pltpu.VMEM),
        scratch_shapes=[
            pltpu.VMEM((2, length, 2, 2, half, width), value.dtype),
            pltpu.VMEM((2, length, 2, 2, half, width), value.dtype),
            pltpu.VMEM((2, length, 2, half, width), value.dtype),
            pltpu.VMEM((2, length, half, width), value.dtype),
            pltpu.VMEM((2, length, 2, half, width), value.dtype),
            pltpu.VMEM((2, length, half, width), FL),
            pltpu.SemaphoreType.DMA((12 * length,)),
            pltpu.SemaphoreType.DMA((4 * length,)),
            pltpu.SemaphoreType.DMA((4 * length,)),
            pltpu.SemaphoreType.DMA((2 * length,)),
            pltpu.SemaphoreType.DMA((2 * length,)),
            pltpu.SemaphoreType.DMA((4 * length,)),
        ],
        compiler_params=pltpu.CompilerParams(
            collective_id=collective_id, has_side_effects=True, vmem_limit_bytes=50 << 20
        ),
    )(value.reshape(length, 2, 2, 2, 2, half, width))
    return out.reshape(rows, width)


def dot(a, b, dims=((1,), (0,))):
    return lax.dot_general(a, b, (dims, ((), ())), preferred_element_type=FL)


def feed_body(mid_ref, grad_ref, weight_ref, w1_ref, w2_ref, part_ref, out_ref, act_ref, pre_ref,
              *, gate_column, shared_width):
    full = w2_ref.shape[0]
    mid, grad = mid_ref[...], grad_ref[...]
    pre = dot(mid, w1_ref[...])
    grad_act = dot(grad, w2_ref[...], ((1,), (1,)))
    gate_pre, up = pre[:, :full], pre[:, full:]
    shared_scale = jax.nn.sigmoid(gate_pre[:, gate_column : gate_column + 1])
    column = lax.broadcasted_iota(jnp.int32, gate_pre.shape, 1)
    factor = jnp.where(column < shared_width, shared_scale, weight_ref[...])
    sig = jax.nn.sigmoid(gate_pre)
    silu = gate_pre * sig
    act = silu * up
    low = (act * factor).astype(BF)
    logit = jnp.sum(
        act[:, :shared_width] * grad_act[:, :shared_width], axis=1, keepdims=True
    )
    d_logit = logit * shared_scale * (1.0 - shared_scale)
    scaled = grad_act * factor
    d_gate = scaled * up * sig * (1.0 + gate_pre * (1.0 - sig))
    d_gate = jnp.where(column == gate_column, d_logit, d_gate)
    act_ref[...] = low
    pre_ref[:, :full] = d_gate.astype(BF)
    pre_ref[:, full:] = (scaled * silu).astype(BF)
    part_ref[...] = dot(pre_ref[...], w1_ref[...], ((1,), (1,))).astype(BF)
    out_ref[...] = dot(low, w2_ref[...]).astype(BF)


def feed(mid, grad, weight, w1, w2, gate_column, shared_width):
    tokens, width = mid.shape
    full = w2.shape[0]
    block = 256
    row = lambda columns: pl.BlockSpec((block, columns), lambda i: (i, 0))
    whole = lambda shape: pl.BlockSpec(
        shape, lambda i: (0, 0), pipeline_mode=pl.Buffered(buffer_count=1)
    )
    return pl.pallas_call(
        functools.partial(feed_body, gate_column=gate_column, shared_width=shared_width),
        grid=(tokens // block,),
        out_shape=(
            jax.ShapeDtypeStruct((tokens, width), BF),
            jax.ShapeDtypeStruct((tokens, width), BF),
            jax.ShapeDtypeStruct((tokens, full), BF),
            jax.ShapeDtypeStruct((tokens, 2 * full), BF),
        ),
        in_specs=[row(width), row(width), row(1), whole(w1.shape), whole(w2.shape)],
        out_specs=(row(width), row(width), row(full), row(2 * full)),
        compiler_params=pltpu.CompilerParams(vmem_limit_bytes=56 << 20),
        cost_estimate=pl.CostEstimate(
            flops=12 * tokens * width * full, bytes_accessed=12 * tokens * width,
            transcendentals=tokens * full,
        ),
    )(mid, grad, weight, w1, w2)


def rms_norm(vector, factor):
    return vector * lax.rsqrt(jnp.mean(vector * vector, axis=-1, keepdims=True) + EPSILON) * factor


def rotate(vector, cosine, sine):
    middle = vector.shape[-1] // 2
    turned = jnp.concatenate([-vector[..., middle:], vector[..., :middle]], axis=-1)
    return vector * cosine + turned * sine


def unrotate(grad, cosine, sine):
    middle = grad.shape[-1] // 2
    scaled = grad * sine
    turned = jnp.concatenate([scaled[..., middle:], -scaled[..., :middle]], axis=-1)
    return grad * cosine + turned


def pair_weight_table(expert_ids, route_weights, order_row, expert_count, capacity):
    rows, top = expert_ids.shape
    pairs = rows * top
    flat = expert_ids.reshape(pairs)
    index = jnp.arange(pairs, dtype=jnp.int32)
    turn = jnp.sum(
        jnp.where(order_row[None, :] == index[:, None], index[None, :], 0), axis=1, dtype=jnp.int32
    )
    before = (turn[None, :] < turn[:, None]) & (flat[None, :] == flat[:, None])
    slots = jnp.sum(before.astype(jnp.int32), axis=1, dtype=jnp.int32)
    kept = (slots < capacity).astype(FL).reshape(rows, top)
    hit = expert_ids[:, :, None] == jnp.arange(expert_count, dtype=jnp.int32)[None, None, :]
    return jnp.sum(jnp.where(hit, (route_weights * kept)[:, :, None], 0.0), axis=1)


def per_device(
    tokens,
    cotangent,
    segment_ids,
    expert_ids,
    route_weights,
    pair_order,
    norm_in_gain,
    qkv_weight,
    qkv_bias,
    out_weight,
    norm_mid_gain,
    shared_gate,
    shared_in,
    shared_out,
    expert_in,
    expert_out,
):
    rows, width = tokens.shape
    count = lax.axis_size(AXIS)
    me = lax.axis_index(AXIS)
    team = SEQ // rows
    teams = count // team
    slab = me // team
    seat = me % team
    heads = width // HEAD_DIM
    own = heads // team
    span = own * HEAD_DIM
    top = expert_ids.shape[1]
    expert_count = count // EXP_PARTS
    capacity = (9 * rows * top + 8 * expert_count - 1) // (8 * expert_count)
    score_scale = HEAD_DIM ** (-0.5)
    in_team = [[s * team + p for p in range(team)] for s in range(teams)]
    across = [[s * team + p for s in range(teams)] for p in range(team)]
    share = width // count
    bias_share = 3 * width // count
    hid_s = shared_out.shape[0]
    hid_e = expert_out.shape[1]

    layered = team == 8 and teams == 4

    def team_gather(value, call):
        if layered:
            return gather(value, 1, call)
        return lax.all_gather(value, AXIS, axis=0, tiled=True, axis_index_groups=in_team)

    def team_scatter(value, call):
        if layered:
            return scatter(value, 1, call)
        return lax.psum_scatter(
            value, AXIS, scatter_dimension=0, tiled=True, axis_index_groups=in_team
        )

    table = pair_weight_table(expert_ids, route_weights, pair_order[0], expert_count, capacity)
    packed = jnp.concatenate(
        [
            norm_in_gain.astype(FL),
            qkv_bias.astype(FL),
            norm_mid_gain.astype(FL),
            shared_gate.astype(FL),
            segment_ids.astype(FL),
            table.T.reshape(-1),
        ]
    )
    if layered:
        entries = packed.shape[0]
        lanes = -(-entries // 2048) * 128
        packed = jnp.pad(packed, (0, 16 * lanes - entries)).reshape(16, lanes)
        small = gather(packed, teams, 6).reshape(count, 16 * lanes)[:, :entries]
    else:
        small = lax.all_gather(packed[None], AXIS, axis=0, tiled=True)
    edge = share
    gain_in = small[:, :edge].reshape(1, width)
    bias = small[:, edge : edge + bias_share].reshape(3, heads, HEAD_DIM)
    edge += bias_share
    gain_mid = small[:, edge : edge + share].reshape(1, width)
    edge += share
    gate = small[:, edge : edge + share].reshape(1, width)
    edge += share
    ids_all = small[:, edge : edge + rows]
    edge += rows
    tables = small[:, edge:].reshape(count, expert_count, rows)
    expert_weight = lax.dynamic_index_in_dim(tables, me // EXP_PARTS, 1, False).reshape(-1)

    mine = qkv_weight.reshape(share, 3, team, span).transpose(2, 0, 1, 3)
    mine = lax.all_to_all(
        mine.reshape(team, share, 3 * span),
        AXIS,
        split_axis=0,
        concat_axis=0,
        tiled=True,
        axis_index_groups=in_team,
    )
    w_qkv = lax.all_gather(
        mine.reshape(team * share, 3 * span), AXIS, axis=0, tiled=True, axis_index_groups=across
    )
    deal = [(p * teams + s, s * team + p) for s in range(teams) for p in range(team)]
    w_out = lax.all_gather(
        lax.ppermute(out_weight, AXIS, deal),
        AXIS, axis=0, tiled=True, axis_index_groups=across,
    )
    bias_own = lax.dynamic_slice_in_dim(bias, seat * own, own, 1).reshape(1, 3 * span)

    shared_cols = shared_in.reshape(share, 2, count, hid_s).transpose(2, 0, 1, 3)
    w_shared = lax.all_to_all(
        shared_cols.reshape(count, share, 2 * hid_s),
        AXIS,
        split_axis=0,
        concat_axis=0,
        tiled=True,
    ).reshape(width, 2 * hid_s)
    wide_s = -(-(hid_s + 1) // 128) * 128
    wide_e = -(-hid_e // 128) * 128
    full = wide_s + wide_e

    def columns(value, wide):
        return jnp.pad(value, ((0, 0), (0, wide - value.shape[1])))

    gate_side = jnp.concatenate([w_shared[:, :hid_s], gate.reshape(width, 1).astype(BF)], axis=1)
    w1 = jnp.concatenate(
        [
            columns(gate_side, wide_s),
            columns(expert_in[0][:, :hid_e], wide_e),
            columns(w_shared[:, hid_s:], wide_s),
            columns(expert_in[0][:, hid_e:], wide_e),
        ],
        axis=1,
    )
    w2 = jnp.concatenate(
        [
            jnp.pad(shared_out, ((0, wide_s - hid_s), (0, 0))),
            jnp.pad(expert_out[0], ((0, wide_e - hid_e), (0, 0))),
        ],
        axis=0,
    )
    grad_all = lax.all_gather(cotangent, AXIS, axis=0, tiled=True)

    inputs = tokens.astype(FL)
    scale_in = lax.rsqrt(jnp.mean(inputs * inputs, axis=-1, keepdims=True) + EPSILON)
    normed = team_gather((inputs * scale_in * gain_in).astype(BF), 0)
    own_ids = lax.dynamic_slice_in_dim(ids_all, slab * team, team, 0).reshape(SEQ)
    prev_ids = lax.dynamic_slice_in_dim(
        ids_all, jnp.maximum(slab - 1, 0) * team, team, 0
    ).reshape(SEQ)
    key_ids = jnp.concatenate([jnp.where(slab > 0, prev_ids, -1.0), own_ids])
    slot = jnp.arange(SEQ, dtype=jnp.int32)
    earlier = (key_ids[None, :] < own_ids[:, None]).astype(jnp.int32)
    positions = (SEQ + slot - jnp.sum(earlier, axis=1, dtype=jnp.int32)).astype(FL)
    inverse = THETA ** (-jnp.arange(0, HEAD_DIM, 2, dtype=FL) / HEAD_DIM)
    angles = positions[:, None] * inverse[None, :]
    angles = jnp.concatenate([angles, angles], axis=-1)
    cosine = jnp.cos(angles)[:, None, :]
    sine = jnp.sin(angles)[:, None, :]

    projected = dot(normed, w_qkv) + bias_own
    queries = rotate(projected[:, :span].reshape(SEQ, own, HEAD_DIM), cosine, sine).astype(BF)
    keys = rotate(projected[:, span : 2 * span].reshape(SEQ, own, HEAD_DIM), cosine, sine)
    key_value = jnp.stack([keys.astype(BF).reshape(SEQ, span), projected[:, 2 * span :].astype(BF)])
    forward = [(source, source + team) for source in range(count - team)]
    backward = [(target, source) for source, target in forward]
    passed = lax.ppermute(key_value, AXIS, forward)
    window = jnp.concatenate([passed, key_value], axis=1).reshape(2, 2 * SEQ, own, HEAD_DIM)
    allowed = (
        jnp.arange(2 * SEQ, dtype=jnp.int32)[None, :] <= slot[:, None] + SEQ
    ) & (key_ids[None, :] == own_ids[:, None])

    def masked_scores():
        scores = (
            jnp.einsum("qhd,khd->hqk", queries, window[0], preferred_element_type=FL) * score_scale
        )
        return jnp.where(allowed[None], scores, MASKED)

    scores = masked_scores()
    top_score = jnp.max(scores, axis=-1, keepdims=True)
    log_total = top_score + jnp.log(
        jnp.sum(jnp.exp(scores - top_score), axis=-1, keepdims=True)
    )
    probs = jnp.exp(scores - log_total).astype(BF)
    attended = jnp.einsum("hqk,khd->qhd", probs, window[1], preferred_element_type=FL)
    attended = attended.reshape(SEQ, span).astype(BF)
    hidden = inputs + team_scatter(dot(attended, w_out).astype(BF), 1).astype(FL)
    scale_mid = lax.rsqrt(jnp.mean(hidden * hidden, axis=-1, keepdims=True) + EPSILON)
    mid = (hidden * scale_mid * gain_mid).astype(BF)

    if layered:
        mid_all = gather(mid, teams, 2)
    else:
        mid_all = lax.all_gather(mid, AXIS, axis=0, tiled=True)
    mid_part, out_part, act_low, d_pre = feed(
        mid_all, grad_all, expert_weight[:, None], w1, w2, hid_s, wide_s
    )
    if layered:
        summed_mid = scatter(mid_part, teams, 3)
    else:
        summed_mid = lax.psum_scatter(mid_part, AXIS, scatter_dimension=0, tiled=True)
    summed_out = lax.psum_scatter(out_part, AXIS, scatter_dimension=0, tiled=True)
    d_w1 = dot(mid_all, d_pre, ((0,), (0,)))
    d_w2 = dot(act_low, grad_all, ((0,), (0,)))
    shared_out_grad = d_w2[:hid_s]
    expert_out_grad = d_w2[wide_s : wide_s + hid_e]
    expert_in_grad = jnp.concatenate(
        [d_w1[:, wide_s : wide_s + hid_e], d_w1[:, full + wide_s : full + wide_s + hid_e]], axis=1
    )
    d_shared = jnp.concatenate([d_w1[:, :hid_s], d_w1[:, full : full + hid_s]], axis=1)
    gate_grad = d_w1[:, hid_s]
    shared_back = lax.all_to_all(
        d_shared.astype(BF).reshape(count, share, 2 * hid_s),
        AXIS,
        split_axis=0,
        concat_axis=0,
        tiled=True,
    )
    shared_in_grad = (
        shared_back.reshape(count, share, 2, hid_s)
        .transpose(1, 2, 0, 3)
        .reshape(share, -1)
        .astype(FL)
    )
    output = (hidden + summed_out.astype(FL)).astype(BF)

    grad_out = cotangent.astype(FL)
    d_mid = summed_mid.astype(FL)

    def norm_back(value, scale, gain, grad):
        unit = value * scale
        weighted = grad * gain
        inner = jnp.mean(weighted * unit, axis=-1, keepdims=True)
        return scale * (weighted - unit * inner), jnp.sum(grad * unit, axis=0)

    d_hidden_part, gain_mid_grad = norm_back(hidden, scale_mid, gain_mid, d_mid)
    d_hidden = grad_out + d_hidden_part
    d_attn = team_gather(d_hidden.astype(BF), 4)
    d_attended = dot(d_attn, w_out, ((1,), (1,))).astype(BF)
    out_grad = dot(attended, d_attn, ((0,), (0,)))
    d_attended = d_attended.reshape(SEQ, own, HEAD_DIM)
    attention = jnp.exp(masked_scores() - log_total)
    d_attention = jnp.einsum("qhd,khd->hqk", d_attended, window[1], preferred_element_type=FL)
    row_delta = jnp.sum(attention * d_attention, axis=-1, keepdims=True)
    d_scores = (attention * (d_attention - row_delta)).astype(BF)
    d_queries = (
        jnp.einsum("hqk,khd->qhd", d_scores, window[0], preferred_element_type=FL) * score_scale
    )
    d_keys = jnp.einsum("hqk,qhd->khd", d_scores, queries, preferred_element_type=FL) * score_scale
    d_values = jnp.einsum(
        "hqk,qhd->khd", attention.astype(BF), d_attended, preferred_element_type=FL
    )
    d_kv = jnp.stack([d_keys.reshape(2 * SEQ, span), d_values.reshape(2 * SEQ, span)])
    returned = lax.ppermute(d_kv[:, :SEQ].astype(BF), AXIS, backward).astype(FL)
    d_kv = d_kv[:, SEQ:] + returned
    d_projected = jnp.concatenate(
        [
            unrotate(d_queries, cosine, sine).reshape(SEQ, span),
            unrotate(d_kv[0].reshape(SEQ, own, HEAD_DIM), cosine, sine).reshape(SEQ, span),
            d_kv[1],
        ],
        axis=1,
    ).astype(BF)
    d_normed = team_scatter(dot(d_projected, w_qkv, ((1,), (1,))).astype(BF), 5).astype(FL)
    d_inputs, gain_in_grad = norm_back(inputs, scale_in, gain_in, d_normed)
    input_grad = d_hidden + d_inputs
    qkv_grad = dot(normed, d_projected, ((0,), (0,)))
    bias_grad = jnp.sum(d_projected.astype(FL), axis=0).reshape(3, own, HEAD_DIM)

    qkv_part = lax.psum_scatter(
        qkv_grad.astype(BF), AXIS, scatter_dimension=0, tiled=True, axis_index_groups=across
    )
    qkv_part = lax.all_to_all(
        qkv_part.reshape(team, share, 3 * span),
        AXIS,
        split_axis=0,
        concat_axis=0,
        tiled=True,
        axis_index_groups=in_team,
    )
    qkv_weight_grad = (
        qkv_part.reshape(team, share, 3, span)
        .transpose(1, 2, 0, 3)
        .reshape(share, 3 * width)
        .astype(FL)
    )
    out_part_grad = lax.psum_scatter(
        out_grad.astype(BF), AXIS, scatter_dimension=0, tiled=True, axis_index_groups=across
    )
    out_weight_grad = lax.ppermute(
        out_part_grad, AXIS, [(target, source) for source, target in deal]
    ).astype(FL)
    bias_spread = lax.dynamic_update_slice_in_dim(
        jnp.zeros((3, heads, HEAD_DIM), FL), bias_grad, seat * own, 1
    )
    small_grads = jnp.concatenate(
        [
            gain_in_grad.reshape(count, share),
            bias_spread.reshape(count, bias_share),
            gain_mid_grad.reshape(count, share),
            gate_grad.reshape(count, share),
        ],
        axis=1,
    )
    if layered:
        entries = small_grads.shape[1]
        lanes = -(-entries // 2048) * 128
        small_grads = jnp.pad(small_grads, ((0, 0), (0, 16 * lanes - entries)))
        small_sum = scatter(small_grads.reshape(count * 16, lanes), teams, 7).reshape(-1)[:entries]
    else:
        small_sum = lax.psum_scatter(small_grads, AXIS, scatter_dimension=0, tiled=True)[0]
    return (
        output,
        input_grad,
        small_sum[:share],
        qkv_weight_grad,
        small_sum[share : share + bias_share],
        out_weight_grad,
        small_sum[share + bias_share : 2 * share + bias_share],
        small_sum[2 * share + bias_share :],
        shared_in_grad,
        shared_out_grad,
        expert_in_grad[None],
        expert_out_grad[None],
    )


def solution(mesh):
    row, flat, deep = P("fsdp", None), P("fsdp"), P("fsdp", None, None)
    return jax.shard_map(
        per_device,
        mesh=mesh,
        in_specs=(
            row, row, flat, row, row, row, flat, row, flat, row, flat, flat, row, row, deep, deep,
        ),
        out_specs=(row, row, flat, row, flat, row, flat, flat, row, row, deep, deep),
        check_vma=False,
    )
```

time: 4400 us -> 1010 us (0.23)
  waiting for transfers between devices: 3290 us -> 182 us
  Pallas kernels: 0 us -> 503 us
  starting transfers between devices: 273 us -> 49.4 us
  matrix products: 301 us -> 114 us
  blocking collectives: 158 us -> 17.6 us
  other arithmetic: 185 us -> 50.5 us
  local copies, waits for them, and re-layouts: 154 us -> 70.7 us
    reduce_scatter x2 -> x3, waiting for transfers between devices: 2040 us -> 118 us  [the longest x1 118 us: per_device(): lax.psum_scatter(out_part, AXIS, scatter_dimension=0, tiled=True)]
    all_to_all x4 -> x3, waiting for transfers between devices: 1080 us -> 0.01 us  [the longest x1 0.01 us: per_device(): lax.all_to_all(d_shared.astype(BF).reshape(count, share, 2 * hid_s), AXIS...]
    pallas_call x0 -> x9, Pallas kernels: none -> 503 us  [the longest x4 218 us: scatter(): pl.pallas_call(functools.partial(scatter_body, length), out_shape=jax.Sha...]
    dot_general x26 -> x14, matrix products: 301 us -> 114 us  [the longest x8 78 us: dot(): return lax.dot_general(a, b, (dims, ((), ())), preferred_element_type=FL)]
    unnamed x2 -> x0, blocking collectives: 158 us -> none
    all_to_all x4 -> x3, starting transfers between devices: 175 us -> 43.1 us  [the longest x1 35.1 us: per_device(): lax.all_to_all(shared_cols.reshape(count, share, 2 * hid_s), AXIS, split_...]
    concatenate x3 -> x7, other arithmetic: 103 us -> 9.76 us  [the longest x1 3.44 us: per_device(): jnp.concatenate([jnp.pad(shared_out, ((0, wide_s - hid_s), (0, 0))), jnp....]
    ppermute x24 -> x4, starting transfers between devices: 97.6 us -> 5.81 us  [the longest x1 1.89 us: per_device(): passed = lax.ppermute(key_value, AXIS, forward)]
  transfers between devices with their start and end apart: 34 -> 13, of which waited for: 16 -> 3; matrix products, arithmetic and copies ran while one was open for 9% -> 18% of each run, Pallas kernels for 0% -> 29%
where the time goes in v1:
time: 1010 us; the launch traced here: 1000 us
  Pallas kernels  503 us (50%)
  waiting for transfers between devices  182 us (18%)
  matrix products  114 us (11%)
  local copies, waits for them, and re-layouts  70.7 us (7%)
  other arithmetic  50.5 us (5%)
  starting transfers between devices  49.4 us (5%)
  blocking collectives  17.6 us (2%)
  between operations  15.6 us (2%)
    pallas_call x4, Pallas kernels, scatter(): pl.pallas_call(functools.partial(scatter_body, length), out_shape=jax.Sha...  218 us
    pallas_call x4, Pallas kernels, gather(): pl.pallas_call(functools.partial(gather_body, length), out_shape=jax.Shap...  205 us
    reduce_scatter x1, waiting for transfers between devices, per_device(): lax.psum_scatter(out_part, AXIS, scatter_dimension=0, tiled=True)  118 us
    pallas_call x1, Pallas kernels, feed(): pl.pallas_call(functools.partial(feed_body, gate_column=gate_column, shar...  80.4 us
    dot_general x8, matrix products, dot(): return lax.dot_general(a, b, (dims, ((), ())), preferred_element_type=FL)  78 us
    all_to_all x1, starting transfers between devices, per_device(): lax.all_to_all(shared_cols.reshape(count, share, 2 * hid_s), AXIS, split_...  35.1 us
    ppermute x1, waiting for transfers between devices, per_device(): passed = lax.ppermute(key_value, AXIS, forward)  33.1 us
    ppermute x1, waiting for transfers between devices, per_device(): returned = lax.ppermute(d_kv[:, :SEQ].astype(BF), AXIS, backward).astype(FL)  30.6 us
  transfers between devices with their start and end apart: 13, of which 3 were waited for; matrix products, arithmetic and copies ran while one was open for 18% of the time, Pallas kernels for 29%

profile of v1, /device:TPU:0, one launch (start us, length us, event | category | flops | bytes accessed | tf_op | source)
XLA Modules:
  0.0 1003.2 jit_solution(14201230519310272132)
XLA Ops:
  10.0 17.6 %all_to_all.20 = bf16[8,64,768]{2,1,0:T(8,128)(2,1)} all-to-all(bf16[8,64,768]{2,1,0:T(8,128)(2,1)S(1)} %reshape.352), channel_id=1, replica_groups={{0,1,2,3,4,5,6,7},{8,9,10,11,12,13,14,15},{16,17,18,19,20,21,22,23},{24..., dimensions={0} | all-to-all | bytes 1572864 | tf_op jit(solution)/shard_map/all_to_all | solution.py:508
  29.9 5.0 reshape.363
  40.9 35.1 %all-to-all-start.1 = ((bf16[32,64,352]{2,1,0:T(8,128)(2,1)}), bf16[32,64,352]{2,1,0:T(8,128)(2,1)}, u32[]{:S(2)}, u32[]{:S(2)}) async-start(bf16[32,64,352]{2,1,0:T(8,128)(2,1)} %reshape.364), calls=%async_computation.1 | async-start | bytes 3145728 | tf_op jit(solution)/shard_map/all_to_all | solution.py:527
  78.0 66.0 %shard_map.247 = f32[4,2,2,2,2,8,128]{6,5,4,3,2,1,0:T(8,128)} custom-call(f32[2,8,128]{2,1,0:T(8,128)} %pad_bitcast_fusion.x_ref), custom_call_target="tpu_custom_call" | custom-call | tf_op jit(solution)/shard_map/pallas_call | solution.py:169
  156.1 28.5 %shard_map.248 = bf16[1,2,2,2,2,64,2048]{6,5,4,3,2,1,0:T(8,128)(2,1)} custom-call(bf16[2,64,2048]{2,1,0:T(8,128)(2,1)} %bitcast.185), custom_call_target="tpu_custom_call" | custom-call | tf_op jit(solution)/shard_map/pallas_call | solution.py:169
  200.9 6.2 convolution_add_fusion
  214.2 33.1 %collective-permute-done = bf16[2,1024,256]{1,2,0:T(8,128)(2,1)S(1)} collective-permute-done((bf16[2,1024,256]{1,2,0:T(8,128)(2,1)S(1)}, bf16[2,1024,256]{1,2,0:T(8,128)(2,1)S(1)}, u32[]{:S(2)}, u32[]{:S(2)}) %collective-permute-start) | collective-permute-done | bytes 1048608 | tf_op jit(solution)/shard_map/ppermute | solution.py:583
  247.7 4.2 fusion
  251.8 5.2 exponential_reduce_fusion
  257.8 5.6 convolution_convert_fusion.4
  263.4 4.7 convolution_convert_fusion
  268.1 24.8 %shard_map.249 = f32[2,64,2048]{2,1,0:T(8,128)S(1)} custom-call(bf16[1,2,2,2,2,64,2048]{6,5,4,3,2,1,0:T(8,128)(2,1)} %bitcast.150), custom_call_target="tpu_custom_call" | custom-call | tf_op jit(solution)/shard_map/pallas_call | solution.py:306
  294.4 87.4 %shard_map.250 = bf16[4,2,2,2,2,64,2048]{6,5,4,3,2,1,0:T(8,128)(2,1)} custom-call(bf16[2,64,2048]{2,1,0:T(8,128)(2,1)} %bitcast.184), custom_call_target="tpu_custom_call" | custom-call | tf_op jit(solution)/shard_map/pallas_call | solution.py:169
  381.8 80.4 %shard_map.251 = (bf16[4096,2048]{1,0:T(8,128)(2,1)}, bf16[4096,2048]{1,0:T(8,128)(2,1)}, bf16[4096,640]{1,0:T(8,128)(2,1)}, bf16[4096,1280]{1,0:T(8,128)(2,1)}) custom-call(bf16[4096,2048]{1,0:T(8,128)(2,1)} %bitcast.151, bf16[4096,2048]{1,0:T(8,128)(2,1)} %all-gather.8.cloned.1.call-done.grad_ref, f32[4096,1]{1,0:T(8,128)} %copy.79.weight_ref, ...), custom_call_target="tpu_custom_call" | custom-call | flops 64424509440 | bytes 100663296 | tf_op jit(solution)/shard_map/pallas_call | solution.py:372
  462.2 111.3 %shard_map.252 = f32[2,64,2048]{2,1,0:T(8,128)S(1)} custom-call(bf16[4,2,2,2,2,64,2048]{6,5,4,3,2,1,0:T(8,128)(2,1)} %bitcast.153), custom_call_target="tpu_custom_call" | custom-call | tf_op jit(solution)/shard_map/pallas_call | solution.py:306
  575.6 23.4 %shard_map.253 = bf16[1,2,2,2,2,64,2048]{6,5,4,3,2,1,0:T(8,128)(2,1)} custom-call(bf16[2,64,2048]{2,1,0:T(8,128)(2,1)} %bitcast.189), custom_call_target="tpu_custom_call" | custom-call | tf_op jit(solution)/shard_map/pallas_call | solution.py:169
  602.8 8.8 fusion.42
  611.6 12.9 %multiply_reduce_fusion = (f32[2,1024]{1,0:T(2,128)S(1)}, f32[2,1024,2048]{2,1,0:T(8,128)}) fusion(f32[2,1024,2048]{2,1,0:T(8,128)} %copy-done.2, f32[2,1024]{1,0:T(2,128)S(1)} %log_add_fusion, pred[1024,2048]{1,0:T(8,128)(4,1)S(1)} %fusion.5, bf16[1024,2,128]{0,2,1:T(8,128)(2,1)S(1)} %bitcast.197, bf16[2048,2,128]{0,2,1:T(8,128)(2,1)S(1)} %bitcast.177), kind=kOutput, calls=%fused_computation.1 | convolution fusion | flops 1094711296 | bytes 37240832 | tf_op jit(solution)/shard_map/qhd,khd->hqk/dot_general | solution.py:659
  624.5 12.2 %multiply_convert_fusion = bf16[2,1024,2048]{2,1,0:T(8,128)(2,1)S(1)} fusion(f32[2,1024,2048]{2,1,0:T(8,128)} %get-tuple-element.60, f32[2,1024,2048]{2,1,0:T(8,128)} %copy-done.2, f32[2,1024]{1,0:T(2,128)S(1)} %get-tuple-element.59, f32[2,1024]{1,0:T(2,128)S(1)} %log_add_fusion, pred[1024,2048]{1,0:T(8,128)(4,1)S(1)} %fusion.5), kind=kLoop, calls=%fused_computation | loop fusion | flops 25165824 | bytes 44056576 | tf_op jit(solution)/shard_map/convert_element_type | solution.py:661
  643.2 30.6 %collective-permute-done.2 = bf16[2,1024,256]{1,2,0:T(8,128)(2,1)S(1)} collective-permute-done((bf16[2,1024,256]{1,2,0:T(8,128)(2,1)S(1)}, bf16[2,1024,256]{1,2,0:T(8,128)(2,1)S(1)}, u32[]{:S(2)}, u32[]{:S(2)}) %collective-permute-start.2) | collective-permute-done | bytes 1048608 | tf_op jit(solution)/shard_map/ppermute | solution.py:670
  677.0 4.9 convolution_convert_fusion.2
  682.0 4.4 convolution_convert_fusion.3
  687.0 29.3 %fusion.54 = (bf16[2048,1280]{0,1:T(8,128)(2,1)S(1)}, f32[2048,1280]{0,1:T(8,128)}) fusion(bf16[4096,2048]{1,0:T(8,128)(2,1)} %bitcast.152, bf16[4096,1280]{1,0:T(8,128)(2,1)} %get-tuple-element.18), kind=kOutput, calls=%fused_computation.144 | convolution fusion | flops 21477457920 | bytes 42991616 | tf_op jit(solution)/shard_map/dot_general | solution.py:333
  723.0 17.6 %fusion.55 = f32[640,2048]{1,0:T(8,128)} fusion(bf16[4096,640]{1,0:T(8,128)(2,1)} %get-tuple-element.19, bf16[4096,2048]{1,0:T(8,128)(2,1)} %all-gather.8.cloned.1.call-done.grad_ref), kind=kOutput, calls=%fused_computation.145 | convolution fusion | flops 10737418240 | bytes 27262976 | tf_op jit(solution)/shard_map/dot_general | solution.py:333
  753.3 7.0 convolution_convert_fusion.1
  760.4 28.0 %shard_map.254 = f32[2,64,2048]{2,1,0:T(8,128)S(1)} custom-call(bf16[1,2,2,2,2,64,2048]{6,5,4,3,2,1,0:T(8,128)(2,1)} %bitcast.168), custom_call_target="tpu_custom_call" | custom-call | tf_op jit(solution)/shard_map/pallas_call | solution.py:306
  788.4 4.2 all-to-all-start.2
  794.9 53.6 %shard_map.255 = f32[2,8,128]{2,1,0:T(8,128)S(1)} custom-call(f32[4,2,2,2,2,8,128]{6,5,4,3,2,1,0:T(8,128)S(1)} %bitcast.145), custom_call_target="tpu_custom_call" | custom-call | tf_op jit(solution)/shard_map/pallas_call | solution.py:306
  850.6 4.9 reshape.382
  855.4 6.7 copy.85
  862.1 5.5 reshape.380
  875.4 117.6 %reduce-scatter.4.cloned.1.call-done = bf16[128,2048]{1,0:T(8,128)(2,1)} async-done(((bf16[4096,2048]{1,0:T(8,128)(2,1)}), bf16[128,2048]{1,0:T(8,128)(2,1)}) %reduce-scatter.4.cloned.1.call-update) | async-done | bytes 524304 | tf_op jit(solution)/shard_map/reduce_scatter | solution.py:618
  (253 shorter events, 100.9 us)
Async XLA Ops:
  7.2 193.7 %all-gather.4.cloned.1.call-start = ((), (), s32[]{:S(2)}) async-start(), calls=%async_computation.7 | async-start | bytes 3932160 | tf_op jit(solution)/shard_map/all_gather | solution.py:516
  27.7 235.7 %all-gather.6.cloned.1.call-start = ((), (), s32[]{:S(2)}) async-start(), calls=%async_computation.8 | async-start | bytes 1310720 | tf_op jit(solution)/shard_map/all_gather | solution.py:520
  27.7 0.7 collective-permute-start.1
  29.1 352.6 %all-gather.8.cloned.1.call-start = ((), (), s32[]{:S(2)}) async-start(), calls=%async_computation.9 | async-start | bytes 17301504 | tf_op jit(solution)/shard_map/all_gather | solution.py:558
  38.8 37.3 %copy-start.54 = (s32[128]{0:T(128)S(1)}, s32[128]{0:T(128)}, u32[]{:S(2)}) copy-start(s32[128]{0:T(128)} %param.18) | copy-start | bytes 1540
  38.8 37.3 %copy-start.46 = (f32[128,4]{0,1:T(4,128)S(1)}, f32[128,4]{0,1:T(4,128)}, u32[]{:S(2)}) copy-start(f32[128,4]{0,1:T(4,128)} %param.20) | copy-start | bytes 6148
  38.8 37.4 %copy-start.39 = (s32[128,4]{0,1:T(4,128)S(1)}, s32[128,4]{0,1:T(4,128)}, u32[]{:S(2)}) copy-start(s32[128,4]{0,1:T(4,128)} %param.19) | copy-start | bytes 6148
  38.8 37.6 %copy-start.47 = (s32[1,512]{1,0:T(1,128)S(1)}, s32[1,512]{1,0:T(1,128)}, u32[]{:S(2)}) copy-start(s32[1,512]{1,0:T(1,128)} %param.21) | copy-start | bytes 6148
  38.8 38.4 %copy-start.48 = (bf16[64]{0:T(256)(128)(2,1)S(1)}, bf16[64]{0:T(256)(128)(2,1)}, u32[]{:S(2)}) copy-start(bf16[64]{0:T(256)(128)(2,1)} %param.22) | copy-start | bytes 388
  38.8 38.4 %copy-start.49 = (bf16[192]{0:T(256)(128)(2,1)S(1)}, bf16[192]{0:T(256)(128)(2,1)}, u32[]{:S(2)}) copy-start(bf16[192]{0:T(256)(128)(2,1)} %param.24) | copy-start | bytes 1156
  38.9 38.4 %copy-start.50 = (bf16[64]{0:T(256)(128)(2,1)S(1)}, bf16[64]{0:T(256)(128)(2,1)}, u32[]{:S(2)}) copy-start(bf16[64]{0:T(256)(128)(2,1)} %param.26) | copy-start | bytes 388
  38.9 38.4 %copy-start.51 = (bf16[64]{0:T(256)(128)(2,1)S(1)}, bf16[64]{0:T(256)(128)(2,1)}, u32[]{:S(2)}) copy-start(bf16[64]{0:T(256)(128)(2,1)} %param.27) | copy-start | bytes 388
  38.9 106.5 %copy-start.5 = (bf16[128,2048]{1,0:T(8,128)(2,1)S(1)}, bf16[128,2048]{1,0:T(8,128)(2,1)}, u32[]{:S(2)}) copy-start(bf16[128,2048]{1,0:T(8,128)(2,1)} %param.16) | copy-start | bytes 1572868
  40.9 155.6 %all-to-all-start.1 = ((bf16[32,64,352]{2,1,0:T(8,128)(2,1)}), bf16[32,64,352]{2,1,0:T(8,128)(2,1)}, u32[]{:S(2)}, u32[]{:S(2)}) async-start(bf16[32,64,352]{2,1,0:T(8,128)(2,1)} %reshape.364), calls=%async_computation.1 | async-start | bytes 3145728 | tf_op jit(solution)/shard_map/all_to_all | solution.py:527
  76.0 712.4 %reduce-scatter.6.cloned.1.call-start = ((), (), s32[]{:S(2)}) async-start(), calls=%async_computation.11 | async-start | bytes 3932160 | tf_op jit(solution)/shard_map/reduce_scatter | solution.py:686
  147.2 426.7 %copy-start.35 = (f32[2048]{0:T(1024)}, f32[2048]{0:T(1024)S(1)}, u32[]{:S(2)}) copy-start(f32[2048]{0:T(1024)S(1)} %mul.263) | copy-start | bytes 24580
  209.0 38.3 %collective-permute-start = (bf16[2,1024,256]{1,2,0:T(8,128)(2,1)S(1)}, bf16[2,1024,256]{1,2,0:T(8,128)(2,1)S(1)}, u32[]{:S(2)}, u32[]{:S(2)}) collective-permute-start(bf16[2,1024,256]{1,2,0:T(8,128)(2,1)S(1)} %pad_maximum_fusion.3), channel_id=1, source_target_pairs={{0,8},{1,9},{2,10},{3,11},{4,12},{5,13},{6,14},{7,15},{8,16},{9,17... | collective-permute-start | bytes 3145736 | tf_op jit(solution)/shard_map/ppermute | solution.py:583
  214.1 33.5 %copy-start.8 = (bf16[1024,2,128]{0,2,1:T(8,128)(2,1)}, bf16[1024,2,128]{0,2,1:T(8,128)(2,1)S(1)}, u32[]{:S(2)}) copy-start(bf16[1024,2,128]{0,2,1:T(8,128)(2,1)S(1)} %fusion.33) | copy-start | bytes 1572868
  293.2 280.7 %copy-start.3 = (f32[128,2048]{1,0:T(8,128)}, f32[128,2048]{1,0:T(8,128)S(1)}, u32[]{:S(2)}) copy-start(f32[128,2048]{1,0:T(8,128)S(1)} %get-tuple-element.25) | copy-start | bytes 3145732
  293.2 280.7 %copy-start.40 = (f32[128]{0:T(128)}, f32[128]{0:T(128)S(1)}, u32[]{:S(2)}) copy-start(f32[128]{0:T(128)S(1)} %add_rsqrt_fusion) | copy-start | bytes 1540
  462.2 112.3 %copy-start.17 = (bf16[128,2048]{1,0:T(8,128)(2,1)S(1)}, bf16[128,2048]{1,0:T(8,128)(2,1)}, u32[]{:S(2)}) copy-start(bf16[128,2048]{1,0:T(8,128)(2,1)} %param.17) | copy-start | bytes 1572868
  638.2 35.6 %collective-permute-start.2 = (bf16[2,1024,256]{1,2,0:T(8,128)(2,1)S(1)}, bf16[2,1024,256]{1,2,0:T(8,128)(2,1)S(1)}, u32[]{:S(2)}, u32[]{:S(2)}) collective-permute-start(bf16[2,1024,256]{1,2,0:T(8,128)(2,1)S(1)} %fusion.13), channel_id=1, source_target_pairs={{8,0},{9,1},{10,2},{11,3},{12,4},{13,5},{14,6},{15,7},{16,8},{17,9... | collective-permute-start | bytes 3145736 | tf_op jit(solution)/shard_map/ppermute | solution.py:670
  681.9 111.2 %reduce-scatter.8.cloned.1.call-start = ((), (), s32[]{:S(2)}) async-start(), calls=%async_computation.12 | async-start | bytes 1310720 | tf_op jit(solution)/shard_map/reduce_scatter | solution.py:703
  686.4 306.6 %reduce-scatter.4.cloned.1.call-start = ((), (), s32[]{:S(2)}) async-start(), calls=%async_computation.10 | async-start | bytes 17301504 | tf_op jit(solution)/shard_map/reduce_scatter | solution.py:618
  719.2 69.2 %all-to-all-start.3 = ((bf16[32,64,352]{2,1,0:T(8,128)(2,1)}), bf16[32,64,352]{2,1,0:T(8,128)(2,1)S(1)}, u32[]{:S(2)}, u32[]{:S(2)}) async-start(bf16[32,64,352]{2,1,0:T(8,128)(2,1)} %pad_maximum_fusion.2), calls=%async_computation.6 | async-start | bytes 3145728 | tf_op jit(solution)/shard_map/all_to_all | solution.py:628
  788.4 79.1 %all-to-all-start.2 = ((bf16[8,64,768]{2,1,0:T(8,128)(2,1)}), bf16[8,64,768]{2,1,0:T(8,128)(2,1)}, u32[]{:S(2)}, u32[]{:S(2)}) async-start(bf16[8,64,768]{2,1,0:T(8,128)(2,1)} %bitcast.195), calls=%async_computation.4 | async-start | bytes 1572864 | tf_op jit(solution)/shard_map/all_to_all | solution.py:689
  793.1 56.6 %collective-permute-start.3 = (bf16[64,2048]{1,0:T(8,128)(2,1)}, bf16[64,2048]{1,0:T(8,128)(2,1)S(1)}, u32[]{:S(2)}, u32[]{:S(2)}) collective-permute-start(bf16[64,2048]{1,0:T(8,128)(2,1)} %reduce-scatter.8.cloned.1.call-done), channel_id=1, source_target_pairs={{0,0},{1,4},{2,8},{3,12},{4,16},{5,20},{6,24},{7,28},{8,1},{9,5},{... | collective-permute-start | bytes 786440 | tf_op jit(solution)/shard_map/ppermute | solution.py:706
  867.5 125.5 %copy-start.1 = (f32[2,64,2048]{2,1,0:T(8,128)S(1)}, f32[2,64,2048]{2,1,0:T(8,128)}, u32[]{:S(2)}) copy-start(f32[2,64,2048]{2,1,0:T(8,128)} %copy-done) | copy-start | bytes 3145732
  867.5 125.5 %copy-start.4 = (f32[128,2048]{1,0:T(8,128)S(1)}, f32[128,2048]{1,0:T(8,128)}, u32[]{:S(2)}) copy-start(f32[128,2048]{1,0:T(8,128)} %copy-done.3) | copy-start | bytes 3145732
  867.6 125.5 %copy-start.36 = (f32[2048]{0:T(1024)S(1)}, f32[2048]{0:T(1024)}, u32[]{:S(2)}) copy-start(f32[2048]{0:T(1024)} %copy-done.35) | copy-start | bytes 24580
  867.6 125.5 %copy-start.41 = (f32[128]{0:T(128)S(1)}, f32[128]{0:T(128)}, u32[]{:S(2)}) copy-start(f32[128]{0:T(128)} %copy-done.40) | copy-start | bytes 1540
  867.6 125.5 %copy-start.45 = (f32[128]{0:T(128)S(1)}, f32[128]{0:T(128)}, u32[]{:S(2)}) copy-start(f32[128]{0:T(128)} %copy-done.44) | copy-start | bytes 1540
  (39 other events, 393.9 us)
Sparse Core Ops, SparseCore 0:
  27.8 95.6 all-gather.3
  125.0 26.9 all-gather.5
  154.9 124.6 all-gather.7
  682.0 71.2 reduce-scatter.5
  756.0 34.6 reduce-scatter.7
  792.9 200.0 reduce-scatter.3

commit v2 on v1

--- a/solution.py
+++ b/solution.py
@@ -18,11 +18,6 @@
 FL = jnp.float32
 AXIS = "fsdp"
 MESH = pl.DeviceIdType.MESH
-PLAN = {
-    1: (("f", 0), ("s", 0), ("z", 0)),
-    4: (("f", 0), ("f", 1), ("s", 0), ("f", 2), ("s", 1), ("f", 3), ("z", 0), ("s", 2), ("z", 1),
-        ("s", 3), ("z", 2), ("z", 3)),
-}
 
 
 def place(length):
@@ -50,9 +45,20 @@
     pl.semaphore_wait(barrier, peers)
 
 
-def gather_body(length, x_ref, o_ref, send_sem, recv_sem, own_sem):
+def line_order(p):
+    return [
+        p,
+        jnp.where(p == 0, 1, p - 1),
+        jnp.where(p == 0, 2, jnp.where(p == 3, 1, p + 1)),
+        jnp.where(p < 2, 3, 0),
+    ]
+
+
+def gather_body(length, x_ref, o_ref, send_sem, recv_sem, own_sem, line=None):
     p, y, x, c, device = place(length)
-    greet(length, p, device, y, x, c)
+    if line is None:
+        greet(length, p, device, y, x, c)
+        line = [lambda: None] * 5
 
     def block(h, z, yy, xx, cc):
         return o_ref.at[z, yy, xx, cc, h]
@@ -89,12 +95,7 @@
         own[h].start()
 
     if length == 4:
-        order = [
-            p,
-            jnp.where(p == 0, 1, p - 1),
-            jnp.where(p == 0, 2, jnp.where(p == 3, 1, p + 1)),
-            jnp.where(p < 2, 3, 0),
-        ]
+        order = line_order(p)
     else:
         order = [p]
 
@@ -142,6 +143,7 @@
                 arrived(h, seconds[i])
                 send(block(h, *seconds[i]), h, seconds[i], 9 * j + 7 + i, device(c=1 - c))
 
+    line[0]()
     stage_z(0)
     for j in range(length):
         if j + 1 < length:
@@ -150,12 +152,15 @@
         if j:
             stage_second(j - 1)
     stage_second(length - 1)
+    line[1]()
     for j in range(length):
         for h in range(2):
             for yy, xx in ((y, x), (1 - y, x), (y, 1 - x), (1 - y, 1 - x)):
                 arrived(h, (order[j], yy, xx, 1 - c))
     for h in range(2):
         own[h].wait()
+    for step in line[2:]:
+        step()
     for made, there in started:
         if there is None:
             made.wait_send()
@@ -181,19 +186,92 @@
     return out.reshape(8 * length * rows, width)
 
 
-def scatter_body(length, in_ref, o_ref, pair_in, near, first_in, second_in, z_in, total,
-                 send_sem, pair_sem, load_sem, first_sem, second_sem, z_sem):
+def layer_and_line_body(many, *refs):
+    x_ref, ins = refs[0], refs[1 : 1 + many]
+    o_ref, outs = refs[1 + many], refs[2 + many : 2 + 2 * many]
+    send_sem, recv_sem, own_sem, line_send, line_recv, line_own = refs[2 + 2 * many :]
+    p, y, x, c, device = place(4)
+    greet(4, p, device, y, x, c)
+    order = line_order(p)
+    started = []
+    own = [pltpu.make_async_copy(ins[k], outs[k].at[p], line_own.at[k]) for k in range(many)]
+
+    def copy(k, j, z, side):
+        return pltpu.make_async_remote_copy(
+            src_ref=outs[k].at[z] if j else ins[k],
+            dst_ref=outs[k].at[z],
+            send_sem=line_send.at[(k * 4 + j) * 2 + side],
+            recv_sem=line_recv.at[k * 4 + z],
+            device_id=(device(1 - 2 * side),),
+            device_id_type=MESH,
+        )
+
+    def stage(j):
+        z = order[j]
+        for k in range(many):
+            if j:
+                pltpu.make_async_remote_copy(
+                    src_ref=outs[k].at[z], dst_ref=outs[k].at[z], send_sem=line_send.at[0],
+                    recv_sem=line_recv.at[k * 4 + z], device_id=(device(c=1 - c),),
+                    device_id_type=MESH,
+                ).wait_recv()
+            else:
+                own[k].start()
+            for side, there in ((0, (p < 3) & (z <= p)), (1, (p > 0) & (z >= p))):
+                made = copy(k, j, z, side)
+                pl.when(there)(made.start)
+                started.append((made, there))
+
+    def finish():
+        for k in range(many):
+            own[k].wait()
+        for made, there in started:
+            pl.when(there)(made.wait_send)
+
+    line = [functools.partial(stage, j) for j in range(4)] + [finish]
+    gather_body(1, x_ref, o_ref, send_sem, recv_sem, own_sem, line)
+
+
+def layer_and_line(value, others, collective_id):
+    rows, width = value.shape
+    half = rows // 2
+    many = len(others)
+    outs = pl.pallas_call(
+        functools.partial(layer_and_line_body, many),
+        out_shape=[jax.ShapeDtypeStruct((1, 2, 2, 2, 2, half, width), value.dtype)]
+        + [jax.ShapeDtypeStruct((4,) + other.shape, other.dtype) for other in others],
+        in_specs=[pl.BlockSpec(memory_space=pltpu.VMEM)] * (1 + many),
+        out_specs=[pl.BlockSpec(memory_space=pl.ANY)] * (1 + many),
+        scratch_shapes=[
+            pltpu.SemaphoreType.DMA((18,)),
+            pltpu.SemaphoreType.DMA((16,)),
+            pltpu.SemaphoreType.DMA((2,)),
+            pltpu.SemaphoreType.DMA((8 * many,)),
+            pltpu.SemaphoreType.DMA((4 * many,)),
+            pltpu.SemaphoreType.DMA((many,)),
+        ],
+        compiler_params=pltpu.CompilerParams(collective_id=collective_id, has_side_effects=True),
+    )(value.reshape(2, half, width), *others)
+    return [outs[0].reshape(8 * rows, width)] + [
+        out.reshape((-1,) + out.shape[2:]) for out in outs[1:]
+    ]
+
+
+def scatter_body(length, many, *refs):
+    in_refs, o_refs = refs[:many], refs[many : 2 * many]
+    (pair_in, near, first_in, second_in, z_in, total,
+     send_sem, pair_sem, load_sem, first_sem, second_sem, z_sem) = refs[2 * many :]
     p, y, x, c, device = place(length)
     greet(length, p, device, y, x, c)
-    half, width = o_ref.shape[1:]
+    half, width = total.shape
     order = [3, 0, 2, 1] if length == 4 else [0]
-    step = min(16, half)
+    row_step = min(16, half)
     started = []
 
-    def part(h, z, far, cc):
-        if h == 0:
-            return in_ref.at[z, :, (1 - x if far else x), cc, h]
-        return in_ref.at[z, (1 - y if far else y), :, cc, h]
+    def part(g, z, far, cc):
+        if g % 2 == 0:
+            return in_refs[g // 2].at[z, :, (1 - x if far else x), cc, 0]
+        return in_refs[g // 2].at[z, (1 - y if far else y), :, cc, 1]
 
     def send(src, dst, slot, sem, target, there=None):
         made = pltpu.make_async_remote_copy(
@@ -210,89 +288,94 @@
     first_to = (device(x=1 - x), device(y=1 - y))
     second_to = (device(y=1 - y), device(x=1 - x))
     place_s = (y, x)
-    slot = lambda h, z, k: (h * length + z) * 6 + k
+    slot = lambda g, z, k: (g * length + z) * 6 + k
     pairs, loads, firsts, seconds = {}, {}, {}, {}
-    for far in (1, 0):
-        for z in order:
-            for h in range(2):
-                k = (h * length + z) * 2 + far
-                pairs[h, z, far] = send(
-                    part(h, z, far, 1 - c), pair_in.at[h, z, far], slot(h, z, far),
-                    pair_sem.at[k], device(c=1 - c),
-                )
-                loads[h, z, far] = pltpu.make_async_copy(
-                    part(h, z, far, c), near.at[h, z, far], load_sem.at[k]
-                )
-                loads[h, z, far].start()
+    steps = [(q, z) for q in range(many) for z in order]
+    for q in range(many):
+        for far in (1, 0):
+            for z in order:
+                for g in (2 * q, 2 * q + 1):
+                    k = (g * length + z) * 2 + far
+                    pairs[g, z, far] = send(
+                        part(g, z, far, 1 - c), pair_in.at[g, z, far], slot(g, z, far),
+                        pair_sem.at[k], device(c=1 - c),
+                    )
+                    loads[g, z, far] = pltpu.make_async_copy(
+                        part(g, z, far, c), near.at[g, z, far], load_sem.at[k]
+                    )
+                    loads[g, z, far].start()
 
     def add(target, sources):
         def body(i, _):
-            rows = pl.ds(pl.multiple_of(i * step, step), step)
+            rows = pl.ds(pl.multiple_of(i * row_step, row_step), row_step)
             value = sources[0][rows, :].astype(FL)
             for source in sources[1:]:
                 value = value + source[rows, :].astype(FL)
             target[rows, :] = value.astype(target.dtype)
             return 0
-        lax.fori_loop(0, half // step, body, 0)
-
-    def stage_first(z):
-        for h in range(2):
-            pairs[h, z, 1].wait_recv()
-            loads[h, z, 1].wait()
+        lax.fori_loop(0, half // row_step, body, 0)
+
+    def stage_first(q, z):
+        for g in (2 * q, 2 * q + 1):
+            pairs[g, z, 1].wait_recv()
+            loads[g, z, 1].wait()
             for s in range(2):
-                add(near.at[h, z, 1, s], [near.at[h, z, 1, s], pair_in.at[h, z, 1, s]])
-            firsts[h, z] = send(
-                near.at[h, z, 1], first_in.at[h, z], slot(h, z, 2),
-                first_sem.at[h * length + z], first_to[h],
+                add(near.at[g, z, 1, s], [near.at[g, z, 1, s], pair_in.at[g, z, 1, s]])
+            firsts[g, z] = send(
+                near.at[g, z, 1], first_in.at[g, z], slot(g, z, 2),
+                first_sem.at[g * length + z], first_to[g % 2],
             )
 
-    def stage_second(z):
-        for h in range(2):
-            s = 1 - place_s[h]
-            pairs[h, z, 0].wait_recv()
-            loads[h, z, 0].wait()
-            firsts[h, z].wait_recv()
-            add(near.at[h, z, 0, s],
-                [near.at[h, z, 0, s], pair_in.at[h, z, 0, s], first_in.at[h, z, s]])
-            seconds[h, z] = send(
-                near.at[h, z, 0, s], second_in.at[h, z], slot(h, z, 3),
-                second_sem.at[h * length + z], second_to[h],
+    def stage_second(q, z):
+        for g in (2 * q, 2 * q + 1):
+            s = 1 - place_s[g % 2]
+            pairs[g, z, 0].wait_recv()
+            loads[g, z, 0].wait()
+            firsts[g, z].wait_recv()
+            add(near.at[g, z, 0, s],
+                [near.at[g, z, 0, s], pair_in.at[g, z, 0, s], first_in.at[g, z, s]])
+            seconds[g, z] = send(
+                near.at[g, z, 0, s], second_in.at[g, z], slot(g, z, 3),
+                second_sem.at[g * length + z], second_to[g % 2],
             )
 
-    def stage_z(z):
-        for h in range(2):
-            s = place_s[h]
-            seconds[h, z].wait_recv()
-            sources = [near.at[h, z, 0, s], pair_in.at[h, z, 0, s], first_in.at[h, z, s],
-                       second_in.at[h, z]]
+    def stage_z(q, z):
+        for g in (2 * q, 2 * q + 1):
+            s = place_s[g % 2]
+            o_half = o_refs[q].at[g % 2]
+            seconds[g, z].wait_recv()
+            sources = [near.at[g, z, 0, s], pair_in.at[g, z, 0, s], first_in.at[g, z, s],
+                       second_in.at[g, z]]
             if length == 1:
-                add(o_ref.at[h], sources)
+                add(o_half, sources)
                 continue
-            add(total.at[h, z], sources)
+            add(total, sources)
             for side, sender in ((0, (p > 0) & (p <= z)), (1, (p < length - 1) & (p >= z))):
                 @pl.when(sender)
                 def _():
-                    k = (h * length + z) * 2 + side
+                    k = (g * length + z) * 2 + side
                     pltpu.make_async_remote_copy(
-                        src_ref=near.at[h, z, 0, s], dst_ref=z_in.at[h, z, side],
+                        src_ref=near.at[g, z, 0, s], dst_ref=z_in.at[g, z, side],
                         send_sem=send_sem.at[0], recv_sem=z_sem.at[k],
                         device_id=(device(c=1 - c),), device_id_type=MESH,
                     ).wait_recv()
-                    add(total.at[h, z], [total.at[h, z], z_in.at[h, z, side]])
+                    add(total, [total, z_in.at[g, z, side]])
             @pl.when(p == z)
             def _():
-                add(o_ref.at[h], [total.at[h, z]])
+                add(o_half, [total])
             @pl.when(p != z)
             def _():
-                add(near.at[h, z, 0, s], [total.at[h, z]])
-            send(near.at[h, z, 0, s], z_in.at[h, z, 0], slot(h, z, 4),
-                 z_sem.at[(h * length + z) * 2], device(1), p < z)
-            send(near.at[h, z, 0, s], z_in.at[h, z, 1], slot(h, z, 5),
-                 z_sem.at[(h * length + z) * 2 + 1], device(-1), p > z)
-
-    stages = {"f": stage_first, "s": stage_second, "z": stage_z}
-    for kind, i in PLAN[length]:
-        stages[kind](order[i])
+                add(near.at[g, z, 0, s], [total])
+            send(near.at[g, z, 0, s], z_in.at[g, z, 0], slot(g, z, 4),
+                 z_sem.at[(g * length + z) * 2], device(1), p < z)
+            send(near.at[g, z, 0, s], z_in.at[g, z, 1], slot(g, z, 5),
+                 z_sem.at[(g * length + z) * 2 + 1], device(-1), p > z)
+
+    count = len(steps)
+    for i in range(count + 3):
+        for stage, j in ((stage_first, i), (stage_z, i - 3), (stage_second, i - 1)):
+            if 0 <= j < count:
+                stage(*steps[j])
     for made, there in started:
         if there is None:
             made.wait_send()
@@ -300,33 +383,36 @@
             pl.when(there)(made.wait_send)
 
 
-def scatter(value, length, collective_id):
-    rows, width = value.shape[0] // (8 * length), value.shape[1]
+def scatter(values, length, collective_id):
+    many = len(values)
+    rows, width = values[0].shape[0] // (8 * length), values[0].shape[1]
     half = rows // 2
-    out = pl.pallas_call(
-        functools.partial(scatter_body, length),
-        out_shape=jax.ShapeDtypeStruct((2, half, width), FL),
-        in_specs=[pl.BlockSpec(memory_space=pl.ANY)],
-        out_specs=pl.BlockSpec(memory_space=pltpu.VMEM),
+    kind = values[0].dtype
+    lanes = 2 * many
+    outs = pl.pallas_call(
+        functools.partial(scatter_body, length, many),
+        out_shape=[jax.ShapeDtypeStruct((2, half, width), FL)] * many,
+        in_specs=[pl.BlockSpec(memory_space=pl.ANY)] * many,
+        out_specs=[pl.BlockSpec(memory_space=pltpu.VMEM)] * many,
         scratch_shapes=[
-            pltpu.VMEM((2, length, 2, 2, half, width), value.dtype),
-            pltpu.VMEM((2, length, 2, 2, half, width), value.dtype),
-            pltpu.VMEM((2, length, 2, half, width), value.dtype),
-            pltpu.VMEM((2, length, half, width), value.dtype),
-            pltpu.VMEM((2, length, 2, half, width), value.dtype),
-            pltpu.VMEM((2, length, half, width), FL),
-            pltpu.SemaphoreType.DMA((12 * length,)),
-            pltpu.SemaphoreType.DMA((4 * length,)),
-            pltpu.SemaphoreType.DMA((4 * length,)),
-            pltpu.SemaphoreType.DMA((2 * length,)),
-            pltpu.SemaphoreType.DMA((2 * length,)),
-            pltpu.SemaphoreType.DMA((4 * length,)),
+            pltpu.VMEM((lanes, length, 2, 2, half, width), kind),
+            pltpu.VMEM((lanes, length, 2, 2, half, width), kind),
+            pltpu.VMEM((lanes, length, 2, half, width), kind),
+            pltpu.VMEM((lanes, length, half, width), kind),
+            pltpu.VMEM((lanes, length, 2, half, width), kind),
+            pltpu.VMEM((half, width), FL),
+            pltpu.SemaphoreType.DMA((6 * lanes * length,)),
+            pltpu.SemaphoreType.DMA((2 * lanes * length,)),
+            pltpu.SemaphoreType.DMA((2 * lanes * length,)),
+            pltpu.SemaphoreType.DMA((lanes * length,)),
+            pltpu.SemaphoreType.DMA((lanes * length,)),
+            pltpu.SemaphoreType.DMA((2 * lanes * length,)),
         ],
         compiler_params=pltpu.CompilerParams(
-            collective_id=collective_id, has_side_effects=True, vmem_limit_bytes=50 << 20
+            collective_id=collective_id, has_side_effects=True, vmem_limit_bytes=62 << 20
         ),
-    )(value.reshape(length, 2, 2, 2, 2, half, width))
-    return out.reshape(rows, width)
+    )(*[value.reshape(length, 2, 2, 2, 2, half, width) for value in values])
+    return [out.reshape(rows, width) for out in outs]
 
 
 def dot(a, b, dims=((1,), (0,))):
@@ -468,7 +554,7 @@
 
     def team_scatter(value, call):
         if layered:
-            return scatter(value, 1, call)
+            return scatter([value], 1, call)[0]
         return lax.psum_scatter(
             value, AXIS, scatter_dimension=0, tiled=True, axis_index_groups=in_team
         )
@@ -491,6 +577,7 @@
         small = gather(packed, teams, 6).reshape(count, 16 * lanes)[:, :entries]
     else:
         small = lax.all_gather(packed[None], AXIS, axis=0, tiled=True)
+    qkv_weight, small = lax.optimization_barrier((qkv_weight, small))
     edge = share
     gain_in = small[:, :edge].reshape(1, width)
     bias = small[:, edge : edge + bias_share].reshape(3, heads, HEAD_DIM)
@@ -513,15 +600,23 @@
         tiled=True,
         axis_index_groups=in_team,
     )
-    w_qkv = lax.all_gather(
-        mine.reshape(team * share, 3 * span), AXIS, axis=0, tiled=True, axis_index_groups=across
-    )
     deal = [(p * teams + s, s * team + p) for s in range(teams) for p in range(team)]
-    w_out = lax.all_gather(
-        lax.ppermute(out_weight, AXIS, deal),
-        AXIS, axis=0, tiled=True, axis_index_groups=across,
-    )
+    mine = mine.reshape(team * share, 3 * span)
+    out_rows = lax.ppermute(out_weight, AXIS, deal)
+    inputs = tokens.astype(FL)
+    scale_in = lax.rsqrt(jnp.mean(inputs * inputs, axis=-1, keepdims=True) + EPSILON)
+    normed = (inputs * scale_in * gain_in).astype(BF)
+    if layered:
+        normed, w_qkv, w_out = layer_and_line(normed, [mine, out_rows], 0)
+    else:
+        normed = team_gather(normed, 0)
+        w_qkv, w_out = [
+            lax.all_gather(value, AXIS, axis=0, tiled=True, axis_index_groups=across)
+            for value in (mine, out_rows)
+        ]
     bias_own = lax.dynamic_slice_in_dim(bias, seat * own, own, 1).reshape(1, 3 * span)
+
+    shared_in, normed = lax.optimization_barrier((shared_in, normed))
 
     shared_cols = shared_in.reshape(share, 2, count, hid_s).transpose(2, 0, 1, 3)
     w_shared = lax.all_to_all(
@@ -531,35 +626,8 @@
         concat_axis=0,
         tiled=True,
     ).reshape(width, 2 * hid_s)
-    wide_s = -(-(hid_s + 1) // 128) * 128
-    wide_e = -(-hid_e // 128) * 128
-    full = wide_s + wide_e
-
-    def columns(value, wide):
-        return jnp.pad(value, ((0, 0), (0, wide - value.shape[1])))
-
-    gate_side = jnp.concatenate([w_shared[:, :hid_s], gate.reshape(width, 1).astype(BF)], axis=1)
-    w1 = jnp.concatenate(
-        [
-            columns(gate_side, wide_s),
-            columns(expert_in[0][:, :hid_e], wide_e),
-            columns(w_shared[:, hid_s:], wide_s),
-            columns(expert_in[0][:, hid_e:], wide_e),
-        ],
-        axis=1,
-    )
-    w2 = jnp.concatenate(
-        [
-            jnp.pad(shared_out, ((0, wide_s - hid_s), (0, 0))),
-            jnp.pad(expert_out[0], ((0, wide_e - hid_e), (0, 0))),
-        ],
-        axis=0,
-    )
     grad_all = lax.all_gather(cotangent, AXIS, axis=0, tiled=True)
 
-    inputs = tokens.astype(FL)
-    scale_in = lax.rsqrt(jnp.mean(inputs * inputs, axis=-1, keepdims=True) + EPSILON)
-    normed = team_gather((inputs * scale_in * gain_in).astype(BF), 0)
     own_ids = lax.dynamic_slice_in_dim(ids_all, slab * team, team, 0).reshape(SEQ)
     prev_ids = lax.dynamic_slice_in_dim(
         ids_all, jnp.maximum(slab - 1, 0) * team, team, 0
@@ -600,6 +668,31 @@
     probs = jnp.exp(scores - log_total).astype(BF)
     attended = jnp.einsum("hqk,khd->qhd", probs, window[1], preferred_element_type=FL)
     attended = attended.reshape(SEQ, span).astype(BF)
+    w_shared, attended = lax.optimization_barrier((w_shared, attended))
+    wide_s = -(-(hid_s + 1) // 128) * 128
+    wide_e = -(-hid_e // 128) * 128
+    full = wide_s + wide_e
+
+    def columns(value, wide):
+        return jnp.pad(value, ((0, 0), (0, wide - value.shape[1])))
+
+    gate_side = jnp.concatenate([w_shared[:, :hid_s], gate.reshape(width, 1).astype(BF)], axis=1)
+    w1 = jnp.concatenate(
+        [
+            columns(gate_side, wide_s),
+            columns(expert_in[0][:, :hid_e], wide_e),
+            columns(w_shared[:, hid_s:], wide_s),
+            columns(expert_in[0][:, hid_e:], wide_e),
+        ],
+        axis=1,
+    )
+    w2 = jnp.concatenate(
+        [
+            jnp.pad(shared_out, ((0, wide_s - hid_s), (0, 0))),
+            jnp.pad(expert_out[0], ((0, wide_e - hid_e), (0, 0))),
+        ],
+        axis=0,
+    )
     hidden = inputs + team_scatter(dot(attended, w_out).astype(BF), 1).astype(FL)
     scale_mid = lax.rsqrt(jnp.mean(hidden * hidden, axis=-1, keepdims=True) + EPSILON)
     mid = (hidden * scale_mid * gain_mid).astype(BF)
@@ -612,10 +705,10 @@
         mid_all, grad_all, expert_weight[:, None], w1, w2, hid_s, wide_s
     )
     if layered:
-        summed_mid = scatter(mid_part, teams, 3)
+        summed_mid, summed_out = scatter([mid_part, out_part], teams, 3)
     else:
         summed_mid = lax.psum_scatter(mid_part, AXIS, scatter_dimension=0, tiled=True)
-    summed_out = lax.psum_scatter(out_part, AXIS, scatter_dimension=0, tiled=True)
+        summed_out = lax.psum_scatter(out_part, AXIS, scatter_dimension=0, tiled=True)
     d_w1 = dot(mid_all, d_pre, ((0,), (0,)))
     d_w2 = dot(act_low, grad_all, ((0,), (0,)))
     shared_out_grad = d_w2[:hid_s]
@@ -632,12 +725,6 @@
         concat_axis=0,
         tiled=True,
     )
-    shared_in_grad = (
-        shared_back.reshape(count, share, 2, hid_s)
-        .transpose(1, 2, 0, 3)
-        .reshape(share, -1)
-        .astype(FL)
-    )
     output = (hidden + summed_out.astype(FL)).astype(BF)
 
     grad_out = cotangent.astype(FL)
@@ -653,7 +740,13 @@
     d_hidden = grad_out + d_hidden_part
     d_attn = team_gather(d_hidden.astype(BF), 4)
     d_attended = dot(d_attn, w_out, ((1,), (1,))).astype(BF)
-    out_grad = dot(attended, d_attn, ((0,), (0,)))
+    out_grad = dot(attended, d_attn, ((0,), (0,))).astype(BF)
+    out_part_grad = lax.psum_scatter(
+        out_grad, AXIS, scatter_dimension=0, tiled=True, axis_index_groups=across
+    )
+    out_weight_grad = lax.ppermute(
+        out_part_grad, AXIS, [(target, source) for source, target in deal]
+    ).astype(FL)
     d_attended = d_attended.reshape(SEQ, own, HEAD_DIM)
     attention = jnp.exp(masked_scores() - log_total)
     d_attention = jnp.einsum("qhd,khd->hqk", d_attended, window[1], preferred_element_type=FL)
@@ -677,7 +770,14 @@
         ],
         axis=1,
     ).astype(BF)
+    d_projected, out_weight_grad = lax.optimization_barrier((d_projected, out_weight_grad))
     d_normed = team_scatter(dot(d_projected, w_qkv, ((1,), (1,))).astype(BF), 5).astype(FL)
+    shared_in_grad = (
+        shared_back.reshape(count, share, 2, hid_s)
+        .transpose(1, 2, 0, 3)
+        .reshape(share, -1)
+        .astype(FL)
+    )
     d_inputs, gain_in_grad = norm_back(inputs, scale_in, gain_in, d_normed)
     input_grad = d_hidden + d_inputs
     qkv_grad = dot(normed, d_projected, ((0,), (0,)))
@@ -700,12 +800,6 @@
         .reshape(share, 3 * width)
         .astype(FL)
     )
-    out_part_grad = lax.psum_scatter(
-        out_grad.astype(BF), AXIS, scatter_dimension=0, tiled=True, axis_index_groups=across
-    )
-    out_weight_grad = lax.ppermute(
-        out_part_grad, AXIS, [(target, source) for source, target in deal]
-    ).astype(FL)
     bias_spread = lax.dynamic_update_slice_in_dim(
         jnp.zeros((3, heads, HEAD_DIM), FL), bias_grad, seat * own, 1
     )
@@ -722,7 +816,8 @@
         entries = small_grads.shape[1]
         lanes = -(-entries // 2048) * 128
         small_grads = jnp.pad(small_grads, ((0, 0), (0, 16 * lanes - entries)))
-        small_sum = scatter(small_grads.reshape(count * 16, lanes), teams, 7).reshape(-1)[:entries]
+        small_sum = scatter([small_grads.reshape(count * 16, lanes)], teams, 7)[0]
+        small_sum = small_sum.reshape(-1)[:entries]
     else:
         small_sum = lax.psum_scatter(small_grads, AXIS, scatter_dimension=0, tiled=True)[0]
     return (

time: 1010 us -> 952 us (0.943)
  waiting for transfers between devices: 182 us -> 29.9 us
  Pallas kernels: 503 us -> 583 us
  local copies, waits for them, and re-layouts: 70.7 us -> 90.4 us
  other arithmetic: 50.5 us -> 69.4 us
  blocking collectives: 17.6 us -> 0 us
  starting transfers between devices: 49.4 us -> 38 us
    pallas_call x4 -> x5, Pallas kernels: 218 us -> 383 us  [the longest x4 260 us: scatter(): pl.pallas_call(functools.partial(scatter_body, length, many), out_shape=[...]
    reduce_scatter x2 -> x1, waiting for transfers between devices: 118 us -> 0.01 us  [per_device(): lax.psum_scatter(out_grad, AXIS, scatter_dimension=0, tiled=True, axis_in...]
    pallas_call x4 -> x3, Pallas kernels: 205 us -> 120 us  [gather(): pl.pallas_call(functools.partial(gather_body, length), out_shape=jax.Shap...]
    ppermute x1, waiting for transfers between devices: 33.1 us -> 0.01 us  [per_device(): passed = lax.ppermute(key_value, AXIS, forward)]
    all_to_all x1, starting transfers between devices: 35.1 us -> 3.42 us  [per_device(): lax.all_to_all(shared_cols.reshape(count, share, 2 * hid_s), AXIS, split_...]
    all_to_all x1 -> x0, blocking collectives: 17.6 us -> none  [per_device(): lax.all_to_all(mine.reshape(team, share, 3 * span), AXIS, split_axis=0, c...]
    all_to_all x1, starting transfers between devices: 3.8 us -> 19.3 us  [per_device(): lax.all_to_all(d_shared.astype(BF).reshape(count, share, 2 * hid_s), AXIS...]
    ppermute x1, waiting for transfers between devices: 30.6 us -> 15.3 us  [per_device(): returned = lax.ppermute(d_kv[:, :SEQ].astype(BF), AXIS, backward).astype(FL)]
  transfers between devices with their start and end apart: 13 -> 11, of which waited for: 3 -> 2; matrix products, arithmetic and copies ran while one was open for 18% -> 22% of each run, Pallas kernels for 29% -> 32%
where the time goes in v2:
time: 952 us; the launch traced here: 942 us
  Pallas kernels  583 us (61%)
  matrix products  117 us (12%)
  local copies, waits for them, and re-layouts  90.4 us (9%)
  other arithmetic  69.4 us (7%)
  starting transfers between devices  38 us (4%)
  waiting for transfers between devices  29.9 us (3%)
  between operations  15.2 us (2%)
    pallas_call x4, Pallas kernels, scatter(): pl.pallas_call(functools.partial(scatter_body, length, many), out_shape=[...  260 us
    pallas_call x1, Pallas kernels, layer_and_line(): pl.pallas_call(functools.partial(layer_and_line_body, many), out_shape=[j...  122 us
    pallas_call x3, Pallas kernels, gather(): pl.pallas_call(functools.partial(gather_body, length), out_shape=jax.Shap...  120 us
    pallas_call x1, Pallas kernels, feed(): pl.pallas_call(functools.partial(feed_body, gate_column=gate_column, shar...  80.4 us
    dot_general x8, matrix products, dot(): return lax.dot_general(a, b, (dims, ((), ())), preferred_element_type=FL)  74.5 us
    all_to_all x1, starting transfers between devices, per_device(): lax.all_to_all(d_shared.astype(BF).reshape(count, share, 2 * hid_s), AXIS...  19.3 us
  transfers between devices with their start and end apart: 11, of which 2 were waited for; matrix products, arithmetic and copies ran while one was open for 22% of the time, Pallas kernels for 32%

profile of v2, /device:TPU:0, one launch (start us, length us, event | category | flops | bytes accessed | tf_op | source)
XLA Modules:
  0.0 942.3 jit_solution(3603511833765491824)
XLA Ops:
  15.8 22.3 %shard_map.247 = f32[4,2,2,2,2,8,128]{6,5,4,3,2,1,0:T(8,128)} custom-call(f32[2,8,128]{2,1,0:T(8,128)} %pad_bitcast_fusion.x_ref), custom_call_target="tpu_custom_call" | custom-call | tf_op jit(solution)/shard_map/pallas_call | solution.py:174
  50.0 4.6 copy.79
  72.9 122.4 %shard_map.248 = (bf16[1,2,2,2,2,64,2048]{6,5,4,3,2,1,0:T(8,128)(2,1)}, bf16[4,512,768]{2,1,0:T(8,128)(2,1)}, bf16[4,64,2048]{2,1,0:T(8,128)(2,1)}) custom-call(bf16[2,64,2048]{2,1,0:T(8,128)(2,1)} %bitcast.189, bf16[512,768]{1,0:T(8,128)(2,1)} %bitcast.6.refs_1_, bf16[64,2048]{1,0:T(8,128)(2,1)} %copy-done.36), custom_call_target="tpu_custom_call" | custom-call | tf_op jit(solution)/shard_map/pallas_call | solution.py:239
  195.3 6.2 convolution_add_fusion
  209.7 5.8 reshape.365
  215.5 5.1 copy.75
  220.6 5.7 reshape.366
  240.3 5.2 exponential_reduce_fusion
  246.1 7.3 convolution_convert_fusion.4
  253.4 13.9 %all-to-all-done.1 = bf16[32,64,352]{2,1,0:T(8,128)(2,1)} async-done(((bf16[32,64,352]{2,1,0:T(8,128)(2,1)}), bf16[32,64,352]{2,1,0:T(8,128)(2,1)}, u32[]{:S(2)}, u32[]{:S(2)}) %all-to-all-start.1) | async-done | bytes 1441824 | tf_op jit(solution)/shard_map/all_to_all | solution.py:622
  267.3 4.7 convolution_convert_fusion
  272.0 26.4 %shard_map.249 = f32[2,64,2048]{2,1,0:T(8,128)} custom-call(bf16[1,2,2,2,2,64,2048]{6,5,4,3,2,1,0:T(8,128)(2,1)} %bitcast.156), custom_call_target="tpu_custom_call" | custom-call | tf_op jit(solution)/shard_map/pallas_call | solution.py:392
  301.0 73.6 %shard_map.250 = bf16[4,2,2,2,2,64,2048]{6,5,4,3,2,1,0:T(8,128)(2,1)} custom-call(bf16[2,64,2048]{2,1,0:T(8,128)(2,1)} %bitcast.188), custom_call_target="tpu_custom_call" | custom-call | tf_op jit(solution)/shard_map/pallas_call | solution.py:174
  380.2 80.4 %shard_map.251 = (bf16[4096,2048]{1,0:T(8,128)(2,1)}, bf16[4096,2048]{1,0:T(8,128)(2,1)}, bf16[4096,640]{1,0:T(8,128)(2,1)}, bf16[4096,1280]{1,0:T(8,128)(2,1)}) custom-call(bf16[4096,2048]{1,0:T(8,128)(2,1)} %bitcast.157, bf16[4096,2048]{1,0:T(8,128)(2,1)} %all-gather.2.cloned.1.call-done.grad_ref, f32[4096,1]{1,0:T(8,128)} %copy.80.weight_ref, ...), custom_call_target="tpu_custom_call" | custom-call | flops 64424509440 | bytes 100663296 | tf_op jit(solution)/shard_map/pallas_call | solution.py:458
  460.5 173.9 %shard_map.252 = (f32[2,64,2048]{2,1,0:T(8,128)}, f32[2,64,2048]{2,1,0:T(8,128)}) custom-call(bf16[4,2,2,2,2,64,2048]{6,5,4,3,2,1,0:T(8,128)(2,1)} %bitcast.159, bf16[4,2,2,2,2,64,2048]{6,5,4,3,2,1,0:T(8,128)(2,1)} %bitcast.160), custom_call_target="tpu_custom_call" | custom-call | tf_op jit(solution)/shard_map/pallas_call | solution.py:392
  638.4 23.6 %shard_map.253 = bf16[1,2,2,2,2,64,2048]{6,5,4,3,2,1,0:T(8,128)(2,1)} custom-call(bf16[2,64,2048]{2,1,0:T(8,128)(2,1)} %bitcast.190), custom_call_target="tpu_custom_call" | custom-call | tf_op jit(solution)/shard_map/pallas_call | solution.py:174
  666.0 12.9 %multiply_reduce_fusion = (f32[2,1024]{1,0:T(2,128)S(1)}, f32[2,1024,2048]{2,1,0:T(8,128)}) fusion(f32[2,1024,2048]{2,1,0:T(8,128)} %copy-done, f32[2,1024]{1,0:T(2,128)S(1)} %log_add_fusion, pred[1024,2048]{1,0:T(8,128)(4,1)S(1)} %copy-done.3, bf16[1024,2,128]{0,2,1:T(8,128)(2,1)S(1)} %bitcast.201, bf16[2048,2,128]{0,2,1:T(8,128)(2,1)S(1)} %bitcast.182), kind=kOutput, calls=%fused_computation.1 | convolution fusion | flops 1094711296 | bytes 37240832 | tf_op jit(solution)/shard_map/qhd,khd->hqk/dot_general | solution.py:752
  678.9 10.2 %fusion.43 = f32[2,128,2048]{2,1,0:T(8,128)} fusion(bf16[1024,2,128]{0,2,1:T(8,128)(2,1)S(1)} %bitcast.202, f32[2,1024,2048]{2,1,0:T(8,128)} %copy-done, f32[2,1024]{1,0:T(2,128)S(1)} %log_add_fusion, pred[1024,2048]{1,0:T(8,128)(4,1)S(1)} %copy-done.3), kind=kOutput, calls=%fused_computation.135 | convolution fusion | flops 1090519040 | bytes 21504000 | tf_op jit(solution)/shard_map/hqk,qhd->khd/dot_general | solution.py:759
  691.3 12.2 %multiply_convert_fusion = bf16[2,1024,2048]{2,1,0:T(8,128)(2,1)S(1)} fusion(f32[2,1024,2048]{2,1,0:T(8,128)} %get-tuple-element.86, f32[2,1024,2048]{2,1,0:T(8,128)} %copy-done, f32[2,1024]{1,0:T(2,128)S(1)} %get-tuple-element.85, f32[2,1024]{1,0:T(2,128)S(1)} %log_add_fusion, pred[1024,2048]{1,0:T(8,128)(4,1)S(1)} %copy-done.3), kind=kLoop, calls=%fused_computation | loop fusion | flops 25165824 | bytes 44056576 | tf_op jit(solution)/shard_map/convert_element_type | solution.py:754
  709.8 29.8 %fusion.55 = (bf16[2048,1280]{0,1:T(8,128)(2,1)}, f32[2048,1280]{0,1:T(8,128)}) fusion(bf16[4096,2048]{1,0:T(8,128)(2,1)} %bitcast.158, bf16[4096,1280]{1,0:T(8,128)(2,1)} %get-tuple-element.43), kind=kOutput, calls=%fused_computation.145 | convolution fusion | flops 21477457920 | bytes 42991616 | tf_op jit(solution)/shard_map/dot_general | solution.py:419
  739.6 6.4 broadcast_multiply_fusion
  747.2 15.3 %collective-permute-done.2 = bf16[2,1024,256]{1,2,0:T(8,128)(2,1)S(1)} collective-permute-done((bf16[2,1024,256]{1,2,0:T(8,128)(2,1)}, bf16[2,1024,256]{1,2,0:T(8,128)(2,1)S(1)}, u32[]{:S(2)}, u32[]{:S(2)}) %collective-permute-start.2) | collective-permute-done | bytes 1048608 | tf_op jit(solution)/shard_map/ppermute | solution.py:763
  770.3 4.9 convolution_convert_fusion.2
  779.5 19.3 %all-to-all-start.3 = ((bf16[32,64,352]{2,1,0:T(8,128)(2,1)}), bf16[32,64,352]{2,1,0:T(8,128)(2,1)}, u32[]{:S(2)}, u32[]{:S(2)}) async-start(bf16[32,64,352]{2,1,0:T(8,128)(2,1)} %pad_maximum_fusion.2), calls=%async_computation.5 | async-start | bytes 3145728 | tf_op jit(solution)/shard_map/all_to_all | solution.py:721
  798.8 17.6 %fusion.56 = f32[640,2048]{1,0:T(8,128)} fusion(bf16[4096,640]{1,0:T(8,128)(2,1)} %get-tuple-element.45, bf16[4096,2048]{1,0:T(8,128)(2,1)} %all-gather.2.cloned.1.call-done.grad_ref), kind=kOutput, calls=%fused_computation.146 | convolution fusion | flops 10737418240 | bytes 27262976 | tf_op jit(solution)/shard_map/dot_general | solution.py:419
  816.4 4.8 fusion.46
  831.6 5.1 convolution_convert_fusion.1
  836.7 28.6 %shard_map.254 = f32[2,64,2048]{2,1,0:T(8,128)} custom-call(bf16[1,2,2,2,2,64,2048]{6,5,4,3,2,1,0:T(8,128)(2,1)} %bitcast.175), custom_call_target="tpu_custom_call" | custom-call | tf_op jit(solution)/shard_map/pallas_call | solution.py:392
  869.8 31.3 %shard_map.255 = f32[2,8,128]{2,1,0:T(8,128)} custom-call(f32[4,2,2,2,2,8,128]{6,5,4,3,2,1,0:T(8,128)} %bitcast.196), custom_call_target="tpu_custom_call" | custom-call | tf_op jit(solution)/shard_map/pallas_call | solution.py:392
  912.0 6.2 reshape.397
  918.1 6.6 copy.86
  924.8 5.5 reshape.395
  (238 shorter events, 129.2 us)
Async XLA Ops:
  7.2 373.0 %all-gather.2.cloned.1.call-start = ((), (), s32[]{:S(2)}) async-start(), calls=%async_computation.6 | async-start | bytes 17301504 | tf_op jit(solution)/shard_map/all_gather | solution.py:629
  9.5 37.3 %copy-start.50 = (bf16[64,2048]{1,0:T(8,128)(2,1)S(1)}, bf16[64,2048]{1,0:T(8,128)(2,1)}, u32[]{:S(2)}) copy-start(bf16[64,2048]{1,0:T(8,128)(2,1)} %param.25) | copy-start | bytes 786436
  42.6 29.6 %all-to-all-start = ((bf16[8,64,768]{2,1,0:T(8,128)(2,1)}), bf16[8,64,768]{2,1,0:T(8,128)(2,1)}, u32[]{:S(2)}, u32[]{:S(2)}) async-start(bf16[8,64,768]{2,1,0:T(8,128)(2,1)} %reshape.362), calls=%async_computation | async-start | bytes 1572864 | tf_op jit(solution)/shard_map/all_to_all | solution.py:595
  46.8 25.3 %collective-permute-start = (bf16[64,2048]{1,0:T(8,128)(2,1)S(1)}, bf16[64,2048]{1,0:T(8,128)(2,1)S(1)}, u32[]{:S(2)}, u32[]{:S(2)}) collective-permute-start(bf16[64,2048]{1,0:T(8,128)(2,1)S(1)} %copy-done.50), channel_id=1, source_target_pairs={{0,0},{4,1},{8,2},{12,3},{16,4},{20,5},{24,6},{28,7},{1,8},{5,9},{... | collective-permute-start | bytes 786440 | tf_op jit(solution)/shard_map/ppermute | solution.py:605
  47.7 19.7 %copy-start.39 = (f32[2048]{0:T(1024)}, f32[2048]{0:T(1024)S(1)}, u32[]{:S(2)}) copy-start(f32[2048]{0:T(1024)S(1)} %mul.240) | copy-start | bytes 24580
  47.9 588.1 %copy-start.37 = (f32[2048]{0:T(1024)}, f32[2048]{0:T(1024)S(1)}, u32[]{:S(2)}) copy-start(f32[2048]{0:T(1024)S(1)} %mul.263) | copy-start | bytes 24580
  64.3 131.0 %copy-start.43 = (f32[128]{0:T(128)}, f32[128]{0:T(128)S(1)}, u32[]{:S(2)}) copy-start(f32[128]{0:T(128)S(1)} %add_rsqrt_fusion.1) | copy-start | bytes 1540
  67.4 178.2 %copy-start.2 = (pred[1024,2048]{1,0:T(8,128)(4,1)}, pred[1024,2048]{1,0:T(8,128)(4,1)S(1)}, u32[]{:S(2)}) copy-start(pred[1024,2048]{1,0:T(8,128)(4,1)S(1)} %fusion.5) | copy-start | bytes 6291460
  206.0 27.1 %collective-permute-start.1 = (bf16[2,1024,256]{1,2,0:T(8,128)(2,1)}, bf16[2,1024,256]{1,2,0:T(8,128)(2,1)}, u32[]{:S(2)}, u32[]{:S(2)}) collective-permute-start(bf16[2,1024,256]{1,2,0:T(8,128)(2,1)} %pad_maximum_fusion.3), channel_id=1, source_target_pairs={{0,8},{1,9},{2,10},{3,11},{4,12},{5,13},{6,14},{7,15},{8,16},{9,17... | collective-permute-start | bytes 3145736 | tf_op jit(solution)/shard_map/ppermute | solution.py:651
  226.3 41.1 %all-to-all-start.1 = ((bf16[32,64,352]{2,1,0:T(8,128)(2,1)}), bf16[32,64,352]{2,1,0:T(8,128)(2,1)}, u32[]{:S(2)}, u32[]{:S(2)}) async-start(bf16[32,64,352]{2,1,0:T(8,128)(2,1)} %reshape.366), calls=%async_computation.1 | async-start | bytes 3145728 | tf_op jit(solution)/shard_map/all_to_all | solution.py:622
  229.7 535.7 %reduce-scatter.3.cloned.1.call-start = ((), (), s32[]{:S(2)}) async-start(), calls=%async_computation.7 | async-start | bytes 1310720 | tf_op jit(solution)/shard_map/reduce_scatter | solution.py:744
  299.9 336.2 %copy-start.4 = (f32[128,2048]{1,0:T(8,128)}, f32[128,2048]{1,0:T(8,128)S(1)}, u32[]{:S(2)}) copy-start(f32[128,2048]{1,0:T(8,128)S(1)} %get-tuple-element.51) | copy-start | bytes 3145732
  299.9 336.2 %copy-start.41 = (f32[128]{0:T(128)}, f32[128]{0:T(128)S(1)}, u32[]{:S(2)}) copy-start(f32[128]{0:T(128)S(1)} %add_rsqrt_fusion) | copy-start | bytes 1540
  460.5 175.6 %copy-start.25 = (bf16[128,2048]{1,0:T(8,128)(2,1)S(1)}, bf16[128,2048]{1,0:T(8,128)(2,1)}, u32[]{:S(2)}) copy-start(bf16[128,2048]{1,0:T(8,128)(2,1)} %param.17) | copy-start | bytes 1572868
  636.1 29.9 %copy-start.45 = (f32[128]{0:T(128)}, f32[128]{0:T(128)S(1)}, u32[]{:S(2)}) copy-start(f32[128]{0:T(128)S(1)} %broadcast_multiply_fusion.6) | copy-start | bytes 1540
  691.3 12.2 %copy-start.13 = (bf16[1024,2,128]{0,2,1:T(8,128)(2,1)S(1)}, bf16[1024,2,128]{0,2,1:T(8,128)(2,1)}, u32[]{:S(2)}) copy-start(bf16[1024,2,128]{0,2,1:T(8,128)(2,1)} %copy-done.12) | copy-start | bytes 1572868
  708.2 54.2 %collective-permute-start.2 = (bf16[2,1024,256]{1,2,0:T(8,128)(2,1)}, bf16[2,1024,256]{1,2,0:T(8,128)(2,1)S(1)}, u32[]{:S(2)}, u32[]{:S(2)}) collective-permute-start(bf16[2,1024,256]{1,2,0:T(8,128)(2,1)} %fusion.13), channel_id=1, source_target_pairs={{8,0},{9,1},{10,2},{11,3},{12,4},{13,5},{14,6},{15,7},{16,8},{17,9... | collective-permute-start | bytes 3145736 | tf_op jit(solution)/shard_map/ppermute | solution.py:763
  709.7 192.8 %reduce-scatter.5.cloned.1.call-start = ((), (), s32[]{:S(2)}) async-start(), calls=%async_computation.8 | async-start | bytes 3932160 | tf_op jit(solution)/shard_map/reduce_scatter | solution.py:786
  709.8 29.9 %copy-start.24 = (f32[1024,128]{0,1:T(8,128)S(1)}, f32[1024,128]{0,1:T(8,128)}, u32[]{:S(2)}) copy-start(f32[1024,128]{0,1:T(8,128)} %get-tuple-element.73) | copy-start | bytes 1572868
  709.8 29.9 %copy-start.30 = (bf16[1,2048,256]{1,2,0:T(8,128)(2,1)S(1)}, bf16[1,2048,256]{1,2,0:T(8,128)(2,1)}, u32[]{:S(2)}) copy-start(bf16[1,2048,256]{1,2,0:T(8,128)(2,1)} %copy-done.29) | copy-start | bytes 3145732
  746.0 16.5 %copy-start.15 = (f32[2,128,2048]{2,1,0:T(8,128)S(1)}, f32[2,128,2048]{2,1,0:T(8,128)}, u32[]{:S(2)}) copy-start(f32[2,128,2048]{2,1,0:T(8,128)} %fusion.43) | copy-start | bytes 6291460
  747.2 17.1 %copy-start.17 = (f32[1024,128]{0,1:T(8,128)S(1)}, f32[1024,128]{0,1:T(8,128)}, u32[]{:S(2)}) copy-start(f32[1024,128]{0,1:T(8,128)} %get-tuple-element.74) | copy-start | bytes 1572868
  765.4 3.6 collective-permute-start.3
  779.5 123.0 %all-to-all-start.3 = ((bf16[32,64,352]{2,1,0:T(8,128)(2,1)}), bf16[32,64,352]{2,1,0:T(8,128)(2,1)}, u32[]{:S(2)}, u32[]{:S(2)}) async-start(bf16[32,64,352]{2,1,0:T(8,128)(2,1)} %pad_maximum_fusion.2), calls=%async_computation.5 | async-start | bytes 3145728 | tf_op jit(solution)/shard_map/all_to_all | solution.py:721
  836.7 30.5 %copy-start.7 = (bf16[128,2048]{1,0:T(8,128)(2,1)S(1)}, bf16[128,2048]{1,0:T(8,128)(2,1)}, u32[]{:S(2)}) copy-start(bf16[128,2048]{1,0:T(8,128)(2,1)} %param.16) | copy-start | bytes 1572868
  836.7 30.5 %copy-start.40 = (f32[2048]{0:T(1024)S(1)}, f32[2048]{0:T(1024)}, u32[]{:S(2)}) copy-start(f32[2048]{0:T(1024)} %copy-done.39) | copy-start | bytes 24580
  836.7 30.5 %copy-start.44 = (f32[128]{0:T(128)S(1)}, f32[128]{0:T(128)}, u32[]{:S(2)}) copy-start(f32[128]{0:T(128)} %copy-done.43) | copy-start | bytes 1540
  865.3 43.0 %copy-start.5 = (f32[128,2048]{1,0:T(8,128)S(1)}, f32[128,2048]{1,0:T(8,128)}, u32[]{:S(2)}) copy-start(f32[128,2048]{1,0:T(8,128)} %copy-done.4) | copy-start | bytes 3145732
  865.3 43.0 %copy-start.38 = (f32[2048]{0:T(1024)S(1)}, f32[2048]{0:T(1024)}, u32[]{:S(2)}) copy-start(f32[2048]{0:T(1024)} %copy-done.37) | copy-start | bytes 24580
  865.3 43.0 %copy-start.42 = (f32[128]{0:T(128)S(1)}, f32[128]{0:T(128)}, u32[]{:S(2)}) copy-start(f32[128]{0:T(128)} %copy-done.41) | copy-start | bytes 1540
  865.3 43.0 %copy-start.46 = (f32[128]{0:T(128)S(1)}, f32[128]{0:T(128)}, u32[]{:S(2)}) copy-start(f32[128]{0:T(128)} %copy-done.45) | copy-start | bytes 1540
  902.5 27.7 %all-to-all-start.2 = ((bf16[8,64,768]{2,1,0:T(8,128)(2,1)}), bf16[8,64,768]{2,1,0:T(8,128)(2,1)}, u32[]{:S(2)}, u32[]{:S(2)}) async-start(bf16[8,64,768]{2,1,0:T(8,128)(2,1)} %bitcast.200), calls=%async_computation.4 | async-start | bytes 1572864 | tf_op jit(solution)/shard_map/all_to_all | solution.py:789
  (32 other events, 124.6 us)
Sparse Core Ops, SparseCore 0:
  10.8 155.4 all-gather.1
  709.8 52.4 reduce-scatter.2
  775.4 102.9 reduce-scatter.4

commit v3 on v2

--- a/solution.py
+++ b/solution.py
@@ -257,15 +257,98 @@
     ]
 
 
-def scatter_body(length, many, *refs):
-    in_refs, o_refs = refs[:many], refs[many : 2 * many]
+def sum_order(p):
+    return [
+        jnp.where(p < 2, 3, 0),
+        jnp.where(p == 0, 2, jnp.where(p == 1, 0, jnp.where(p == 2, 3, 1))),
+        jnp.where((p == 0) | (p == 2), 1, 2),
+        p,
+    ]
+
+
+def add_rows(target, sources):
+    rows_in_all = target.shape[0]
+    row_step = min(16, rows_in_all)
+
+    def body(i, _):
+        rows = pl.ds(pl.multiple_of(i * row_step, row_step), row_step)
+        value = sources[0][rows, :].astype(FL)
+        for source in sources[1:]:
+            value = value + source[rows, :].astype(FL)
+        target[rows, :] = value.astype(target.dtype)
+        return 0
+
+    lax.fori_loop(0, rows_in_all // row_step, body, 0)
+
+
+def line_sums(p, device, c, ins, outs, nears, arrivals, load_sem, send_sem, z_sem):
+    many = len(ins)
+    started = []
+
+    def load(k, t):
+        return pltpu.make_async_copy(ins[k].at[t], nears[k].at[t], load_sem.at[k * 4 + t])
+
+    def begin():
+        for t in range(4):
+            for k in range(many):
+                load(k, t).start()
+
+    def step(t):
+        for k in range(many):
+            near = nears[k].at[t]
+            load(k, t).wait()
+            for side, there in ((0, (p > 0) & (p <= t)), (1, (p < 3) & (p >= t))):
+                kept = jnp.where(p == t, 4, t) if side else t
+
+                @pl.when(there)
+                def _():
+                    pltpu.make_async_remote_copy(
+                        src_ref=near, dst_ref=arrivals[k].at[kept], send_sem=send_sem.at[0],
+                        recv_sem=z_sem.at[(k * 4 + t) * 2 + side],
+                        device_id=(device(c=1 - c),), device_id_type=MESH,
+                    ).wait_recv()
+                    add_rows(near, [near, arrivals[k].at[kept]])
+            @pl.when(p == t)
+            def _():
+                add_rows(outs[k], [near])
+            for side, there in ((0, p < t), (1, p > t)):
+                kept = jnp.where(p - 1 == t, 4, t) if side else t
+                slot = (k * 4 + t) * 2 + side
+                made = pltpu.make_async_remote_copy(
+                    src_ref=near, dst_ref=arrivals[k].at[kept], send_sem=send_sem.at[slot],
+                    recv_sem=z_sem.at[slot],
+                    device_id=(device(1 - 2 * side),), device_id_type=MESH,
+                )
+                pl.when(there)(made.start)
+                started.append((made, there))
+
+    def finish():
+        for made, there in started:
+            pl.when(there)(made.wait_send)
+
+    return [begin] + [functools.partial(step, t) for t in sum_order(p)] + [finish]
+
+
+def scatter_body(length, many, extra, *refs):
+    in_refs, extra_in, refs = refs[:many], refs[many : many + extra], refs[many + extra :]
+    o_refs, extra_out, refs = refs[:many], refs[many : many + extra], refs[many + extra :]
     (pair_in, near, first_in, second_in, z_in, total,
-     send_sem, pair_sem, load_sem, first_sem, second_sem, z_sem) = refs[2 * many :]
-    p, y, x, c, device = place(length)
-    greet(length, p, device, y, x, c)
+     send_sem, pair_sem, load_sem, first_sem, second_sem, z_sem) = refs[:12]
+    if extra:
+        p, y, x, c, device = place(4)
+        greet(4, p, device, y, x, c)
+        work = line_sums(
+            p, device, c, extra_in, extra_out, refs[12 : 12 + extra],
+            refs[12 + extra : 12 + 2 * extra], *refs[12 + 2 * extra :]
+        )
+        p = p * 0
+    else:
+        p, y, x, c, device = place(length)
+        greet(length, p, device, y, x, c)
+        work = []
     half, width = total.shape
-    order = [3, 0, 2, 1] if length == 4 else [0]
-    row_step = min(16, half)
+    order = sum_order(p) if length == 4 else [0]
+    places = range(length)
     started = []
 
     def part(g, z, far, cc):
@@ -290,66 +373,62 @@
     place_s = (y, x)
     slot = lambda g, z, k: (g * length + z) * 6 + k
     pairs, loads, firsts, seconds = {}, {}, {}, {}
-    steps = [(q, z) for q in range(many) for z in order]
+    for begin in work[:2]:
+        begin()
+    steps = [(q, n) for q in range(many) for n in places]
     for q in range(many):
         for far in (1, 0):
-            for z in order:
+            for n in places:
+                z = order[n]
                 for g in (2 * q, 2 * q + 1):
                     k = (g * length + z) * 2 + far
-                    pairs[g, z, far] = send(
+                    pairs[g, n, far] = send(
                         part(g, z, far, 1 - c), pair_in.at[g, z, far], slot(g, z, far),
                         pair_sem.at[k], device(c=1 - c),
                     )
-                    loads[g, z, far] = pltpu.make_async_copy(
+                    loads[g, n, far] = pltpu.make_async_copy(
                         part(g, z, far, c), near.at[g, z, far], load_sem.at[k]
                     )
-                    loads[g, z, far].start()
-
-    def add(target, sources):
-        def body(i, _):
-            rows = pl.ds(pl.multiple_of(i * row_step, row_step), row_step)
-            value = sources[0][rows, :].astype(FL)
-            for source in sources[1:]:
-                value = value + source[rows, :].astype(FL)
-            target[rows, :] = value.astype(target.dtype)
-            return 0
-        lax.fori_loop(0, half // row_step, body, 0)
-
-    def stage_first(q, z):
+                    loads[g, n, far].start()
+
+    def stage_first(q, n):
+        z = order[n]
         for g in (2 * q, 2 * q + 1):
-            pairs[g, z, 1].wait_recv()
-            loads[g, z, 1].wait()
+            pairs[g, n, 1].wait_recv()
+            loads[g, n, 1].wait()
             for s in range(2):
-                add(near.at[g, z, 1, s], [near.at[g, z, 1, s], pair_in.at[g, z, 1, s]])
-            firsts[g, z] = send(
+                add_rows(near.at[g, z, 1, s], [near.at[g, z, 1, s], pair_in.at[g, z, 1, s]])
+            firsts[g, n] = send(
                 near.at[g, z, 1], first_in.at[g, z], slot(g, z, 2),
                 first_sem.at[g * length + z], first_to[g % 2],
             )
 
-    def stage_second(q, z):
+    def stage_second(q, n):
+        z = order[n]
         for g in (2 * q, 2 * q + 1):
             s = 1 - place_s[g % 2]
-            pairs[g, z, 0].wait_recv()
-            loads[g, z, 0].wait()
-            firsts[g, z].wait_recv()
-            add(near.at[g, z, 0, s],
+            pairs[g, n, 0].wait_recv()
+            loads[g, n, 0].wait()
+            firsts[g, n].wait_recv()
+            add_rows(near.at[g, z, 0, s],
                 [near.at[g, z, 0, s], pair_in.at[g, z, 0, s], first_in.at[g, z, s]])
-            seconds[g, z] = send(
+            seconds[g, n] = send(
                 near.at[g, z, 0, s], second_in.at[g, z], slot(g, z, 3),
                 second_sem.at[g * length + z], second_to[g % 2],
             )
 
-    def stage_z(q, z):
+    def stage_z(q, n):
+        z = order[n]
         for g in (2 * q, 2 * q + 1):
             s = place_s[g % 2]
             o_half = o_refs[q].at[g % 2]
-            seconds[g, z].wait_recv()
+            seconds[g, n].wait_recv()
             sources = [near.at[g, z, 0, s], pair_in.at[g, z, 0, s], first_in.at[g, z, s],
                        second_in.at[g, z]]
             if length == 1:
-                add(o_half, sources)
+                add_rows(o_half, sources)
                 continue
-            add(total, sources)
+            add_rows(total, sources)
             for side, sender in ((0, (p > 0) & (p <= z)), (1, (p < length - 1) & (p >= z))):
                 @pl.when(sender)
                 def _():
@@ -359,13 +438,13 @@
                         send_sem=send_sem.at[0], recv_sem=z_sem.at[k],
                         device_id=(device(c=1 - c),), device_id_type=MESH,
                     ).wait_recv()
-                    add(total, [total, z_in.at[g, z, side]])
+                    add_rows(total, [total, z_in.at[g, z, side]])
             @pl.when(p == z)
             def _():
-                add(o_half, [total])
+                add_rows(o_half, [total])
             @pl.when(p != z)
             def _():
-                add(near.at[g, z, 0, s], [total])
+                add_rows(near.at[g, z, 0, s], [total])
             send(near.at[g, z, 0, s], z_in.at[g, z, 0], slot(g, z, 4),
                  z_sem.at[(g * length + z) * 2], device(1), p < z)
             send(near.at[g, z, 0, s], z_in.at[g, z, 1], slot(g, z, 5),
@@ -376,6 +455,10 @@
         for stage, j in ((stage_first, i), (stage_z, i - 3), (stage_second, i - 1)):
             if 0 <= j < count:
                 stage(*steps[j])
+                if stage is stage_first and work:
+                    work[2]()
+    for step in work[3:]:
+        step()
     for made, there in started:
         if there is None:
             made.wait_send()
@@ -383,17 +466,26 @@
             pl.when(there)(made.wait_send)
 
 
-def scatter(values, length, collective_id):
-    many = len(values)
+def scatter(values, length, collective_id, others=()):
+    many, extra = len(values), len(others)
     rows, width = values[0].shape[0] // (8 * length), values[0].shape[1]
     half = rows // 2
     kind = values[0].dtype
     lanes = 2 * many
+    others = [other.reshape((4, other.shape[0] // 4) + other.shape[1:]) for other in others]
+    extra_scratch = []
+    if extra:
+        extra_scratch = (
+            [pltpu.VMEM(other.shape, other.dtype) for other in others]
+            + [pltpu.VMEM((5,) + other.shape[1:], other.dtype) for other in others]
+            + [pltpu.SemaphoreType.DMA((n * extra,)) for n in (4, 8, 8)]
+        )
     outs = pl.pallas_call(
-        functools.partial(scatter_body, length, many),
-        out_shape=[jax.ShapeDtypeStruct((2, half, width), FL)] * many,
-        in_specs=[pl.BlockSpec(memory_space=pl.ANY)] * many,
-        out_specs=[pl.BlockSpec(memory_space=pltpu.VMEM)] * many,
+        functools.partial(scatter_body, length, many, extra),
+        out_shape=[jax.ShapeDtypeStruct((2, half, width), FL)] * many
+        + [jax.ShapeDtypeStruct(other.shape[1:], other.dtype) for other in others],
+        in_specs=[pl.BlockSpec(memory_space=pl.ANY)] * (many + extra),
+        out_specs=[pl.BlockSpec(memory_space=pltpu.VMEM)] * (many + extra),
         scratch_shapes=[
             pltpu.VMEM((lanes, length, 2, 2, half, width), kind),
             pltpu.VMEM((lanes, length, 2, 2, half, width), kind),
@@ -407,12 +499,30 @@
             pltpu.SemaphoreType.DMA((lanes * length,)),
             pltpu.SemaphoreType.DMA((lanes * length,)),
             pltpu.SemaphoreType.DMA((2 * lanes * length,)),
-        ],
+        ] + extra_scratch,
         compiler_params=pltpu.CompilerParams(
             collective_id=collective_id, has_side_effects=True, vmem_limit_bytes=62 << 20
         ),
-    )(*[value.reshape(length, 2, 2, 2, 2, half, width) for value in values])
-    return [out.reshape(rows, width) for out in outs]
+    )(*[value.reshape(length, 2, 2, 2, 2, half, width) for value in values], *others)
+    return [out.reshape(rows, width) for out in outs[:many]] + list(outs[many:])
+
+
+def side_by_side(value, parts):
+    blocks, rows, columns = value.shape
+    columns = columns // parts
+
+    def body(in_ref, out_ref):
+        for part in range(parts):
+            pieces = [
+                in_ref[block].astype(FL)[:, part * columns : (part + 1) * columns]
+                for block in range(blocks)
+            ]
+            lanes = pl.ds(part * blocks * columns, blocks * columns)
+            out_ref[:, lanes] = jnp.concatenate(pieces, axis=1)
+
+    return pl.pallas_call(
+        body, out_shape=jax.ShapeDtypeStruct((rows, parts * blocks * columns), FL)
+    )(value)
 
 
 def dot(a, b, dims=((1,), (0,))):
@@ -711,8 +821,6 @@
         summed_out = lax.psum_scatter(out_part, AXIS, scatter_dimension=0, tiled=True)
     d_w1 = dot(mid_all, d_pre, ((0,), (0,)))
     d_w2 = dot(act_low, grad_all, ((0,), (0,)))
-    shared_out_grad = d_w2[:hid_s]
-    expert_out_grad = d_w2[wide_s : wide_s + hid_e]
     expert_in_grad = jnp.concatenate(
         [d_w1[:, wide_s : wide_s + hid_e], d_w1[:, full + wide_s : full + wide_s + hid_e]], axis=1
     )
@@ -741,12 +849,6 @@
     d_attn = team_gather(d_hidden.astype(BF), 4)
     d_attended = dot(d_attn, w_out, ((1,), (1,))).astype(BF)
     out_grad = dot(attended, d_attn, ((0,), (0,))).astype(BF)
-    out_part_grad = lax.psum_scatter(
-        out_grad, AXIS, scatter_dimension=0, tiled=True, axis_index_groups=across
-    )
-    out_weight_grad = lax.ppermute(
-        out_part_grad, AXIS, [(target, source) for source, target in deal]
-    ).astype(FL)
     d_attended = d_attended.reshape(SEQ, own, HEAD_DIM)
     attention = jnp.exp(masked_scores() - log_total)
     d_attention = jnp.einsum("qhd,khd->hqk", d_attended, window[1], preferred_element_type=FL)
@@ -770,22 +872,38 @@
         ],
         axis=1,
     ).astype(BF)
-    d_projected, out_weight_grad = lax.optimization_barrier((d_projected, out_weight_grad))
-    d_normed = team_scatter(dot(d_projected, w_qkv, ((1,), (1,))).astype(BF), 5).astype(FL)
-    shared_in_grad = (
-        shared_back.reshape(count, share, 2, hid_s)
-        .transpose(1, 2, 0, 3)
-        .reshape(share, -1)
-        .astype(FL)
-    )
+    d_projected, shared_back, d_w2 = lax.optimization_barrier((d_projected, shared_back, d_w2))
+    d_normed = dot(d_projected, w_qkv, ((1,), (1,))).astype(BF)
+    qkv_grad = dot(normed, d_projected, ((0,), (0,))).astype(BF)
+    if layered:
+        d_normed, qkv_part, out_part_grad = scatter([d_normed], 1, 5, [qkv_grad, out_grad])
+    else:
+        d_normed = team_scatter(d_normed, 5).astype(FL)
+        qkv_part, out_part_grad = [
+            lax.psum_scatter(
+                value, AXIS, scatter_dimension=0, tiled=True, axis_index_groups=across
+            )
+            for value in (qkv_grad, out_grad)
+        ]
+    out_weight_grad = lax.ppermute(
+        out_part_grad, AXIS, [(target, source) for source, target in deal]
+    ).astype(FL)
     d_inputs, gain_in_grad = norm_back(inputs, scale_in, gain_in, d_normed)
     input_grad = d_hidden + d_inputs
-    qkv_grad = dot(normed, d_projected, ((0,), (0,)))
     bias_grad = jnp.sum(d_projected.astype(FL), axis=0).reshape(3, own, HEAD_DIM)
 
-    qkv_part = lax.psum_scatter(
-        qkv_grad.astype(BF), AXIS, scatter_dimension=0, tiled=True, axis_index_groups=across
-    )
+    if layered:
+        shared_in_grad = side_by_side(shared_back, 2)
+    else:
+        shared_in_grad = (
+            shared_back.reshape(count, share, 2, hid_s)
+            .transpose(1, 2, 0, 3)
+            .reshape(share, -1)
+            .astype(FL)
+        )
+
+    shared_out_grad = d_w2[:hid_s]
+    expert_out_grad = d_w2[wide_s : wide_s + hid_e]
     qkv_part = lax.all_to_all(
         qkv_part.reshape(team, share, 3 * span),
         AXIS,

time: 952 us -> 928 us (0.975)
  Pallas kernels: 583 us -> 600 us
  local copies, waits for them, and re-layouts: 90.4 us -> 74.8 us
  waiting for transfers between devices: 29.9 us -> 15.1 us
  starting transfers between devices: 38 us -> 27.1 us
    convert_element_type x3 -> x0, local copies, waits for them, and re-layouts: 18.3 us -> none  [per_device(): shared_in_grad = shared_back.reshape(count, share, 2, hid_s).transpose(1,...]
    pallas_call x4 -> x5, Pallas kernels: 260 us -> 277 us  [the longest x4 274 us: scatter(): pl.pallas_call(functools.partial(scatter_body, length, many, extra), out_...]
    ppermute x1, waiting for transfers between devices: 15.3 us -> 0.01 us  [per_device(): returned = lax.ppermute(d_kv[:, :SEQ].astype(BF), AXIS, backward).astype(FL)]
    all_to_all x1, starting transfers between devices: 19.3 us -> 8.26 us  [per_device(): lax.all_to_all(d_shared.astype(BF).reshape(count, share, 2 * hid_s), AXIS...]
  transfers between devices with their start and end apart: 11 -> 9, of which waited for: 2 -> 1; matrix products, arithmetic and copies ran while one was open for 22% -> 21% of each run, Pallas kernels for 32% -> 30%
where the time goes in v3:
time: 928 us; the launch traced here: 919 us
  Pallas kernels  600 us (65%)
  matrix products  115 us (12%)
  local copies, waits for them, and re-layouts  74.8 us (8%)
  other arithmetic  72.4 us (8%)
  starting transfers between devices  27.1 us (3%)
  between operations  15.3 us (2%)
  waiting for transfers between devices  15.1 us (2%)
    pallas_call x4, Pallas kernels, scatter(): pl.pallas_call(functools.partial(scatter_body, length, many, extra), out_...  274 us
    pallas_call x1, Pallas kernels, layer_and_line(): pl.pallas_call(functools.partial(layer_and_line_body, many), out_shape=[j...  122 us
    pallas_call x3, Pallas kernels, gather(): pl.pallas_call(functools.partial(gather_body, length), out_shape=jax.Shap...  120 us
    pallas_call x1, Pallas kernels, feed(): pl.pallas_call(functools.partial(feed_body, gate_column=gate_column, shar...  80.4 us
    dot_general x8, matrix products, dot(): return lax.dot_general(a, b, (dims, ((), ())), preferred_element_type=FL)  76.1 us
  transfers between devices with their start and end apart: 9, of which 1 were waited for; matrix products, arithmetic and copies ran while one was open for 21% of the time, Pallas kernels for 30%

profile of v3, /device:TPU:0, one launch (start us, length us, event | category | flops | bytes accessed | tf_op | source)
XLA Modules:
  0.0 919.4 jit_solution(1705395253445509618)
XLA Ops:
  15.8 22.3 %shard_map.247 = f32[4,2,2,2,2,8,128]{6,5,4,3,2,1,0:T(8,128)} custom-call(f32[2,8,128]{2,1,0:T(8,128)} %pad_bitcast_fusion.x_ref), custom_call_target="tpu_custom_call" | custom-call | tf_op jit(solution)/shard_map/pallas_call | solution.py:174
  42.6 4.2 all-to-all-start
  50.0 4.6 copy.78
  72.8 122.4 %shard_map.248 = (bf16[1,2,2,2,2,64,2048]{6,5,4,3,2,1,0:T(8,128)(2,1)}, bf16[4,512,768]{2,1,0:T(8,128)(2,1)}, bf16[4,64,2048]{2,1,0:T(8,128)(2,1)}) custom-call(bf16[2,64,2048]{2,1,0:T(8,128)(2,1)} %bitcast.186, bf16[512,768]{1,0:T(8,128)(2,1)} %bitcast.6.refs_1_, bf16[64,2048]{1,0:T(8,128)(2,1)} %copy-done.32), custom_call_target="tpu_custom_call" | custom-call | tf_op jit(solution)/shard_map/pallas_call | solution.py:239
  195.2 6.2 convolution_add_fusion
  209.7 5.8 reshape.365
  215.5 5.1 copy.74
  220.6 5.7 reshape.366
  236.2 4.2 fusion
  240.4 5.2 exponential_reduce_fusion
  246.1 7.4 convolution_convert_fusion.4
  253.5 14.4 %all-to-all-done.1 = bf16[32,64,352]{2,1,0:T(8,128)(2,1)} async-done(((bf16[32,64,352]{2,1,0:T(8,128)(2,1)}), bf16[32,64,352]{2,1,0:T(8,128)(2,1)}, u32[]{:S(2)}, u32[]{:S(2)}) %all-to-all-start.1) | async-done | bytes 1441824 | tf_op jit(solution)/shard_map/all_to_all | solution.py:732
  268.0 4.7 convolution_convert_fusion
  272.7 26.3 %shard_map.249 = f32[2,64,2048]{2,1,0:T(8,128)} custom-call(bf16[1,2,2,2,2,64,2048]{6,5,4,3,2,1,0:T(8,128)(2,1)} %bitcast.155), custom_call_target="tpu_custom_call" | custom-call | tf_op jit(solution)/shard_map/pallas_call | solution.py:483
  301.5 73.6 %shard_map.250 = bf16[4,2,2,2,2,64,2048]{6,5,4,3,2,1,0:T(8,128)(2,1)} custom-call(bf16[2,64,2048]{2,1,0:T(8,128)(2,1)} %bitcast.185), custom_call_target="tpu_custom_call" | custom-call | tf_op jit(solution)/shard_map/pallas_call | solution.py:174
  380.6 80.4 %shard_map.251 = (bf16[4096,2048]{1,0:T(8,128)(2,1)}, bf16[4096,2048]{1,0:T(8,128)(2,1)}, bf16[4096,640]{1,0:T(8,128)(2,1)}, bf16[4096,1280]{1,0:T(8,128)(2,1)}) custom-call(bf16[4096,2048]{1,0:T(8,128)(2,1)} %bitcast.156, bf16[4096,2048]{1,0:T(8,128)(2,1)} %all-gather.2.cloned.1.call-done.grad_ref, f32[4096,1]{1,0:T(8,128)} %copy.79.weight_ref, ...), custom_call_target="tpu_custom_call" | custom-call | flops 64424509440 | bytes 100663296 | tf_op jit(solution)/shard_map/pallas_call | solution.py:568
  461.0 150.1 %shard_map.252 = (f32[2,64,2048]{2,1,0:T(8,128)}, f32[2,64,2048]{2,1,0:T(8,128)}) custom-call(bf16[4,2,2,2,2,64,2048]{6,5,4,3,2,1,0:T(8,128)(2,1)} %bitcast.158, bf16[4,2,2,2,2,64,2048]{6,5,4,3,2,1,0:T(8,128)(2,1)} %bitcast.159), custom_call_target="tpu_custom_call" | custom-call | tf_op jit(solution)/shard_map/pallas_call | solution.py:483
  615.2 23.9 %shard_map.253 = bf16[1,2,2,2,2,64,2048]{6,5,4,3,2,1,0:T(8,128)(2,1)} custom-call(bf16[2,64,2048]{2,1,0:T(8,128)(2,1)} %bitcast.187), custom_call_target="tpu_custom_call" | custom-call | tf_op jit(solution)/shard_map/pallas_call | solution.py:174
  642.8 12.9 %multiply_reduce_fusion = (f32[2,1024]{1,0:T(2,128)S(1)}, f32[2,1024,2048]{2,1,0:T(8,128)}) fusion(f32[2,1024,2048]{2,1,0:T(8,128)} %copy-done, f32[2,1024]{1,0:T(2,128)S(1)} %log_add_fusion, pred[1024,2048]{1,0:T(8,128)(4,1)S(1)} %copy-done.2, bf16[1024,2,128]{0,2,1:T(8,128)(2,1)S(1)} %bitcast.199, bf16[2048,2,128]{0,2,1:T(8,128)(2,1)S(1)} %bitcast.180), kind=kOutput, calls=%fused_computation.1 | convolution fusion | flops 1094711296 | bytes 37240832 | tf_op jit(solution)/shard_map/qhd,khd->hqk/dot_general | solution.py:854
  655.7 8.7 fusion.43
  664.5 12.9 %multiply_convert_fusion = bf16[2,1024,2048]{2,1,0:T(8,128)(2,1)S(1)} fusion(f32[2,1024,2048]{2,1,0:T(8,128)} %get-tuple-element.94, f32[2,1024,2048]{2,1,0:T(8,128)} %copy-done, f32[2,1024]{1,0:T(2,128)S(1)} %get-tuple-element.93, f32[2,1024]{1,0:T(2,128)S(1)} %log_add_fusion, pred[1024,2048]{1,0:T(8,128)(4,1)S(1)} %copy-done.2), kind=kLoop, calls=%fused_computation | loop fusion | flops 25165824 | bytes 44056576 | tf_op jit(solution)/shard_map/convert_element_type | solution.py:856
  681.6 4.0 broadcast_multiply_fusion
  685.6 29.7 %fusion.55 = (bf16[2048,1280]{0,1:T(8,128)(2,1)}, f32[2048,1280]{0,1:T(8,128)}) fusion(bf16[4096,2048]{1,0:T(8,128)(2,1)} %bitcast.157, bf16[4096,1280]{1,0:T(8,128)(2,1)} %get-tuple-element.46), kind=kOutput, calls=%fused_computation.145 | convolution fusion | flops 21477457920 | bytes 42991616 | tf_op jit(solution)/shard_map/dot_general | solution.py:529
  725.6 8.3 all-to-all-start.2
  733.9 5.9 fusion.46
  739.8 17.6 %fusion.56 = f32[640,2048]{1,0:T(8,128)} fusion(bf16[4096,640]{1,0:T(8,128)(2,1)} %get-tuple-element.47, bf16[4096,2048]{1,0:T(8,128)(2,1)} %all-gather.2.cloned.1.call-done.grad_ref), kind=kOutput, calls=%fused_computation.146 | convolution fusion | flops 10737418240 | bytes 27262976 | tf_op jit(solution)/shard_map/dot_general | solution.py:529
  761.2 5.2 maximum_bitcast_fusion
  771.8 7.1 convolution_convert_fusion.1
  779.0 4.9 convolution_convert_fusion.2
  784.2 73.7 %shard_map.254 = (f32[2,64,2048]{2,1,0:T(8,128)}, bf16[512,768]{1,0:T(8,128)(2,1)}, bf16[64,2048]{1,0:T(8,128)(2,1)}) custom-call(bf16[1,2,2,2,2,64,2048]{6,5,4,3,2,1,0:T(8,128)(2,1)} %bitcast.176, bf16[4,512,768]{2,1,0:T(8,128)(2,1)} %bitcast.184, bf16[4,64,2048]{2,1,0:T(8,128)(2,1)} %bitcast.196), custom_call_target="tpu_custom_call" | custom-call | tf_op jit(solution)/shard_map/pallas_call | solution.py:483
  859.8 4.2 all-to-all-start.3
  876.4 23.8 %shard_map.255 = f32[2,8,128]{2,1,0:T(8,128)} custom-call(f32[4,2,2,2,2,8,128]{6,5,4,3,2,1,0:T(8,128)} %bitcast.193), custom_call_target="tpu_custom_call" | custom-call | tf_op jit(solution)/shard_map/pallas_call | solution.py:483
  (215 shorter events, 118.6 us)
Async XLA Ops:
  7.2 373.5 %all-gather.2.cloned.1.call-start = ((), (), s32[]{:S(2)}) async-start(), calls=%async_computation.4 | async-start | bytes 17301504 | tf_op jit(solution)/shard_map/all_gather | solution.py:739
  9.5 37.3 %copy-start.45 = (bf16[64,2048]{1,0:T(8,128)(2,1)S(1)}, bf16[64,2048]{1,0:T(8,128)(2,1)}, u32[]{:S(2)}) copy-start(bf16[64,2048]{1,0:T(8,128)(2,1)} %param.25) | copy-start | bytes 786436
  42.6 29.5 %all-to-all-start = ((bf16[8,64,768]{2,1,0:T(8,128)(2,1)}), bf16[8,64,768]{2,1,0:T(8,128)(2,1)}, u32[]{:S(2)}, u32[]{:S(2)}) async-start(bf16[8,64,768]{2,1,0:T(8,128)(2,1)} %reshape.362), calls=%async_computation | async-start | bytes 1572864 | tf_op jit(solution)/shard_map/all_to_all | solution.py:705
  46.8 25.3 %collective-permute-start = (bf16[64,2048]{1,0:T(8,128)(2,1)S(1)}, bf16[64,2048]{1,0:T(8,128)(2,1)S(1)}, u32[]{:S(2)}, u32[]{:S(2)}) collective-permute-start(bf16[64,2048]{1,0:T(8,128)(2,1)S(1)} %copy-done.45), channel_id=1, source_target_pairs={{0,0},{4,1},{8,2},{12,3},{16,4},{20,5},{24,6},{28,7},{1,8},{5,9},{... | collective-permute-start | bytes 786440 | tf_op jit(solution)/shard_map/ppermute | solution.py:715
  47.7 19.7 %copy-start.35 = (f32[2048]{0:T(1024)}, f32[2048]{0:T(1024)S(1)}, u32[]{:S(2)}) copy-start(f32[2048]{0:T(1024)S(1)} %mul.240) | copy-start | bytes 24580
  47.9 564.8 %copy-start.33 = (f32[2048]{0:T(1024)}, f32[2048]{0:T(1024)S(1)}, u32[]{:S(2)}) copy-start(f32[2048]{0:T(1024)S(1)} %mul.263) | copy-start | bytes 24580
  50.0 10.1 %copy-start.5 = (bf16[128,2048]{1,0:T(8,128)(2,1)S(1)}, bf16[128,2048]{1,0:T(8,128)(2,1)}, u32[]{:S(2)}) copy-start(bf16[128,2048]{1,0:T(8,128)(2,1)} %param.16) | copy-start | bytes 1572868
  64.3 131.0 %copy-start.39 = (f32[128]{0:T(128)}, f32[128]{0:T(128)S(1)}, u32[]{:S(2)}) copy-start(f32[128]{0:T(128)S(1)} %add_rsqrt_fusion.1) | copy-start | bytes 1540
  67.4 178.2 %copy-start.1 = (pred[1024,2048]{1,0:T(8,128)(4,1)}, pred[1024,2048]{1,0:T(8,128)(4,1)S(1)}, u32[]{:S(2)}) copy-start(pred[1024,2048]{1,0:T(8,128)(4,1)S(1)} %fusion.5) | copy-start | bytes 6291460
  202.7 5.7 copy-start.7
  205.9 27.6 %collective-permute-start.1 = (bf16[2,1024,256]{1,2,0:T(8,128)(2,1)}, bf16[2,1024,256]{1,2,0:T(8,128)(2,1)}, u32[]{:S(2)}, u32[]{:S(2)}) collective-permute-start(bf16[2,1024,256]{1,2,0:T(8,128)(2,1)} %pad_maximum_fusion.3), channel_id=1, source_target_pairs={{0,8},{1,9},{2,10},{3,11},{4,12},{5,13},{6,14},{7,15},{8,16},{9,17... | collective-permute-start | bytes 3145736 | tf_op jit(solution)/shard_map/ppermute | solution.py:761
  226.3 41.7 %all-to-all-start.1 = ((bf16[32,64,352]{2,1,0:T(8,128)(2,1)}), bf16[32,64,352]{2,1,0:T(8,128)(2,1)}, u32[]{:S(2)}, u32[]{:S(2)}) async-start(bf16[32,64,352]{2,1,0:T(8,128)(2,1)} %reshape.366), calls=%async_computation.1 | async-start | bytes 3145728 | tf_op jit(solution)/shard_map/all_to_all | solution.py:732
  240.4 5.7 copy-start
  300.4 312.4 %copy-start.3 = (f32[128,2048]{1,0:T(8,128)}, f32[128,2048]{1,0:T(8,128)S(1)}, u32[]{:S(2)}) copy-start(f32[128,2048]{1,0:T(8,128)S(1)} %get-tuple-element.59) | copy-start | bytes 3145732
  300.4 312.4 %copy-start.37 = (f32[128]{0:T(128)}, f32[128]{0:T(128)S(1)}, u32[]{:S(2)}) copy-start(f32[128]{0:T(128)S(1)} %add_rsqrt_fusion) | copy-start | bytes 1540
  461.0 151.7 %copy-start.20 = (bf16[128,2048]{1,0:T(8,128)(2,1)S(1)}, bf16[128,2048]{1,0:T(8,128)(2,1)}, u32[]{:S(2)}) copy-start(bf16[128,2048]{1,0:T(8,128)(2,1)} %param.17) | copy-start | bytes 1572868
  612.7 26.4 %copy-start.31 = (bf16[4,64,2048]{2,1,0:T(8,128)(2,1)S(1)}, bf16[4,64,2048]{2,1,0:T(8,128)(2,1)}, u32[]{:S(2)}) copy-start(bf16[4,64,2048]{2,1,0:T(8,128)(2,1)} %get-tuple-element.40) | copy-start | bytes 3145732
  612.8 30.0 %copy-start.41 = (f32[128]{0:T(128)}, f32[128]{0:T(128)S(1)}, u32[]{:S(2)}) copy-start(f32[128]{0:T(128)S(1)} %broadcast_multiply_fusion.6) | copy-start | bytes 1540
  664.4 14.3 %copy-start.11 = (f32[2,128,2048]{2,1,0:T(8,128)}, f32[2,128,2048]{2,1,0:T(8,128)S(1)}, u32[]{:S(2)}) copy-start(f32[2,128,2048]{2,1,0:T(8,128)S(1)} %fusion.43) | copy-start | bytes 6291460
  664.5 13.0 %copy-start.10 = (bf16[1024,2,128]{0,2,1:T(8,128)(2,1)S(1)}, bf16[1024,2,128]{0,2,1:T(8,128)(2,1)}, u32[]{:S(2)}) copy-start(bf16[1024,2,128]{0,2,1:T(8,128)(2,1)} %copy-done.9) | copy-start | bytes 1572868
  679.9 88.7 %collective-permute-start.2 = (bf16[2,1024,256]{1,2,0:T(8,128)(2,1)}, bf16[2,1024,256]{1,2,0:T(8,128)(2,1)}, u32[]{:S(2)}, u32[]{:S(2)}) collective-permute-start(bf16[2,1024,256]{1,2,0:T(8,128)(2,1)} %fusion.13), channel_id=1, source_target_pairs={{8,0},{9,1},{10,2},{11,3},{12,4},{13,5},{14,6},{15,7},{16,8},{17,9... | collective-permute-start | bytes 3145736 | tf_op jit(solution)/shard_map/ppermute | solution.py:865
  725.6 46.2 %all-to-all-start.2 = ((bf16[32,64,352]{2,1,0:T(8,128)(2,1)}), bf16[32,64,352]{2,1,0:T(8,128)(2,1)}, u32[]{:S(2)}, u32[]{:S(2)}) async-start(bf16[32,64,352]{2,1,0:T(8,128)(2,1)} %pad_maximum_fusion.2), calls=%async_computation.2 | async-start | bytes 3145728 | tf_op jit(solution)/shard_map/all_to_all | solution.py:829
  771.8 7.1 copy-start.44
  784.2 73.8 %copy-start.6 = (bf16[128,2048]{1,0:T(8,128)(2,1)S(1)}, bf16[128,2048]{1,0:T(8,128)(2,1)}, u32[]{:S(2)}) copy-start(bf16[128,2048]{1,0:T(8,128)(2,1)} %param.16) | copy-start | bytes 1572868
  784.2 73.8 %copy-start.36 = (f32[2048]{0:T(1024)S(1)}, f32[2048]{0:T(1024)}, u32[]{:S(2)}) copy-start(f32[2048]{0:T(1024)} %copy-done.35) | copy-start | bytes 24580
  784.2 73.8 %copy-start.40 = (f32[128]{0:T(128)S(1)}, f32[128]{0:T(128)}, u32[]{:S(2)}) copy-start(f32[128]{0:T(128)} %copy-done.39) | copy-start | bytes 1540
  784.2 81.4 %copy-start.4 = (f32[128,2048]{1,0:T(8,128)S(1)}, f32[128,2048]{1,0:T(8,128)}, u32[]{:S(2)}) copy-start(f32[128,2048]{1,0:T(8,128)} %copy-done.3) | copy-start | bytes 3145732
  784.2 81.4 %copy-start.34 = (f32[2048]{0:T(1024)S(1)}, f32[2048]{0:T(1024)}, u32[]{:S(2)}) copy-start(f32[2048]{0:T(1024)} %copy-done.33) | copy-start | bytes 24580
  784.2 81.4 %copy-start.38 = (f32[128]{0:T(128)S(1)}, f32[128]{0:T(128)}, u32[]{:S(2)}) copy-start(f32[128]{0:T(128)} %copy-done.37) | copy-start | bytes 1540
  784.2 81.4 %copy-start.42 = (f32[128]{0:T(128)S(1)}, f32[128]{0:T(128)}, u32[]{:S(2)}) copy-start(f32[128]{0:T(128)} %copy-done.41) | copy-start | bytes 1540
  859.8 47.5 %all-to-all-start.3 = ((bf16[8,64,768]{2,1,0:T(8,128)(2,1)}), bf16[8,64,768]{2,1,0:T(8,128)(2,1)}, u32[]{:S(2)}, u32[]{:S(2)}) async-start(bf16[8,64,768]{2,1,0:T(8,128)(2,1)} %bitcast.198), calls=%async_computation.3 | async-start | bytes 1572864 | tf_op jit(solution)/shard_map/all_to_all | solution.py:907
  864.0 42.4 %collective-permute-start.3 = (bf16[64,2048]{1,0:T(8,128)(2,1)}, bf16[64,2048]{1,0:T(8,128)(2,1)S(1)}, u32[]{:S(2)}, u32[]{:S(2)}) collective-permute-start(bf16[64,2048]{1,0:T(8,128)(2,1)} %get-tuple-element.51), channel_id=1, source_target_pairs={{0,0},{1,4},{2,8},{3,12},{4,16},{5,20},{6,24},{7,28},{8,1},{9,5},{... | collective-permute-start | bytes 786440 | tf_op jit(solution)/shard_map/ppermute | solution.py:888
  (23 other events, 63.4 us)
Sparse Core Ops, SparseCore 0:
  10.8 155.4 all-gather.1

commit v4 on v3

--- a/solution.py
+++ b/solution.py
@@ -778,7 +778,10 @@
     probs = jnp.exp(scores - log_total).astype(BF)
     attended = jnp.einsum("hqk,khd->qhd", probs, window[1], preferred_element_type=FL)
     attended = attended.reshape(SEQ, span).astype(BF)
-    w_shared, attended = lax.optimization_barrier((w_shared, attended))
+    hidden = inputs + team_scatter(dot(attended, w_out).astype(BF), 1).astype(FL)
+    scale_mid = lax.rsqrt(jnp.mean(hidden * hidden, axis=-1, keepdims=True) + EPSILON)
+    mid = (hidden * scale_mid * gain_mid).astype(BF)
+    w_shared, mid = lax.optimization_barrier((w_shared, mid))
     wide_s = -(-(hid_s + 1) // 128) * 128
     wide_e = -(-hid_e // 128) * 128
     full = wide_s + wide_e
@@ -803,9 +806,6 @@
         ],
         axis=0,
     )
-    hidden = inputs + team_scatter(dot(attended, w_out).astype(BF), 1).astype(FL)
-    scale_mid = lax.rsqrt(jnp.mean(hidden * hidden, axis=-1, keepdims=True) + EPSILON)
-    mid = (hidden * scale_mid * gain_mid).astype(BF)
 
     if layered:
         mid_all = gather(mid, teams, 2)

time: 928 us -> 917 us (0.988)
  waiting for transfers between devices: 15.1 us -> 0.7 us
    all_to_all x1, waiting for transfers between devices: 14.4 us -> 0.01 us  [per_device(): lax.all_to_all(shared_cols.reshape(count, share, 2 * hid_s), AXIS, split_...]
  transfers between devices with their start and end apart: 9 -> 9, of which waited for: 1 -> 0; matrix products, arithmetic and copies ran while one was open for 21% -> 21% of each run, Pallas kernels for 30% -> 30%
where the time goes in v4:
time: 917 us; the launch traced here: 908 us
  Pallas kernels  603 us (66%)
  matrix products  114 us (12%)
  local copies, waits for them, and re-layouts  75.6 us (8%)
  other arithmetic  72.4 us (8%)
  starting transfers between devices  27.4 us (3%)
  between operations  15.3 us (2%)
    pallas_call x4, Pallas kernels, scatter(): pl.pallas_call(functools.partial(scatter_body, length, many, extra), out_...  275 us
    pallas_call x1, Pallas kernels, layer_and_line(): pl.pallas_call(functools.partial(layer_and_line_body, many), out_shape=[j...  122 us
    pallas_call x3, Pallas kernels, gather(): pl.pallas_call(functools.partial(gather_body, length), out_shape=jax.Shap...  121 us
    pallas_call x1, Pallas kernels, feed(): pl.pallas_call(functools.partial(feed_body, gate_column=gate_column, shar...  80.4 us
    dot_general x8, matrix products, dot(): return lax.dot_general(a, b, (dims, ((), ())), preferred_element_type=FL)  76.1 us
  transfers between devices with their start and end apart: 9, of which 0 were waited for; matrix products, arithmetic and copies ran while one was open for 21% of the time, Pallas kernels for 30%

profile of v4, /device:TPU:0, one launch (start us, length us, event | category | flops | bytes accessed | tf_op | source)
XLA Modules:
  0.0 907.9 jit_solution(3211932601115550820)
XLA Ops:
  15.8 22.3 %shard_map.247 = f32[4,2,2,2,2,8,128]{6,5,4,3,2,1,0:T(8,128)} custom-call(f32[2,8,128]{2,1,0:T(8,128)} %pad_bitcast_fusion.x_ref), custom_call_target="tpu_custom_call" | custom-call | tf_op jit(solution)/shard_map/pallas_call | solution.py:174
  42.6 4.2 all-to-all-start
  50.0 4.6 copy.78
  72.8 122.4 %shard_map.248 = (bf16[1,2,2,2,2,64,2048]{6,5,4,3,2,1,0:T(8,128)(2,1)}, bf16[4,512,768]{2,1,0:T(8,128)(2,1)}, bf16[4,64,2048]{2,1,0:T(8,128)(2,1)}) custom-call(bf16[2,64,2048]{2,1,0:T(8,128)(2,1)} %bitcast.186, bf16[512,768]{1,0:T(8,128)(2,1)} %bitcast.6.refs_1_, bf16[64,2048]{1,0:T(8,128)(2,1)} %copy-done.33), custom_call_target="tpu_custom_call" | custom-call | tf_op jit(solution)/shard_map/pallas_call | solution.py:239
  195.2 6.2 convolution_add_fusion
  209.7 5.8 reshape.374
  215.5 5.1 copy.76
  220.6 5.7 reshape.375
  226.3 3.9 all-to-all-start.1
  236.2 4.2 fusion
  240.4 5.2 exponential_reduce_fusion
  246.2 6.6 convolution_convert_fusion.4
  253.6 4.5 convolution_convert_fusion
  258.1 27.7 %shard_map.249 = f32[2,64,2048]{2,1,0:T(8,128)} custom-call(bf16[1,2,2,2,2,64,2048]{6,5,4,3,2,1,0:T(8,128)(2,1)} %bitcast.155), custom_call_target="tpu_custom_call" | custom-call | tf_op jit(solution)/shard_map/pallas_call | solution.py:483
  288.5 75.0 %shard_map.250 = bf16[4,2,2,2,2,64,2048]{6,5,4,3,2,1,0:T(8,128)(2,1)} custom-call(bf16[2,64,2048]{2,1,0:T(8,128)(2,1)} %bitcast.185), custom_call_target="tpu_custom_call" | custom-call | tf_op jit(solution)/shard_map/pallas_call | solution.py:174
  368.9 80.4 %shard_map.251 = (bf16[4096,2048]{1,0:T(8,128)(2,1)}, bf16[4096,2048]{1,0:T(8,128)(2,1)}, bf16[4096,640]{1,0:T(8,128)(2,1)}, bf16[4096,1280]{1,0:T(8,128)(2,1)}) custom-call(bf16[4096,2048]{1,0:T(8,128)(2,1)} %bitcast.156, bf16[4096,2048]{1,0:T(8,128)(2,1)} %all-gather.2.cloned.1.call-done.grad_ref, f32[4096,1]{1,0:T(8,128)} %copy.79.weight_ref, ...), custom_call_target="tpu_custom_call" | custom-call | flops 64424509440 | bytes 100663296 | tf_op jit(solution)/shard_map/pallas_call | solution.py:568
  449.3 150.1 %shard_map.252 = (f32[2,64,2048]{2,1,0:T(8,128)}, f32[2,64,2048]{2,1,0:T(8,128)}) custom-call(bf16[4,2,2,2,2,64,2048]{6,5,4,3,2,1,0:T(8,128)(2,1)} %bitcast.158, bf16[4,2,2,2,2,64,2048]{6,5,4,3,2,1,0:T(8,128)(2,1)} %bitcast.159), custom_call_target="tpu_custom_call" | custom-call | tf_op jit(solution)/shard_map/pallas_call | solution.py:483
  603.4 23.7 %shard_map.253 = bf16[1,2,2,2,2,64,2048]{6,5,4,3,2,1,0:T(8,128)(2,1)} custom-call(bf16[2,64,2048]{2,1,0:T(8,128)(2,1)} %bitcast.187), custom_call_target="tpu_custom_call" | custom-call | tf_op jit(solution)/shard_map/pallas_call | solution.py:174
  630.8 12.9 %multiply_reduce_fusion = (f32[2,1024]{1,0:T(2,128)S(1)}, f32[2,1024,2048]{2,1,0:T(8,128)}) fusion(f32[2,1024,2048]{2,1,0:T(8,128)} %copy-done, f32[2,1024]{1,0:T(2,128)S(1)} %log_add_fusion, pred[1024,2048]{1,0:T(8,128)(4,1)S(1)} %copy-done.2, bf16[1024,2,128]{0,2,1:T(8,128)(2,1)S(1)} %bitcast.199, bf16[2048,2,128]{0,2,1:T(8,128)(2,1)S(1)} %bitcast.180), kind=kOutput, calls=%fused_computation.1 | convolution fusion | flops 1094711296 | bytes 37240832 | tf_op jit(solution)/shard_map/qhd,khd->hqk/dot_general | solution.py:854
  643.7 8.7 fusion.43
  652.5 12.9 %multiply_convert_fusion = bf16[2,1024,2048]{2,1,0:T(8,128)(2,1)S(1)} fusion(f32[2,1024,2048]{2,1,0:T(8,128)} %get-tuple-element.94, f32[2,1024,2048]{2,1,0:T(8,128)} %copy-done, f32[2,1024]{1,0:T(2,128)S(1)} %get-tuple-element.93, f32[2,1024]{1,0:T(2,128)S(1)} %log_add_fusion, pred[1024,2048]{1,0:T(8,128)(4,1)S(1)} %copy-done.2), kind=kLoop, calls=%fused_computation | loop fusion | flops 25165824 | bytes 44056576 | tf_op jit(solution)/shard_map/convert_element_type | solution.py:856
  669.7 4.0 broadcast_multiply_fusion
  673.6 29.7 %fusion.55 = (bf16[2048,1280]{0,1:T(8,128)(2,1)}, f32[2048,1280]{0,1:T(8,128)}) fusion(bf16[4096,2048]{1,0:T(8,128)(2,1)} %bitcast.157, bf16[4096,1280]{1,0:T(8,128)(2,1)} %get-tuple-element.46), kind=kOutput, calls=%fused_computation.145 | convolution fusion | flops 21477457920 | bytes 42991616 | tf_op jit(solution)/shard_map/dot_general | solution.py:529
  713.7 8.5 all-to-all-start.2
  722.2 5.9 fusion.46
  728.1 17.7 %fusion.56 = f32[640,2048]{1,0:T(8,128)} fusion(bf16[4096,640]{1,0:T(8,128)(2,1)} %get-tuple-element.47, bf16[4096,2048]{1,0:T(8,128)(2,1)} %all-gather.2.cloned.1.call-done.grad_ref), kind=kOutput, calls=%fused_computation.146 | convolution fusion | flops 10737418240 | bytes 27262976 | tf_op jit(solution)/shard_map/dot_general | solution.py:529
  749.6 5.2 maximum_bitcast_fusion
  760.3 7.1 convolution_convert_fusion.1
  767.4 4.9 convolution_convert_fusion.2
  772.7 73.7 %shard_map.254 = (f32[2,64,2048]{2,1,0:T(8,128)}, bf16[512,768]{1,0:T(8,128)(2,1)}, bf16[64,2048]{1,0:T(8,128)(2,1)}) custom-call(bf16[1,2,2,2,2,64,2048]{6,5,4,3,2,1,0:T(8,128)(2,1)} %bitcast.176, bf16[4,512,768]{2,1,0:T(8,128)(2,1)} %bitcast.184, bf16[4,64,2048]{2,1,0:T(8,128)(2,1)} %bitcast.196), custom_call_target="tpu_custom_call" | custom-call | tf_op jit(solution)/shard_map/pallas_call | solution.py:483
  848.3 4.2 all-to-all-start.3
  864.9 23.8 %shard_map.255 = f32[2,8,128]{2,1,0:T(8,128)} custom-call(f32[4,2,2,2,2,8,128]{6,5,4,3,2,1,0:T(8,128)} %bitcast.193), custom_call_target="tpu_custom_call" | custom-call | tf_op jit(solution)/shard_map/pallas_call | solution.py:483
  (217 shorter events, 115.4 us)
Async XLA Ops:
  7.2 361.7 %all-gather.2.cloned.1.call-start = ((), (), s32[]{:S(2)}) async-start(), calls=%async_computation.4 | async-start | bytes 17301504 | tf_op jit(solution)/shard_map/all_gather | solution.py:739
  9.5 37.3 %copy-start.46 = (bf16[64,2048]{1,0:T(8,128)(2,1)S(1)}, bf16[64,2048]{1,0:T(8,128)(2,1)}, u32[]{:S(2)}) copy-start(bf16[64,2048]{1,0:T(8,128)(2,1)} %param.25) | copy-start | bytes 786436
  42.6 29.5 %all-to-all-start = ((bf16[8,64,768]{2,1,0:T(8,128)(2,1)}), bf16[8,64,768]{2,1,0:T(8,128)(2,1)}, u32[]{:S(2)}, u32[]{:S(2)}) async-start(bf16[8,64,768]{2,1,0:T(8,128)(2,1)} %reshape.363), calls=%async_computation | async-start | bytes 1572864 | tf_op jit(solution)/shard_map/all_to_all | solution.py:705
  46.8 25.3 %collective-permute-start = (bf16[64,2048]{1,0:T(8,128)(2,1)S(1)}, bf16[64,2048]{1,0:T(8,128)(2,1)S(1)}, u32[]{:S(2)}, u32[]{:S(2)}) collective-permute-start(bf16[64,2048]{1,0:T(8,128)(2,1)S(1)} %copy-done.46), channel_id=1, source_target_pairs={{0,0},{4,1},{8,2},{12,3},{16,4},{20,5},{24,6},{28,7},{1,8},{5,9},{... | collective-permute-start | bytes 786440 | tf_op jit(solution)/shard_map/ppermute | solution.py:715
  47.7 19.7 %copy-start.36 = (f32[2048]{0:T(1024)}, f32[2048]{0:T(1024)S(1)}, u32[]{:S(2)}) copy-start(f32[2048]{0:T(1024)S(1)} %mul.240) | copy-start | bytes 24580
  47.9 553.0 %copy-start.34 = (f32[2048]{0:T(1024)}, f32[2048]{0:T(1024)S(1)}, u32[]{:S(2)}) copy-start(f32[2048]{0:T(1024)S(1)} %mul.263) | copy-start | bytes 24580
  50.0 10.1 %copy-start.5 = (bf16[128,2048]{1,0:T(8,128)(2,1)S(1)}, bf16[128,2048]{1,0:T(8,128)(2,1)}, u32[]{:S(2)}) copy-start(bf16[128,2048]{1,0:T(8,128)(2,1)} %param.16) | copy-start | bytes 1572868
  64.3 131.0 %copy-start.40 = (f32[128]{0:T(128)}, f32[128]{0:T(128)S(1)}, u32[]{:S(2)}) copy-start(f32[128]{0:T(128)S(1)} %add_rsqrt_fusion.1) | copy-start | bytes 1540
  67.4 178.2 %copy-start.1 = (pred[1024,2048]{1,0:T(8,128)(4,1)}, pred[1024,2048]{1,0:T(8,128)(4,1)S(1)}, u32[]{:S(2)}) copy-start(pred[1024,2048]{1,0:T(8,128)(4,1)S(1)} %fusion.5) | copy-start | bytes 6291460
  202.7 5.7 copy-start.7
  205.9 27.6 %collective-permute-start.1 = (bf16[2,1024,256]{1,2,0:T(8,128)(2,1)}, bf16[2,1024,256]{1,2,0:T(8,128)(2,1)}, u32[]{:S(2)}, u32[]{:S(2)}) collective-permute-start(bf16[2,1024,256]{1,2,0:T(8,128)(2,1)} %pad_maximum_fusion.3), channel_id=1, source_target_pairs={{0,8},{1,9},{2,10},{3,11},{4,12},{5,13},{6,14},{7,15},{8,16},{9,17... | collective-permute-start | bytes 3145736 | tf_op jit(solution)/shard_map/ppermute | solution.py:761
  226.3 62.2 %all-to-all-start.1 = ((bf16[32,64,352]{2,1,0:T(8,128)(2,1)}), bf16[32,64,352]{2,1,0:T(8,128)(2,1)}, u32[]{:S(2)}, u32[]{:S(2)}) async-start(bf16[32,64,352]{2,1,0:T(8,128)(2,1)} %reshape.375), calls=%async_computation.1 | async-start | bytes 3145728 | tf_op jit(solution)/shard_map/all_to_all | solution.py:732
  240.4 5.8 copy-start
  287.3 313.7 %copy-start.3 = (f32[128,2048]{1,0:T(8,128)}, f32[128,2048]{1,0:T(8,128)S(1)}, u32[]{:S(2)}) copy-start(f32[128,2048]{1,0:T(8,128)S(1)} %get-tuple-element.59) | copy-start | bytes 3145732
  287.3 313.7 %copy-start.38 = (f32[128]{0:T(128)}, f32[128]{0:T(128)S(1)}, u32[]{:S(2)}) copy-start(f32[128]{0:T(128)S(1)} %add_rsqrt_fusion) | copy-start | bytes 1540
  449.3 151.7 %copy-start.20 = (bf16[128,2048]{1,0:T(8,128)(2,1)S(1)}, bf16[128,2048]{1,0:T(8,128)(2,1)}, u32[]{:S(2)}) copy-start(bf16[128,2048]{1,0:T(8,128)(2,1)} %param.17) | copy-start | bytes 1572868
  600.9 26.2 %copy-start.32 = (bf16[4,64,2048]{2,1,0:T(8,128)(2,1)S(1)}, bf16[4,64,2048]{2,1,0:T(8,128)(2,1)}, u32[]{:S(2)}) copy-start(bf16[4,64,2048]{2,1,0:T(8,128)(2,1)} %get-tuple-element.38) | copy-start | bytes 3145732
  601.0 29.8 %copy-start.42 = (f32[128]{0:T(128)}, f32[128]{0:T(128)S(1)}, u32[]{:S(2)}) copy-start(f32[128]{0:T(128)S(1)} %broadcast_multiply_fusion.6) | copy-start | bytes 1540
  652.5 14.3 %copy-start.11 = (f32[2,128,2048]{2,1,0:T(8,128)}, f32[2,128,2048]{2,1,0:T(8,128)S(1)}, u32[]{:S(2)}) copy-start(f32[2,128,2048]{2,1,0:T(8,128)S(1)} %fusion.43) | copy-start | bytes 6291460
  652.5 13.0 %copy-start.10 = (bf16[1024,2,128]{0,2,1:T(8,128)(2,1)S(1)}, bf16[1024,2,128]{0,2,1:T(8,128)(2,1)}, u32[]{:S(2)}) copy-start(bf16[1024,2,128]{0,2,1:T(8,128)(2,1)} %copy-done.9) | copy-start | bytes 1572868
  668.0 89.1 %collective-permute-start.2 = (bf16[2,1024,256]{1,2,0:T(8,128)(2,1)}, bf16[2,1024,256]{1,2,0:T(8,128)(2,1)}, u32[]{:S(2)}, u32[]{:S(2)}) collective-permute-start(bf16[2,1024,256]{1,2,0:T(8,128)(2,1)} %fusion.13), channel_id=1, source_target_pairs={{8,0},{9,1},{10,2},{11,3},{12,4},{13,5},{14,6},{15,7},{16,8},{17,9... | collective-permute-start | bytes 3145736 | tf_op jit(solution)/shard_map/ppermute | solution.py:865
  713.7 46.6 %all-to-all-start.2 = ((bf16[32,64,352]{2,1,0:T(8,128)(2,1)}), bf16[32,64,352]{2,1,0:T(8,128)(2,1)}, u32[]{:S(2)}, u32[]{:S(2)}) async-start(bf16[32,64,352]{2,1,0:T(8,128)(2,1)} %pad_maximum_fusion.2), calls=%async_computation.2 | async-start | bytes 3145728 | tf_op jit(solution)/shard_map/all_to_all | solution.py:829
  760.3 7.1 copy-start.45
  772.6 73.8 %copy-start.6 = (bf16[128,2048]{1,0:T(8,128)(2,1)S(1)}, bf16[128,2048]{1,0:T(8,128)(2,1)}, u32[]{:S(2)}) copy-start(bf16[128,2048]{1,0:T(8,128)(2,1)} %param.16) | copy-start | bytes 1572868
  772.6 73.8 %copy-start.37 = (f32[2048]{0:T(1024)S(1)}, f32[2048]{0:T(1024)}, u32[]{:S(2)}) copy-start(f32[2048]{0:T(1024)} %copy-done.36) | copy-start | bytes 24580
  772.6 73.8 %copy-start.41 = (f32[128]{0:T(128)S(1)}, f32[128]{0:T(128)}, u32[]{:S(2)}) copy-start(f32[128]{0:T(128)} %copy-done.40) | copy-start | bytes 1540
  772.6 81.5 %copy-start.4 = (f32[128,2048]{1,0:T(8,128)S(1)}, f32[128,2048]{1,0:T(8,128)}, u32[]{:S(2)}) copy-start(f32[128,2048]{1,0:T(8,128)} %copy-done.3) | copy-start | bytes 3145732
  772.6 81.5 %copy-start.35 = (f32[2048]{0:T(1024)S(1)}, f32[2048]{0:T(1024)}, u32[]{:S(2)}) copy-start(f32[2048]{0:T(1024)} %copy-done.34) | copy-start | bytes 24580
  772.7 81.4 %copy-start.39 = (f32[128]{0:T(128)S(1)}, f32[128]{0:T(128)}, u32[]{:S(2)}) copy-start(f32[128]{0:T(128)} %copy-done.38) | copy-start | bytes 1540
  772.7 81.4 %copy-start.43 = (f32[128]{0:T(128)S(1)}, f32[128]{0:T(128)}, u32[]{:S(2)}) copy-start(f32[128]{0:T(128)} %copy-done.42) | copy-start | bytes 1540
  848.3 47.5 %all-to-all-start.3 = ((bf16[8,64,768]{2,1,0:T(8,128)(2,1)}), bf16[8,64,768]{2,1,0:T(8,128)(2,1)}, u32[]{:S(2)}, u32[]{:S(2)}) async-start(bf16[8,64,768]{2,1,0:T(8,128)(2,1)} %bitcast.198), calls=%async_computation.3 | async-start | bytes 1572864 | tf_op jit(solution)/shard_map/all_to_all | solution.py:907
  852.5 42.4 %collective-permute-start.3 = (bf16[64,2048]{1,0:T(8,128)(2,1)}, bf16[64,2048]{1,0:T(8,128)(2,1)S(1)}, u32[]{:S(2)}, u32[]{:S(2)}) collective-permute-start(bf16[64,2048]{1,0:T(8,128)(2,1)} %get-tuple-element.51), channel_id=1, source_target_pairs={{0,0},{1,4},{2,8},{3,12},{4,16},{5,20},{6,24},{7,28},{8,1},{9,5},{... | collective-permute-start | bytes 786440 | tf_op jit(solution)/shard_map/ppermute | solution.py:888
  (24 other events, 64.2 us)
Sparse Core Ops, SparseCore 0:
  10.8 155.4 all-gather.1
